TPU v7x, 32 devices: a whole 2x2x4 slice. The times are simulated.
32 devices in a mesh: mem: 4 (over x, core), band: 8 (over z, y).
Axes of the slice: x: 2, y: 2, z: 4, core: 2. Of those that a mesh axis runs over, the one named last changes fastest.
Arguments:
- sample_collection: float32 [24, 3, 64, 4096], P('mem', None, 'band'), may hold values from -6 to 6
- seabed_profile: float32 [64, 4096], P('band'), may hold values from 0.5 to 2
- gauge_grid_position: int32 [32, 128], P('band'), may hold values from 0 to 262143, as said below
- observed_values: float32 [32, 128], P('band'), may hold values from -6 to 6
- error_scale: float32 [32, 128], P('band'), may hold values from 0.3 to 3
- perturbation: float32 [24, 32, 128], P('mem', 'band'), may hold values from -6 to 6
- inflation: float32 [1], replicated, may hold values from 1 to 16
Outputs:
- analysis: float32 [24, 3, 64, 4096], P('mem', None, 'band')
Inputs may be any that keep to these rules, and one draw needn't show every extreme that they name: Every entry in row r of gauge_grid_position lies in grid rows b * 8 to (b + 1) * 8 - 1 with b = r // 4; cells may repeat.
All inputs are finite; a program needn't handle non-finite values.
Results may differ from a plain program's by a relative error of at most 0.000071.
Values sent between devices are 32-bit elements; how exact they have to be, the bound alone decides.
No kernel may reach another device: no remote copies, remote signals or barrier semaphores. Data moves between devices by JAX's collectives and lax.ppermute only.
A program may use at most 128 MiB of HBM per device.

v0:
```python
import functools
import math

import jax
import jax.numpy as jnp
from jax import lax
from jax.experimental import pallas as pl
from jax.experimental.pallas import tpu as pltpu
from jax.sharding import PartitionSpec as P


LANES = 128

courant = 0.5
coriolis_base = 0.15
coriolis_slope = 0.3


f32 = jnp.float32


def pad8(count):
    return -(-count // 8) * 8


def cost(flops, moved):
    return pl.CostEstimate(flops=flops, bytes_accessed=moved, transcendentals=0)


def shift_both(low_edge, high_edge):
    count = lax.axis_size("band")
    above = lax.ppermute(high_edge, "band", [(i, i + 1) for i in range(count - 1)])
    below = lax.ppermute(low_edge, "band", [(i + 1, i) for i in range(count - 1)])
    return above, below


def band_sum(part):
    count = lax.axis_size("band")
    if count & (count - 1):
        return lax.psum(part, "band")
    step = 1
    while step < count:
        other = lax.ppermute(part, "band", [(i, i ^ step) for i in range(count)])
        part = part + other
        step *= 2
    return part


def mem_plan(count):
    if count % 2 or count == 1:
        return [(s, None) for s in range(1, count)]
    far = [(2 * s, None) for s in range(1, count // 2)]
    return far


def far_gather(block):
    count = lax.axis_size("mem")
    return [
        lax.ppermute(block, "mem", [(i, (i + s) % count) for i in range(count)])
        for s, _ in mem_plan(count)
    ]


def near_swap(block):
    count = lax.axis_size("mem")
    return lax.ppermute(block, "mem", [(i, i ^ 1) for i in range(count)])


def east(q):
    columns = q.shape[-1]
    return (pltpu.roll(q, columns - 1, 1) - pltpu.roll(q, 1, 1)) * 0.5


def north(q, above, below):
    rows = q.shape[0]
    index = lax.broadcasted_iota(jnp.int32, q.shape, 0)
    up = jnp.where(index == rows - 1, below, pltpu.roll(q, rows - 1, 0))
    down = jnp.where(index == 0, above, pltpu.roll(q, 1, 0))
    return (up - down) * 0.5


def spin(first_row, shape, total_rows):
    rows = (first_row + lax.broadcasted_iota(jnp.int32, shape, 0)).astype(f32)
    return coriolis_base + coriolis_slope * (rows + 0.5) / total_rows


def edge_kernel(x_ref, b_ref, lo_out, hi_out):
    def member(m, _):
        flux = b_ref[...] * x_ref[m, 2]
        lo_out[m] = flux[:1]
        hi_out[m] = flux[-1:]
        return 0

    lax.fori_loop(0, x_ref.shape[0], member, 0)


def height_kernel(parts, h_ref, u_ref, v_ref, b_ref, above_ref, below_ref, h_out, lo_out, hi_out):
    depth = b_ref[...]

    def member(m, _):
        h0, u, v = (r[m] if q is None else r[m, q] for r, q in zip((h_ref, u_ref, v_ref), parts))
        h = h0 - courant * (east(depth * u) + north(depth * v, above_ref[m], below_ref[m]))
        h_out[m] = h
        lo_out[m] = h[:1]
        hi_out[m] = h[-1:]
        return 0

    lax.fori_loop(0, h_out.shape[0], member, 0)


def speed_kernel(
    total_rows, row_ref, h_ref, x_ref, b_ref, above_ref, below_ref,
    u_out, v_out, w_out, lo_out, hi_out,
):
    depth = b_ref[...]
    turn = spin(row_ref[0], depth.shape, total_rows)

    def member(m, _):
        h, v0 = h_ref[m], x_ref[m, 2]
        u = x_ref[m, 1] - courant * east(h) + turn * v0
        v = v0 - courant * north(h, above_ref[m], below_ref[m]) - turn * u
        u_out[m] = u
        v_out[m] = v
        w_out[m] = u + turn * v
        flux = depth * v
        lo_out[m] = flux[:1]
        hi_out[m] = flux[-1:]
        return 0

    lax.fori_loop(0, h_ref.shape[0], member, 0)


def last_kernel(total_rows, row_ref, h_ref, w_ref, v_ref, above_ref, below_ref, v_out):
    turn = spin(row_ref[0], h_ref.shape[1:], total_rows)

    def member(m, _):
        h = h_ref[m]
        u = w_ref[m] - courant * east(h)
        v_out[m] = v_ref[m] - courant * north(h, above_ref[m], below_ref[m]) - turn * u
        return 0

    lax.fori_loop(0, h_ref.shape[0], member, 0)


def probe_kernel(
    row_ref, cell_ref, h_ref, u_ref, v_ref, b_ref, above_ref, below_ref,
    h_out, lo_out, hi_out, out_ref, cells,
):
    members, rows, columns = h_ref.shape
    stride = rows * columns // LANES
    depth = b_ref[...]

    def member(m, _):
        h = h_ref[m] - courant * (
            east(depth * u_ref[m]) + north(depth * v_ref[m], above_ref[m], below_ref[m])
        )
        h_out[m] = h
        lo_out[m] = h[:1]
        hi_out[m] = h[-1:]
        base = pl.multiple_of(m * stride, 8)
        for c in range(columns // LANES):
            cells[pl.ds(base + c * rows, rows), :] = h[:, c * LANES : (c + 1) * LANES]
        return 0

    lax.fori_loop(0, members, member, 0)
    first = row_ref[0] * columns
    out_ref[...] = jnp.zeros_like(out_ref)
    lane = lax.broadcasted_iota(jnp.int32, (members, LANES), 1)
    for k in range(out_ref.shape[0]):

        def take(i, held, k=k):
            cell = cell_ref[k, i] - first
            row, column = cell // columns, lax.rem(cell, columns)
            start = (column // LANES) * rows + row
            piece = cells[pl.ds(start, members, stride=stride), :]
            turned = pltpu.roll(piece, lax.rem(i - lax.rem(column, LANES) + LANES, LANES), 1)
            return jnp.where(lane == i, turned, held)

        out_ref[k, :members, :] = lax.fori_loop(
            0, LANES, take, jnp.zeros((members, LANES), f32), unroll=8
        )


def gram_kernel(total, members, inf_ref, obs_ref, scale_ref, pert_ref, *refs):
    out_ref, spread, both = refs[-3:]
    groups = refs[:-3]
    padded = groups[0].shape[1]
    real = lax.broadcasted_iota(jnp.int32, (padded, LANES), 0) < members
    root = jnp.sqrt(jnp.full((1, LANES), inf_ref[0], f32))
    both[...] = jnp.zeros_like(both)
    for k in range(groups[0].shape[0]):
        at = slice(k * LANES, (k + 1) * LANES)
        scale = scale_ref[k : k + 1, :]
        sums = groups[0][k]
        for g in groups[1:]:
            sums = sums + g[k]
        centre = jnp.sum(sums, axis=0, keepdims=True) / total
        for n, g in enumerate(groups):
            s = jnp.where(real, (g[k] - centre) / (scale * math.sqrt(total - 1)), 0.0)
            spread[n * padded : (n + 1) * padded, at] = s
            both[n * padded : (n + 1) * padded, at] = s
        for m in range(members):
            both[len(groups) * padded + m : len(groups) * padded + m + 1, at] = (
                obs_ref[k : k + 1, :]
                + root * scale * pert_ref[m, k : k + 1, :]
                - groups[0][k, m : m + 1, :]
            ) / scale
    out_ref[...] = lax.dot_general(
        spread[...], both[...], (((1,), (1,)), ((), ())),
        precision=lax.Precision.HIGHEST, preferred_element_type=f32,
    )


def solve_kernel(total, members, groups, inf_ref, part_ref, out_ref):
    a = part_ref[...]
    size = a.shape[0]
    padded = size // groups
    row = lax.broadcasted_iota(jnp.int32, a.shape, 0)
    lane = lax.broadcasted_iota(jnp.int32, a.shape, 1)
    a = a + jnp.where(row == lane, inf_ref[0], 0.0)
    for g in range(groups):
        for m in range(members):
            k = g * padded + m
            pivot = a[k : k + 1, k : k + 1]
            inverse = 1.0 / jnp.sqrt(pivot)
            line = a[k : k + 1, :] * inverse
            column = a[:, k : k + 1] * inverse
            a = jnp.where(row == k, line, a - column * line)
    diagonal = jnp.sum(jnp.where(row == lane, a, 0.0), axis=1, keepdims=True)
    real = lax.rem(row, padded) < members
    w = jnp.where(real, a / diagonal, 0.0)
    mean = jnp.sum(w, axis=0, keepdims=True) / total
    unit = jnp.where(lane - size == row, 1.0, 0.0)
    out_ref[...] = unit + (w - mean) / math.sqrt(total - 1)


def weighted(t_ref, pieces, at, first, members, rows, width, start=None):
    total = list(start) if start is not None else [jnp.zeros((rows, width), f32)] * members
    for g, ref in pieces:
        for i in range(members):
            value = ref[i, :, at]
            for j in range(members):
                total[j] = total[j] + t_ref[g + i, first + j] * value
    return total


def blend_kernel(groups, padded, near, width, t_ref, *refs):
    ins, (out_ref, v_out, h_new, u_new, sems) = refs[:-5], refs[-5:]
    members, rows, columns = v_out.shape
    first = groups * padded
    heights = [(g * padded, r) for g, r in enumerate(ins[:groups])]
    speeds = [(g * padded, r) for g, r in enumerate(ins[groups : 2 * groups])]
    sides = [(g * padded, r) for g, r in zip(near, ins[2 * groups :])]

    def chunk(c, _):
        at = pl.ds(pl.multiple_of(c * width, LANES), width)
        for pieces, out in ((heights, h_new), (speeds, u_new), (sides, v_out)):
            for j, t in enumerate(weighted(t_ref, pieces, at, first, members, rows, width)):
                out[j, :, at] = t
        return 0

    lax.fori_loop(0, columns // width, chunk, 0)
    copies = [pltpu.make_async_copy(h_new, out_ref.at[:, 0], sems.at[0])]
    copies[0].start()

    def member(j, _):
        u_new[j] = u_new[j] - courant * east(h_new[j])
        return 0

    lax.fori_loop(0, members, member, 0)
    copies.append(pltpu.make_async_copy(u_new, out_ref.at[:, 1], sems.at[1]))
    copies[1].start()
    for copy in copies:
        copy.wait()


def finish_kernel(groups, padded, far, width, t_ref, part_ref, *refs):
    ins, (held_ref, out_ref, v_new, sems) = refs[:-4], refs[-4:]
    del held_ref
    members, rows, columns = part_ref.shape
    first = groups * padded
    sides = [(g * padded, r) for g, r in zip(far, ins)]
    copies = []
    for c in range(columns // width):
        at = pl.ds(c * width, width)
        start = [part_ref[j, :, at] for j in range(members)]
        for j, t in enumerate(weighted(t_ref, sides, at, first, members, rows, width, start)):
            v_new[j, :, at] = t
        copies.append(
            pltpu.make_async_copy(v_new.at[:, :, at], out_ref.at[:, 2, :, at], sems.at[c])
        )
        copies[-1].start()
    for copy in copies:
        copy.wait()


def body(
    sample_collection,
    seabed_profile,
    gauge_grid_position,
    observed_values,
    error_scale,
    perturbation,
    inflation,
):
    members, _, rows, columns = sample_collection.shape
    bands, mems = lax.axis_size("band"), lax.axis_size("mem")
    total_rows, total = rows * bands, members * mems
    padded = pad8(members)
    first_row = lax.axis_index("band") * rows
    row_index = first_row.reshape(1)

    field = jax.ShapeDtypeStruct((members, rows, columns), f32)
    edge = jax.ShapeDtypeStruct((members, 1, columns), f32)
    smem = pl.BlockSpec(memory_space=pltpu.SMEM)
    vmem = pl.BlockSpec(memory_space=pltpu.VMEM)
    hbm = pl.BlockSpec(memory_space=pl.ANY)
    size = 4 * members * rows * columns

    def call(kernel, ins, outs, shapes, limit, flops, moved, scratch=(), aliases={}):
        return pl.pallas_call(
            kernel,
            in_specs=ins,
            out_specs=outs,
            out_shape=shapes,
            scratch_shapes=list(scratch),
            input_output_aliases=aliases,
            compiler_params=pltpu.CompilerParams(vmem_limit_bytes=limit << 20),
            cost_estimate=cost(flops, moved),
        )

    x = sample_collection
    low, high = call(
        edge_kernel, [vmem] * 2, [vmem] * 2, [edge, edge], 6, size, size
    )(x, seabed_profile)
    above, below = shift_both(low, high)
    h, low, high = call(
        functools.partial(height_kernel, (0, 1, 2)),
        [vmem] * 6, [vmem] * 3, [field, edge, edge], 12, 20 * size, 4 * size,
    )(x, x, x, seabed_profile, above, below)
    above, below = shift_both(low, high)
    u, v, w, low, high = call(
        functools.partial(speed_kernel, total_rows),
        [smem] + [vmem] * 5, [vmem] * 5, [field, field, field, edge, edge], 12,
        30 * size, 6 * size,
    )(row_index, h, x, seabed_profile, above, below)
    above, below = shift_both(low, high)
    w_far = far_gather(w)

    lines = gauge_grid_position.shape[0]
    h, low, high, predicted = call(
        probe_kernel,
        [smem, smem] + [vmem] * 6, [vmem] * 4,
        [field, edge, edge, jax.ShapeDtypeStruct((lines, padded, LANES), f32)], 12,
        20 * size, 4 * size,
        scratch=[pltpu.VMEM((members * rows * columns // LANES, LANES), f32)],
    )(row_index, gauge_grid_position, h, u, v, seabed_profile, above, below)
    gathered = [predicted] + far_gather(predicted)
    if mems % 2 == 0:
        gathered = gathered + [near_swap(b) for b in gathered]
    n = len(gathered)
    height_rows = n * padded
    reach = -(-(height_rows + padded) // LANES) * LANES
    partial = call(
        functools.partial(gram_kernel, total, members),
        [smem] + [vmem] * (3 + n), vmem, jax.ShapeDtypeStruct((height_rows, reach), f32), 8,
        1000000, 200000,
        scratch=[
            pltpu.VMEM((height_rows, lines * LANES), f32),
            pltpu.VMEM((reach, lines * LANES), f32),
        ],
    )(inflation, observed_values, error_scale, perturbation, *gathered)
    summed = band_sum(partial)
    transform = call(
        functools.partial(solve_kernel, total, members, n),
        [smem, vmem], vmem, jax.ShapeDtypeStruct((height_rows, reach), f32), 4,
        1000000, 40000,
    )(inflation, summed)

    h_far = far_gather(h)
    above, below = shift_both(low, high)
    v = call(
        functools.partial(last_kernel, total_rows),
        [smem] + [vmem] * 5, vmem, field, 12, 20 * size, 4 * size,
    )(row_index, h, w, v, above, below)
    v_far = far_gather(v)

    def grouped(own, far):
        if mems % 2:
            return [own] + far
        own_near = near_swap(own)
        return [own] + far + [own_near] + [near_swap(b) for b in far]

    heights, speeds, sides = grouped(h, h_far), grouped(w, w_far), grouped(v, v_far)
    near = [0] if mems % 2 else [0, n // 2]
    far = [g for g in range(n) if g not in near]
    width = math.gcd(512, columns)
    whole = jax.ShapeDtypeStruct((members, 3, rows, columns), f32)
    out, v_part = call(
        functools.partial(blend_kernel, n, padded, near, width),
        [smem] + [vmem] * (2 * n + len(near)), [hbm, vmem], [whole, field], 4 + 2 * n,
        200 * size, 15 * size,
        scratch=[
            pltpu.VMEM((members, rows, columns), f32),
            pltpu.VMEM((members, rows, columns), f32),
            pltpu.SemaphoreType.DMA((2,)),
        ],
    )(transform, *heights, *speeds, *[sides[g] for g in near])
    return call(
        functools.partial(finish_kernel, n, padded, far, width),
        [smem] + [vmem] * (1 + len(far)) + [hbm], hbm, whole, 4 + n,
        100 * size, 5 * size,
        scratch=[
            pltpu.VMEM((members, rows, columns), f32),
            pltpu.SemaphoreType.DMA((columns // width,)),
        ],
        aliases={2 + len(far): 0},
    )(transform, v_part, *[sides[g] for g in far], out)


def solution(mesh):
    in_specs = (
        P("mem", None, "band", None),
        P("band", None),
        P("band", None),
        P("band", None),
        P("band", None),
        P("mem", "band", None),
        P(),
    )
    out_specs = P("mem", None, "band", None)

    return jax.shard_map(body, mesh=mesh, in_specs=in_specs, out_specs=out_specs, check_vma=False)
```

profile of v0, /device:TPU:0, one launch (start us, length us, event | category | flops | bytes accessed | tf_op | source)
XLA Modules:
  0.0 134.5 jit_solution(995974380196022906)
XLA Ops:
  0.0 1.7 %copy-done = f32[6,3,8,4096]{3,2,1,0:T(8,128)S(1)} copy-done((f32[6,3,8,4096]{3,2,1,0:T(8,128)S(1)}, f32[6,3,8,4096]{3,2,1,0:T(8,128)}, u32[]{:S(2)}) %copy-start) | copy-done | bytes 2359320
  2.7 5.0 %collective-permute-start = (f32[6,1,4096]{2,1,0:T(1,128)S(1)}, f32[6,1,4096]{2,1,0:T(1,128)S(1)}, u32[]{:S(2)}, u32[]{:S(2)}) collective-permute-start(f32[6,1,4096]{2,1,0:T(1,128)S(1)} %get-tuple-element.21), channel_id=1, source_target_pairs={{0,1},{1,2},{2,3},{3,4},{4,5},{5,6},{6,7},{8,9},{9,10},{10,11},{11... | collective-permute-start | bytes 294920 | tf_op jit(solution)/shard_map/ppermute | solution.py:32
  7.8 1.3 collective-permute-start.1
  10.0 4.3 %collective-permute-done.1.below_ref = f32[6,1,4096]{2,1,0:T(1,128)S(1)} collective-permute-done((f32[6,1,4096]{2,1,0:T(1,128)S(1)}, f32[6,1,4096]{2,1,0:T(1,128)S(1)}, u32[]{:S(2)}, u32[]{:S(2)}) %collective-permute-start.1) | collective-permute-done | bytes 98336 | tf_op jit(solution)/shard_map/ppermute | solution.py:33
  14.3 1.6 %shard_map.74 = (f32[6,8,4096]{2,1,0:T(8,128)S(1)}, f32[6,1,4096]{2,1,0:T(1,128)}, f32[6,1,4096]{2,1,0:T(1,128)}) custom-call(f32[6,3,8,4096]{3,2,1,0:T(8,128)S(1)} %copy-done.1, f32[6,3,8,4096]{3,2,1,0:T(8,128)S(1)} %copy-done.1, f32[6,3,8,4096]{3,2,1,0:T(8,128)S(1)} %copy-done.1, f32[8,4096]{1,0:T(8,128)S(1)} %copy-done.3, ...), custom_call_target="tpu_custom_call" | custom-call | flops 15728640 | bytes 3145728 | tf_op jit(solution)/shard_map/pallas_call | solution.py:337
  15.9 4.4 %collective-permute-start.2 = (f32[6,1,4096]{2,1,0:T(1,128)}, f32[6,1,4096]{2,1,0:T(1,128)S(1)}, u32[]{:S(2)}, u32[]{:S(2)}) collective-permute-start(f32[6,1,4096]{2,1,0:T(1,128)} %get-tuple-element.24), channel_id=1, source_target_pairs={{0,1},{1,2},{2,3},{3,4},{4,5},{5,6},{6,7},{8,9},{9,10},{10,11},{11... | collective-permute-start | bytes 294920 | tf_op jit(solution)/shard_map/ppermute | solution.py:32
  20.4 1.3 collective-permute-start.3
  21.7 2.2 %collective-permute-done.2.above_ref = f32[6,1,4096]{2,1,0:T(1,128)S(1)} collective-permute-done((f32[6,1,4096]{2,1,0:T(1,128)}, f32[6,1,4096]{2,1,0:T(1,128)S(1)}, u32[]{:S(2)}, u32[]{:S(2)}) %collective-permute-start.2) | collective-permute-done | bytes 98336 | tf_op jit(solution)/shard_map/ppermute | solution.py:32
  23.9 3.2 %collective-permute-done.3.below_ref = f32[6,1,4096]{2,1,0:T(1,128)S(1)} collective-permute-done((f32[6,1,4096]{2,1,0:T(1,128)}, f32[6,1,4096]{2,1,0:T(1,128)S(1)}, u32[]{:S(2)}, u32[]{:S(2)}) %collective-permute-start.3) | collective-permute-done | bytes 98336 | tf_op jit(solution)/shard_map/ppermute | solution.py:33
  27.1 1.1 shard_map.75
  28.2 3.4 %collective-permute-start.4 = (f32[6,1,4096]{2,1,0:T(1,128)S(1)}, f32[6,1,4096]{2,1,0:T(1,128)S(1)}, u32[]{:S(2)}, u32[]{:S(2)}) collective-permute-start(f32[6,1,4096]{2,1,0:T(1,128)S(1)} %get-tuple-element.28), channel_id=1, source_target_pairs={{0,1},{1,2},{2,3},{3,4},{4,5},{5,6},{6,7},{8,9},{9,10},{10,11},{11... | collective-permute-start | bytes 294920 | tf_op jit(solution)/shard_map/ppermute | solution.py:32
  31.7 1.3 collective-permute-start.5
  33.0 1.9 %collective-permute-done.4.above_ref = f32[6,1,4096]{2,1,0:T(1,128)S(1)} collective-permute-done((f32[6,1,4096]{2,1,0:T(1,128)S(1)}, f32[6,1,4096]{2,1,0:T(1,128)S(1)}, u32[]{:S(2)}, u32[]{:S(2)}) %collective-permute-start.4) | collective-permute-done | bytes 98336 | tf_op jit(solution)/shard_map/ppermute | solution.py:32
  34.9 3.3 %collective-permute-done.5.below_ref = f32[6,1,4096]{2,1,0:T(1,128)S(1)} collective-permute-done((f32[6,1,4096]{2,1,0:T(1,128)S(1)}, f32[6,1,4096]{2,1,0:T(1,128)S(1)}, u32[]{:S(2)}, u32[]{:S(2)}) %collective-permute-start.5) | collective-permute-done | bytes 98336 | tf_op jit(solution)/shard_map/ppermute | solution.py:33
  38.2 11.5 %shard_map.76 = (f32[6,8,4096]{2,1,0:T(8,128)S(1)}, f32[6,1,4096]{2,1,0:T(1,128)S(1)}, f32[6,1,4096]{2,1,0:T(1,128)S(1)}, f32[4,8,128]{2,1,0:T(8,128)S(1)}) custom-call(s32[1]{0:T(128)} %bitcast.row_ref, s32[4,128]{1,0:T(4,128)S(1)} %copy-done.5, f32[6,8,4096]{2,1,0:T(8,128)S(1)} %get-tuple-element.23.h_ref, f32[6,8,4096]{2,1,0:T(8,128)S(1)} %get-tuple-element.26.u_ref, ...), custom_call_target="tpu_custom_call" | custom-call | flops 15728640 | bytes 3145728 | tf_op jit(solution)/shard_map/pallas_call | solution.py:351
  49.7 4.3 %collective-permute-start.18 = (f32[6,1,4096]{2,1,0:T(1,128)S(1)}, f32[6,1,4096]{2,1,0:T(1,128)S(1)}, u32[]{:S(2)}, u32[]{:S(2)}) collective-permute-start(f32[6,1,4096]{2,1,0:T(1,128)S(1)} %get-tuple-element.33), channel_id=1, source_target_pairs={{0,1},{1,2},{2,3},{3,4},{4,5},{5,6},{6,7},{8,9},{9,10},{10,11},{11... | collective-permute-start | bytes 294920 | tf_op jit(solution)/shard_map/ppermute | solution.py:32
  54.1 1.3 collective-permute-start.19
  55.4 1.6 %collective-permute-start.15 = (f32[6,8,4096]{2,1,0:T(8,128)S(1)}, f32[6,8,4096]{2,1,0:T(8,128)S(1)}, u32[]{:S(2)}, u32[]{:S(2)}) collective-permute-start(f32[6,8,4096]{2,1,0:T(8,128)S(1)} %get-tuple-element.32.w_ref.refs_4_), channel_id=1, source_target_pairs={{0,16},{8,24},{16,0},{24,8},{1,17},{9,25},{17,1},{25,9},{2,18},{10... | collective-permute-start | bytes 2359304 | tf_op jit(solution)/shard_map/ppermute | solution.py:59
  57.5 3.1 %collective-permute-done.19.below_ref = f32[6,1,4096]{2,1,0:T(1,128)S(1)} collective-permute-done((f32[6,1,4096]{2,1,0:T(1,128)S(1)}, f32[6,1,4096]{2,1,0:T(1,128)S(1)}, u32[]{:S(2)}, u32[]{:S(2)}) %collective-permute-start.19) | collective-permute-done | bytes 98336 | tf_op jit(solution)/shard_map/ppermute | solution.py:33
  61.5 1.6 %collective-permute-start.21 = (f32[6,8,4096]{2,1,0:T(8,128)S(1)}, f32[6,8,4096]{2,1,0:T(8,128)S(1)}, u32[]{:S(2)}, u32[]{:S(2)}) collective-permute-start(f32[6,8,4096]{2,1,0:T(8,128)S(1)} %shard_map.79.refs_8_), channel_id=1, source_target_pairs={{0,16},{8,24},{16,0},{24,8},{1,17},{9,25},{17,1},{25,9},{2,18},{10... | collective-permute-start | bytes 2359304 | tf_op jit(solution)/shard_map/ppermute | solution.py:59
  63.6 41.2 %collective-permute-done.6.refs_1_ = f32[4,8,128]{2,1,0:T(8,128)S(1)} collective-permute-done((f32[4,8,128]{2,1,0:T(8,128)S(1)}, f32[4,8,128]{2,1,0:T(8,128)S(1)}, u32[]{:S(2)}, u32[]{:S(2)}) %collective-permute-start.6) | collective-permute-done | bytes 16416 | tf_op jit(solution)/shard_map/ppermute | solution.py:59
  104.8 1.2 collective-permute-done.7.refs_2_
  107.5 2.4 %collective-permute-start.9 = (f32[32,128]{1,0:T(8,128)S(1)}, f32[32,128]{1,0:T(8,128)S(1)}, u32[]{:S(2)}, u32[]{:S(2)}) collective-permute-start(f32[32,128]{1,0:T(8,128)S(1)} %shard_map.77), channel_id=1, source_target_pairs={{0,1},{1,0},{2,3},{3,2},{4,5},{5,4},{6,7},{7,6},{8,9},{9,8},{10,11... | collective-permute-start | bytes 49160 | tf_op jit(solution)/shard_map/ppermute | solution.py:43
  110.0 1.7 %collective-permute-done.9 = f32[32,128]{1,0:T(8,128)S(1)} collective-permute-done((f32[32,128]{1,0:T(8,128)S(1)}, f32[32,128]{1,0:T(8,128)S(1)}, u32[]{:S(2)}, u32[]{:S(2)}) %collective-permute-start.9) | collective-permute-done | bytes 16416 | tf_op jit(solution)/shard_map/ppermute | solution.py:43
  111.7 1.9 %collective-permute-start.10 = (f32[32,128]{1,0:T(8,128)S(1)}, f32[32,128]{1,0:T(8,128)S(1)}, u32[]{:S(2)}, u32[]{:S(2)}) collective-permute-start(f32[32,128]{1,0:T(8,128)S(1)} %add.9), channel_id=1, source_target_pairs={{0,2},{1,3},{2,0},{3,1},{4,6},{5,7},{6,4},{7,5},{8,10},{9,11},{10,... | collective-permute-start | bytes 49160 | tf_op jit(solution)/shard_map/ppermute | solution.py:43
  113.5 1.9 %collective-permute-done.10 = f32[32,128]{1,0:T(8,128)S(1)} collective-permute-done((f32[32,128]{1,0:T(8,128)S(1)}, f32[32,128]{1,0:T(8,128)S(1)}, u32[]{:S(2)}, u32[]{:S(2)}) %collective-permute-start.10) | collective-permute-done | bytes 16416 | tf_op jit(solution)/shard_map/ppermute | solution.py:43
  115.4 2.8 %collective-permute-start.11 = (f32[32,128]{1,0:T(8,128)S(1)}, f32[32,128]{1,0:T(8,128)S(1)}, u32[]{:S(2)}, u32[]{:S(2)}) collective-permute-start(f32[32,128]{1,0:T(8,128)S(1)} %add.10), channel_id=1, source_target_pairs={{0,4},{1,5},{2,6},{3,7},{4,0},{5,1},{6,2},{7,3},{8,12},{9,13},{10,... | collective-permute-start | bytes 49160 | tf_op jit(solution)/shard_map/ppermute | solution.py:43
  118.2 1.9 %collective-permute-done.11 = f32[32,128]{1,0:T(8,128)S(1)} collective-permute-done((f32[32,128]{1,0:T(8,128)S(1)}, f32[32,128]{1,0:T(8,128)S(1)}, u32[]{:S(2)}, u32[]{:S(2)}) %collective-permute-start.11) | collective-permute-done | bytes 16416 | tf_op jit(solution)/shard_map/ppermute | solution.py:43
  121.2 2.4 %shard_map.78.t_ref = f32[32,128]{1,0:T(8,128)S(1)} custom-call(f32[1]{0:T(128)S(6)} %copy.10.inf_ref, f32[32,128]{1,0:T(8,128)S(1)} %add.11.part_ref), custom_call_target="tpu_custom_call" | custom-call | flops 1000000 | bytes 40000 | tf_op jit(solution)/shard_map/pallas_call | solution.py:374
  124.6 1.1 collective-permute-done.14.refs_3_
  125.7 6.6 %shard_map.80 = (f32[6,3,8,4096]{3,2,1,0:T(8,128)}, f32[6,8,4096]{2,1,0:T(8,128)S(1)}) custom-call(f32[32,128]{1,0:T(8,128)S(1)} %shard_map.78.t_ref, f32[6,8,4096]{2,1,0:T(8,128)S(1)} %get-tuple-element.31.h_ref.refs_0_, f32[6,8,4096]{2,1,0:T(8,128)S(1)} %collective-permute-done.12.refs_1_, f32[6,8,4096]{2,1,0:T(8,128)S(1)} %collective-permute-done.13.refs_2_, ...), custom_call_target="tpu_custom_call" | custom-call | flops 157286400 | bytes 11796480 | tf_op jit(solution)/shard_map/pallas_call | solution.py:399
  132.3 2.2 %shard_map.81 = f32[6,3,8,4096]{3,2,1,0:T(8,128)} custom-call(f32[32,128]{1,0:T(8,128)S(1)} %shard_map.78.t_ref, f32[6,8,4096]{2,1,0:T(8,128)S(1)} %get-tuple-element.35.part_ref, f32[6,8,4096]{2,1,0:T(8,128)S(1)} %collective-permute-done.21.refs_0_, f32[6,8,4096]{2,1,0:T(8,128)S(1)} %collective-permute-done.22.refs_1_, ...), custom_call_target="tpu_custom_call", output_to_operand_aliasing={{}: (4, {})} | custom-call | flops 78643200 | bytes 3932160 | tf_op jit(solution)/shard_map/pallas_call | solution.py:409
  (42 shorter events, 7.0 us)
Async XLA Ops:
  0.0 1.7 %copy-start = (f32[6,3,8,4096]{3,2,1,0:T(8,128)S(1)}, f32[6,3,8,4096]{3,2,1,0:T(8,128)}, u32[]{:S(2)}) copy-start(f32[6,3,8,4096]{3,2,1,0:T(8,128)} %x_ref.3) | copy-start | bytes 7077892
  1.7 0.9 copy-start.2
  2.6 11.7 %copy-start.1 = (f32[6,3,8,4096]{3,2,1,0:T(8,128)S(1)}, f32[6,3,8,4096]{3,2,1,0:T(8,128)}, u32[]{:S(2)}) copy-start(f32[6,3,8,4096]{3,2,1,0:T(8,128)} %x_ref.3) | copy-start | bytes 7077892
  2.6 11.7 %copy-start.3 = (f32[8,4096]{1,0:T(8,128)S(1)}, f32[8,4096]{1,0:T(8,128)}, u32[]{:S(2)}) copy-start(f32[8,4096]{1,0:T(8,128)} %b_ref.7) | copy-start | bytes 393220
  2.7 7.2 %collective-permute-start = (f32[6,1,4096]{2,1,0:T(1,128)S(1)}, f32[6,1,4096]{2,1,0:T(1,128)S(1)}, u32[]{:S(2)}, u32[]{:S(2)}) collective-permute-start(f32[6,1,4096]{2,1,0:T(1,128)S(1)} %get-tuple-element.21), channel_id=1, source_target_pairs={{0,1},{1,2},{2,3},{3,4},{4,5},{5,6},{6,7},{8,9},{9,10},{10,11},{11... | collective-permute-start | bytes 294920 | tf_op jit(solution)/shard_map/ppermute | solution.py:32
  7.8 6.5 %collective-permute-start.1 = (f32[6,1,4096]{2,1,0:T(1,128)S(1)}, f32[6,1,4096]{2,1,0:T(1,128)S(1)}, u32[]{:S(2)}, u32[]{:S(2)}) collective-permute-start(f32[6,1,4096]{2,1,0:T(1,128)S(1)} %get-tuple-element.22), channel_id=1, source_target_pairs={{1,0},{2,1},{3,2},{4,3},{5,4},{6,5},{7,6},{9,8},{10,9},{11,10},{12... | collective-permute-start | bytes 294920 | tf_op jit(solution)/shard_map/ppermute | solution.py:33
  15.9 22.3 %copy-start.5 = (s32[4,128]{1,0:T(4,128)S(1)}, s32[4,128]{1,0:T(4,128)}, u32[]{:S(2)}) copy-start(s32[4,128]{1,0:T(4,128)} %cell_ref.1) | copy-start | bytes 6148
  15.9 8.0 %collective-permute-start.2 = (f32[6,1,4096]{2,1,0:T(1,128)}, f32[6,1,4096]{2,1,0:T(1,128)S(1)}, u32[]{:S(2)}, u32[]{:S(2)}) collective-permute-start(f32[6,1,4096]{2,1,0:T(1,128)} %get-tuple-element.24), channel_id=1, source_target_pairs={{0,1},{1,2},{2,3},{3,4},{4,5},{5,6},{6,7},{8,9},{9,10},{10,11},{11... | collective-permute-start | bytes 294920 | tf_op jit(solution)/shard_map/ppermute | solution.py:32
  20.4 6.7 %collective-permute-start.3 = (f32[6,1,4096]{2,1,0:T(1,128)}, f32[6,1,4096]{2,1,0:T(1,128)S(1)}, u32[]{:S(2)}, u32[]{:S(2)}) collective-permute-start(f32[6,1,4096]{2,1,0:T(1,128)} %get-tuple-element.25), channel_id=1, source_target_pairs={{1,0},{2,1},{3,2},{4,3},{5,4},{6,5},{7,6},{9,8},{10,9},{11,10},{12... | collective-permute-start | bytes 294920 | tf_op jit(solution)/shard_map/ppermute | solution.py:33
  28.2 6.6 %collective-permute-start.4 = (f32[6,1,4096]{2,1,0:T(1,128)S(1)}, f32[6,1,4096]{2,1,0:T(1,128)S(1)}, u32[]{:S(2)}, u32[]{:S(2)}) collective-permute-start(f32[6,1,4096]{2,1,0:T(1,128)S(1)} %get-tuple-element.28), channel_id=1, source_target_pairs={{0,1},{1,2},{2,3},{3,4},{4,5},{5,6},{6,7},{8,9},{9,10},{10,11},{11... | collective-permute-start | bytes 294920 | tf_op jit(solution)/shard_map/ppermute | solution.py:32
  31.7 6.5 %collective-permute-start.5 = (f32[6,1,4096]{2,1,0:T(1,128)S(1)}, f32[6,1,4096]{2,1,0:T(1,128)S(1)}, u32[]{:S(2)}, u32[]{:S(2)}) collective-permute-start(f32[6,1,4096]{2,1,0:T(1,128)S(1)} %get-tuple-element.29), channel_id=1, source_target_pairs={{1,0},{2,1},{3,2},{4,3},{5,4},{6,5},{7,6},{9,8},{10,9},{11,10},{12... | collective-permute-start | bytes 294920 | tf_op jit(solution)/shard_map/ppermute | solution.py:33
  38.2 69.0 %copy-start.4 = (f32[6,4,128]{2,1,0:T(4,128)S(1)}, f32[6,4,128]{2,1,0:T(4,128)}, u32[]{:S(2)}) copy-start(f32[6,4,128]{2,1,0:T(4,128)} %pert_ref.1) | copy-start | bytes 36868
  38.2 69.0 %copy-start.6 = (f32[4,128]{1,0:T(4,128)S(1)}, f32[4,128]{1,0:T(4,128)}, u32[]{:S(2)}) copy-start(f32[4,128]{1,0:T(4,128)} %obs_ref.1) | copy-start | bytes 6148
  38.2 69.0 %copy-start.7 = (f32[4,128]{1,0:T(4,128)S(1)}, f32[4,128]{1,0:T(4,128)}, u32[]{:S(2)}) copy-start(f32[4,128]{1,0:T(4,128)} %scale_ref.1) | copy-start | bytes 6148
  49.7 7.7 %collective-permute-start.18 = (f32[6,1,4096]{2,1,0:T(1,128)S(1)}, f32[6,1,4096]{2,1,0:T(1,128)S(1)}, u32[]{:S(2)}, u32[]{:S(2)}) collective-permute-start(f32[6,1,4096]{2,1,0:T(1,128)S(1)} %get-tuple-element.33), channel_id=1, source_target_pairs={{0,1},{1,2},{2,3},{3,4},{4,5},{5,6},{6,7},{8,9},{9,10},{10,11},{11... | collective-permute-start | bytes 294920 | tf_op jit(solution)/shard_map/ppermute | solution.py:32
  54.1 6.5 %collective-permute-start.19 = (f32[6,1,4096]{2,1,0:T(1,128)S(1)}, f32[6,1,4096]{2,1,0:T(1,128)S(1)}, u32[]{:S(2)}, u32[]{:S(2)}) collective-permute-start(f32[6,1,4096]{2,1,0:T(1,128)S(1)} %get-tuple-element.34), channel_id=1, source_target_pairs={{1,0},{2,1},{3,2},{4,3},{5,4},{6,5},{7,6},{9,8},{10,9},{11,10},{12... | collective-permute-start | bytes 294920 | tf_op jit(solution)/shard_map/ppermute | solution.py:33
  55.4 64.7 %collective-permute-start.15 = (f32[6,8,4096]{2,1,0:T(8,128)S(1)}, f32[6,8,4096]{2,1,0:T(8,128)S(1)}, u32[]{:S(2)}, u32[]{:S(2)}) collective-permute-start(f32[6,8,4096]{2,1,0:T(8,128)S(1)} %get-tuple-element.32.w_ref.refs_4_), channel_id=1, source_target_pairs={{0,16},{8,24},{16,0},{24,8},{1,17},{9,25},{17,1},{25,9},{2,18},{10... | collective-permute-start | bytes 2359304 | tf_op jit(solution)/shard_map/ppermute | solution.py:59
  56.9 63.7 %collective-permute-start.16 = (f32[6,8,4096]{2,1,0:T(8,128)S(1)}, f32[6,8,4096]{2,1,0:T(8,128)S(1)}, u32[]{:S(2)}, u32[]{:S(2)}) collective-permute-start(f32[6,8,4096]{2,1,0:T(8,128)S(1)} %get-tuple-element.32.w_ref.refs_4_), channel_id=1, source_target_pairs={{0,8},{8,0},{16,24},{24,16},{1,9},{9,1},{17,25},{25,17},{2,10},{10... | collective-permute-start | bytes 2359304 | tf_op jit(solution)/shard_map/ppermute | solution.py:66
  56.9 63.7 %collective-permute-start.12 = (f32[6,8,4096]{2,1,0:T(8,128)S(1)}, f32[6,8,4096]{2,1,0:T(8,128)S(1)}, u32[]{:S(2)}, u32[]{:S(2)}) collective-permute-start(f32[6,8,4096]{2,1,0:T(8,128)S(1)} %get-tuple-element.31.h_ref.refs_0_), channel_id=1, source_target_pairs={{0,16},{8,24},{16,0},{24,8},{1,17},{9,25},{17,1},{25,9},{2,18},{10... | collective-permute-start | bytes 2359304 | tf_op jit(solution)/shard_map/ppermute | solution.py:59
  61.5 59.6 %collective-permute-start.21 = (f32[6,8,4096]{2,1,0:T(8,128)S(1)}, f32[6,8,4096]{2,1,0:T(8,128)S(1)}, u32[]{:S(2)}, u32[]{:S(2)}) collective-permute-start(f32[6,8,4096]{2,1,0:T(8,128)S(1)} %shard_map.79.refs_8_), channel_id=1, source_target_pairs={{0,16},{8,24},{16,0},{24,8},{1,17},{9,25},{17,1},{25,9},{2,18},{10... | collective-permute-start | bytes 2359304 | tf_op jit(solution)/shard_map/ppermute | solution.py:59
  63.1 41.7 %collective-permute-start.6 = (f32[4,8,128]{2,1,0:T(8,128)S(1)}, f32[4,8,128]{2,1,0:T(8,128)S(1)}, u32[]{:S(2)}, u32[]{:S(2)}) collective-permute-start(f32[4,8,128]{2,1,0:T(8,128)S(1)} %get-tuple-element.30.refs_0_), channel_id=1, source_target_pairs={{0,16},{8,24},{16,0},{24,8},{1,17},{9,25},{17,1},{25,9},{2,18},{10... | collective-permute-start | bytes 49160 | tf_op jit(solution)/shard_map/ppermute | solution.py:59
  104.8 1.2 collective-permute-start.7
  105.9 1.2 collective-permute-start.8
  107.5 4.1 %collective-permute-start.9 = (f32[32,128]{1,0:T(8,128)S(1)}, f32[32,128]{1,0:T(8,128)S(1)}, u32[]{:S(2)}, u32[]{:S(2)}) collective-permute-start(f32[32,128]{1,0:T(8,128)S(1)} %shard_map.77), channel_id=1, source_target_pairs={{0,1},{1,0},{2,3},{3,2},{4,5},{5,4},{6,7},{7,6},{8,9},{9,8},{10,11... | collective-permute-start | bytes 49160 | tf_op jit(solution)/shard_map/ppermute | solution.py:43
  111.7 3.7 %collective-permute-start.10 = (f32[32,128]{1,0:T(8,128)S(1)}, f32[32,128]{1,0:T(8,128)S(1)}, u32[]{:S(2)}, u32[]{:S(2)}) collective-permute-start(f32[32,128]{1,0:T(8,128)S(1)} %add.9), channel_id=1, source_target_pairs={{0,2},{1,3},{2,0},{3,1},{4,6},{5,7},{6,4},{7,5},{8,10},{9,11},{10,... | collective-permute-start | bytes 49160 | tf_op jit(solution)/shard_map/ppermute | solution.py:43
  115.4 4.6 %collective-permute-start.11 = (f32[32,128]{1,0:T(8,128)S(1)}, f32[32,128]{1,0:T(8,128)S(1)}, u32[]{:S(2)}, u32[]{:S(2)}) collective-permute-start(f32[32,128]{1,0:T(8,128)S(1)} %add.10), channel_id=1, source_target_pairs={{0,4},{1,5},{2,6},{3,7},{4,0},{5,1},{6,2},{7,3},{8,12},{9,13},{10,... | collective-permute-start | bytes 49160 | tf_op jit(solution)/shard_map/ppermute | solution.py:43
  120.1 3.5 %collective-permute-start.13 = (f32[6,8,4096]{2,1,0:T(8,128)S(1)}, f32[6,8,4096]{2,1,0:T(8,128)S(1)}, u32[]{:S(2)}, u32[]{:S(2)}) collective-permute-start(f32[6,8,4096]{2,1,0:T(8,128)S(1)} %get-tuple-element.31.h_ref.refs_0_), channel_id=1, source_target_pairs={{0,8},{8,0},{16,24},{24,16},{1,9},{9,1},{17,25},{25,17},{2,10},{10... | collective-permute-start | bytes 2359304 | tf_op jit(solution)/shard_map/ppermute | solution.py:66
  120.1 3.5 %collective-permute-start.20 = (f32[6,8,4096]{2,1,0:T(8,128)S(1)}, f32[6,8,4096]{2,1,0:T(8,128)S(1)}, u32[]{:S(2)}, u32[]{:S(2)}) collective-permute-start(f32[6,8,4096]{2,1,0:T(8,128)S(1)} %shard_map.79.refs_8_), channel_id=1, source_target_pairs={{0,8},{8,0},{16,24},{24,16},{1,9},{9,1},{17,25},{25,17},{2,10},{10... | collective-permute-start | bytes 2359304 | tf_op jit(solution)/shard_map/ppermute | solution.py:66
  120.6 4.0 %collective-permute-start.17 = (f32[6,8,4096]{2,1,0:T(8,128)S(1)}, f32[6,8,4096]{2,1,0:T(8,128)S(1)}, u32[]{:S(2)}, u32[]{:S(2)}) collective-permute-start(f32[6,8,4096]{2,1,0:T(8,128)S(1)} %collective-permute-done.15.refs_5_), channel_id=1, source_target_pairs={{0,8},{8,0},{16,24},{24,16},{1,9},{9,1},{17,25},{25,17},{2,10},{10... | collective-permute-start | bytes 2359304 | tf_op jit(solution)/shard_map/ppermute | solution.py:66
  120.7 5.1 %collective-permute-start.14 = (f32[6,8,4096]{2,1,0:T(8,128)S(1)}, f32[6,8,4096]{2,1,0:T(8,128)S(1)}, u32[]{:S(2)}, u32[]{:S(2)}) collective-permute-start(f32[6,8,4096]{2,1,0:T(8,128)S(1)} %collective-permute-done.12.refs_1_), channel_id=1, source_target_pairs={{0,8},{8,0},{16,24},{24,16},{1,9},{9,1},{17,25},{25,17},{2,10},{10... | collective-permute-start | bytes 2359304 | tf_op jit(solution)/shard_map/ppermute | solution.py:66
  121.1 11.2 %collective-permute-start.22 = (f32[6,8,4096]{2,1,0:T(8,128)S(1)}, f32[6,8,4096]{2,1,0:T(8,128)S(1)}, u32[]{:S(2)}, u32[]{:S(2)}) collective-permute-start(f32[6,8,4096]{2,1,0:T(8,128)S(1)} %collective-permute-done.21.refs_0_), channel_id=1, source_target_pairs={{0,8},{8,0},{16,24},{24,16},{1,9},{9,1},{17,25},{25,17},{2,10},{10... | collective-permute-start | bytes 2359304 | tf_op jit(solution)/shard_map/ppermute | solution.py:66
where the time goes:
time: 135 us
  waiting for transfers between devices  69.3 us (51%)
  starting transfers between devices  34.9 us (26%)
  Pallas kernels  26.9 us (20%)
  local copies, waits for them, and re-layouts  2.59 us (2%)
    ppermute x4, waiting for transfers between devices, far_gather(): lax.ppermute(block, 'mem', [(i, (i + s) % count) for i in range(count)])  41.2 us
    ppermute x4, starting transfers between devices, shift_both(): lax.ppermute(high_edge, 'band', [(i, i + 1) for i in range(count - 1)])  17.2 us
    ppermute x4, waiting for transfers between devices, shift_both(): lax.ppermute(low_edge, 'band', [(i + 1, i) for i in range(count - 1)])  13.9 us
    pallas_call x1, Pallas kernels, body(): call(probe_kernel, [smem, smem] + [vmem] * 6, [vmem] * 4, [field, edge, e...  11.5 us
    ppermute x3, starting transfers between devices, band_sum(): other = lax.ppermute(part, 'band', [(i, i ^ step) for i in range(count)])  7.05 us
    pallas_call x1, Pallas kernels, body(): call(functools.partial(blend_kernel, n, padded, near, width), [smem] + [v...  6.58 us
    ppermute x3, waiting for transfers between devices, band_sum(): other = lax.ppermute(part, 'band', [(i, i ^ step) for i in range(count)])  5.47 us
    ppermute x4, starting transfers between devices, shift_both(): lax.ppermute(low_edge, 'band', [(i + 1, i) for i in range(count - 1)])  5.17 us
  transfers between devices with their start and end apart: 23, of which 15 were waited for; matrix products, arithmetic and copies ran while one was open for 0% of the time, Pallas kernels for 8%

commit v1 on v0

v1 whole, which is shorter than its diff:
```python
import functools
import math

import jax
import jax.numpy as jnp
from jax import lax
from jax.experimental import pallas as pl
from jax.experimental.pallas import tpu as pltpu
from jax.sharding import PartitionSpec as P


LANES = 128

courant = 0.5
coriolis_base = 0.15
coriolis_slope = 0.3


f32 = jnp.float32


def pad8(count):
    return -(-count // 8) * 8


def cost(flops, moved):
    return pl.CostEstimate(flops=flops, bytes_accessed=moved, transcendentals=0)


def swap_edges(even, odd):
    count = lax.axis_size("band")

    def pairs(start):
        first = [(i, i + 1) for i in range(start, count - 1, 2)]
        return first + [(j, i) for i, j in first]

    even = lax.ppermute(even, "band", pairs(0))
    odd = lax.ppermute(odd, "band", pairs(1))
    return even, odd


def pick(row_ref, rows, top, bottom):
    odd = lax.rem(lax.div(row_ref[0], rows), 2) == 1
    return jnp.where(odd, top, bottom), jnp.where(odd, bottom, top)


def band_sum(part):
    count = lax.axis_size("band")
    if count & (count - 1):
        return lax.psum(part, "band")
    step = 1
    while step < count:
        other = lax.ppermute(part, "band", [(i, i ^ step) for i in range(count)])
        part = part + other
        step *= 2
    return part


def mem_plan(count):
    if count % 2 or count == 1:
        return [(s, None) for s in range(1, count)]
    far = [(2 * s, None) for s in range(1, count // 2)]
    return far


def far_gather(block):
    count = lax.axis_size("mem")
    return [
        lax.ppermute(block, "mem", [(i, (i + s) % count) for i in range(count)])
        for s, _ in mem_plan(count)
    ]


def near_swap(block):
    count = lax.axis_size("mem")
    return lax.ppermute(block, "mem", [(i, i ^ 1) for i in range(count)])


def east(q):
    columns = q.shape[-1]
    return (pltpu.roll(q, columns - 1, 1) - pltpu.roll(q, 1, 1)) * 0.5


def north(q, above, below):
    rows = q.shape[0]
    index = lax.broadcasted_iota(jnp.int32, q.shape, 0)
    up = jnp.where(index == rows - 1, below, pltpu.roll(q, rows - 1, 0))
    down = jnp.where(index == 0, above, pltpu.roll(q, 1, 0))
    return (up - down) * 0.5


def spin(first_row, shape, total_rows):
    rows = (first_row + lax.broadcasted_iota(jnp.int32, shape, 0)).astype(f32)
    return coriolis_base + coriolis_slope * (rows + 0.5) / total_rows


def edge_kernel(row_ref, x_ref, b_ref, even_out, odd_out, speed, depth, sems):
    copies = [
        pltpu.make_async_copy(b_ref, depth, sems.at[0]),
        pltpu.make_async_copy(x_ref.at[:, 2], speed, sems.at[1]),
    ]
    for copy in copies:
        copy.start()
    for copy in copies:
        copy.wait()

    def member(m, _):
        flux = depth[...] * speed[m]
        even_out[m], odd_out[m] = pick(row_ref, depth.shape[0], flux[:1], flux[-1:])
        return 0

    lax.fori_loop(0, x_ref.shape[0], member, 0)


def height_kernel(
    total_rows, row_ref, x_ref, b_ref, even_ref, odd_ref, h_out, u_out, even_out, odd_out
):
    depth = b_ref[...]
    rows = depth.shape[0]
    turn = spin(row_ref[0], depth.shape, total_rows)

    def member(m, _):
        u, v = x_ref[m, 1], x_ref[m, 2]
        above, below = pick(row_ref, rows, even_ref[m], odd_ref[m])
        h = x_ref[m, 0] - courant * (east(depth * u) + north(depth * v, above, below))
        h_out[m] = h
        u_out[m] = u - courant * east(h) + turn * v
        even_out[m], odd_out[m] = pick(row_ref, rows, h[:1], h[-1:])
        return 0

    lax.fori_loop(0, h_out.shape[0], member, 0)


def speed_kernel(
    total_rows, row_ref, h_ref, u_ref, x_ref, b_ref, even_ref, odd_ref, even_out, odd_out, *v_outs
):
    depth = b_ref[...]
    rows = depth.shape[0]
    turn = spin(row_ref[0], depth.shape, total_rows)
    base = 0
    for v_out in v_outs:

        def member(i, _, v_out=v_out, base=base):
            m = base + i
            above, below = pick(row_ref, rows, even_ref[m], odd_ref[m])
            v = x_ref[m, 2] - courant * north(h_ref[m], above, below) - turn * u_ref[m]
            v_out[i] = v
            flux = depth * v
            even_out[m], odd_out[m] = pick(row_ref, rows, flux[:1], flux[-1:])
            return 0

        lax.fori_loop(0, v_out.shape[0], member, 0)
        base += v_out.shape[0]


def split(value, by):
    if by & (by - 1):
        return lax.div(value, by), lax.rem(value, by)
    return lax.shift_right_logical(value, by.bit_length() - 1), value & (by - 1)


def probe_kernel(row_ref, code_ref, h_ref, u_ref, b_ref, even_ref, odd_ref, *refs):
    v_refs, (h_out, even_out, odd_out, out_ref, cells) = refs[:-5], refs[-5:]
    members, rows, columns = h_ref.shape
    stride = rows * columns // LANES
    depth = b_ref[...]
    offset = 0
    for v_ref in v_refs:

        def member(i, _, v_ref=v_ref, offset=offset):
            m = offset + i
            above, below = pick(row_ref, rows, even_ref[m], odd_ref[m])
            h = h_ref[m] - courant * (
                east(depth * u_ref[m]) + north(depth * v_ref[i], above, below)
            )
            h_out[m] = h
            even_out[m], odd_out[m] = pick(row_ref, rows, h[:1], h[-1:])
            base = pl.multiple_of(m * stride, 8)
            for c in range(columns // LANES):
                cells[pl.ds(base + c * rows, rows), :] = h[:, c * LANES : (c + 1) * LANES]
            return 0

        lax.fori_loop(0, v_ref.shape[0], member, 0)
        offset += v_ref.shape[0]
    out_ref[...] = jnp.zeros_like(out_ref)
    lane = lax.broadcasted_iota(jnp.int32, (members, LANES), 1)
    for k in range(out_ref.shape[0]):

        def take(i, held, k=k):
            start, turn = split(code_ref[k, i], LANES)
            piece = cells[pl.ds(start, members, stride=stride), :]
            turned = pltpu.roll(piece, turn, 1)
            return jnp.where(lane == i, turned, held)

        out_ref[k, :members, :] = lax.fori_loop(
            0, LANES, take, jnp.zeros((members, LANES), f32), unroll=16
        )


def pack_kernel(rows, row_ref, even_ref, odd_ref, out_ref):
    width = out_ref.shape[-1]

    def member(m, _):
        for side, line in enumerate(pick(row_ref, rows, even_ref[m], odd_ref[m])):
            for s in range(8):
                out_ref[m, side, s : s + 1, :] = line[:, s * width : (s + 1) * width]
        return 0

    lax.fori_loop(0, out_ref.shape[0], member, 0)


def gram_kernel(total, members, inf_ref, obs_ref, scale_ref, pert_ref, *refs):
    out_ref, spread, both = refs[-3:]
    groups = refs[:-3]
    padded = groups[0].shape[1]
    real = lax.broadcasted_iota(jnp.int32, (padded, LANES), 0) < members
    root = jnp.sqrt(jnp.full((1, LANES), inf_ref[0], f32))
    both[...] = jnp.zeros_like(both)
    for k in range(groups[0].shape[0]):
        at = slice(k * LANES, (k + 1) * LANES)
        scale = scale_ref[k : k + 1, :]
        sums = groups[0][k]
        for g in groups[1:]:
            sums = sums + g[k]
        centre = jnp.sum(sums, axis=0, keepdims=True) / total
        for n, g in enumerate(groups):
            s = jnp.where(real, (g[k] - centre) / (scale * math.sqrt(total - 1)), 0.0)
            spread[n * padded : (n + 1) * padded, at] = s
            both[n * padded : (n + 1) * padded, at] = s
        for m in range(members):
            both[len(groups) * padded + m : len(groups) * padded + m + 1, at] = (
                obs_ref[k : k + 1, :]
                + root * scale * pert_ref[m, k : k + 1, :]
                - groups[0][k, m : m + 1, :]
            ) / scale
    out_ref[...] = lax.dot_general(
        spread[...], both[...], (((1,), (1,)), ((), ())),
        precision=lax.Precision.HIGHEST, preferred_element_type=f32,
    )


def solve_kernel(total, members, groups, inf_ref, part_ref, out_ref):
    a = part_ref[...]
    size = a.shape[0]
    padded = size // groups
    row = lax.broadcasted_iota(jnp.int32, a.shape, 0)
    lane = lax.broadcasted_iota(jnp.int32, a.shape, 1)
    a = a + jnp.where(row == lane, inf_ref[0], 0.0)
    for g in range(groups):
        for m in range(members):
            k = g * padded + m
            pivot = a[k : k + 1, k : k + 1]
            inverse = 1.0 / jnp.sqrt(pivot)
            line = a[k : k + 1, :] * inverse
            column = a[:, k : k + 1] * inverse
            a = jnp.where(row == k, line, a - column * line)
    diagonal = jnp.sum(jnp.where(row == lane, a, 0.0), axis=1, keepdims=True)
    real = lax.rem(row, padded) < members
    w = jnp.where(real, a / diagonal, 0.0)
    mean = jnp.sum(w, axis=0, keepdims=True) / total
    unit = jnp.where(lane - size == row, 1.0, 0.0)
    out_ref[...] = unit + (w - mean) / math.sqrt(total - 1)


def weighted(t_ref, pieces, at, first, members, rows, width, start=None):
    total = list(start) if start is not None else [jnp.zeros((rows, width), f32)] * members
    for g, ref in pieces:
        for i in range(ref.shape[0]):
            value = ref[i, :, at]
            for j in range(members):
                total[j] = total[j] + t_ref[g + i, first + j] * value
    return total


def blend_kernel(lists, first, width, t_ref, *refs):
    outs = refs[-len(lists) :]
    members, rows, columns = outs[0].shape

    def chunk(c, _):
        at = pl.ds(pl.multiple_of(c * width, LANES), width)
        start = 0
        for places, out in zip(lists, outs):
            pieces = list(zip(places, refs[start:]))
            start += len(places)
            for j, t in enumerate(weighted(t_ref, pieces, at, first, members, rows, width)):
                out[j, :, at] = t
        return 0

    lax.fori_loop(0, columns // width, chunk, 0)


def settle_kernel(places, first, width, t_ref, part_ref, *refs):
    pieces = list(zip(places, refs))
    h_out = refs[len(places)]
    members, rows, columns = part_ref.shape

    def chunk(c, _):
        at = pl.ds(pl.multiple_of(c * width, LANES), width)
        start = [part_ref[j, :, at] for j in range(members)]
        for j, t in enumerate(weighted(t_ref, pieces, at, first, members, rows, width, start)):
            h_out[j, :, at] = t
        return 0

    lax.fori_loop(0, columns // width, chunk, 0)


def turn_kernel(total_rows, row_ref, h_ref, u_ref, v_ref, out_ref, v_out, u_new, sems):
    copies = [pltpu.make_async_copy(h_ref, out_ref.at[:, 0], sems.at[0])]
    copies[0].start()
    members, rows, columns = h_ref.shape
    turn = spin(row_ref[0], (rows, columns), total_rows)

    def eastward(j, _):
        u_new[j] = u_ref[j] - courant * east(h_ref[j]) + turn * v_ref[j]
        return 0

    lax.fori_loop(0, members, eastward, 0)
    copies.append(pltpu.make_async_copy(u_new, out_ref.at[:, 1], sems.at[1]))
    copies[1].start()

    def northward(j, _):
        v_out[j] = v_ref[j] - courant * north(h_ref[j], 0.0, 0.0) - turn * u_new[j]
        return 0

    lax.fori_loop(0, members, northward, 0)
    for copy in copies:
        copy.wait()


def finish_kernel(places, first, t_ref, part_ref, *refs):
    ins, (held_ref, out_ref, v_new, sems) = refs[:-4], refs[-4:]
    del held_ref
    members, rows, columns = part_ref.shape
    width = columns // 8
    copies = []
    totals = []
    for side in range(2):
        total = [jnp.zeros((8, width), f32)] * members
        for g, ref in zip(places, ins):
            for i in range(members):
                value = ref[i, side]
                for j in range(members):
                    total[j] = total[j] + t_ref[g + i, first + j] * value
        totals.append(total)
    for j in range(members):
        v_new[j] = part_ref[j]
        for s in range(8):
            at = slice(s * width, (s + 1) * width)
            v_new[j, :1, at] = v_new[j, :1, at] + (courant * 0.5) * totals[0][j][s : s + 1]
            v_new[j, rows - 1 :, at] = (
                v_new[j, rows - 1 :, at] - (courant * 0.5) * totals[1][j][s : s + 1]
            )
        copies.append(pltpu.make_async_copy(v_new.at[j], out_ref.at[j, 2], sems.at[j]))
        copies[-1].start()
    for copy in copies:
        copy.wait()


def body(
    sample_collection,
    seabed_profile,
    gauge_grid_position,
    observed_values,
    error_scale,
    perturbation,
    inflation,
):
    members, _, rows, columns = sample_collection.shape
    bands, mems = lax.axis_size("band"), lax.axis_size("mem")
    total_rows, total = rows * bands, members * mems
    padded = pad8(members)
    first_row = lax.axis_index("band") * rows
    row_index = first_row.reshape(1)

    field = jax.ShapeDtypeStruct((members, rows, columns), f32)
    edge = jax.ShapeDtypeStruct((members, 1, columns), f32)
    smem = pl.BlockSpec(memory_space=pltpu.SMEM)
    vmem = pl.BlockSpec(memory_space=pltpu.VMEM)
    hbm = pl.BlockSpec(memory_space=pl.ANY)
    size = 4 * members * rows * columns

    def call(kernel, ins, outs, shapes, limit, flops, moved, scratch=(), aliases={}):
        return pl.pallas_call(
            kernel,
            in_specs=ins,
            out_specs=outs,
            out_shape=shapes,
            scratch_shapes=list(scratch),
            input_output_aliases=aliases,
            compiler_params=pltpu.CompilerParams(vmem_limit_bytes=limit << 20),
            cost_estimate=cost(flops, moved),
        )

    x = sample_collection
    early = -(-2 * members // 3)
    halves = [count for count in (early, members - early) if count]
    fields = [jax.ShapeDtypeStruct((count, rows, columns), f32) for count in halves]
    even, odd = call(
        edge_kernel, [smem, hbm, hbm], [vmem] * 2, [edge, edge], 60, size, size,
        scratch=[
            pltpu.VMEM((members, rows, columns), f32),
            pltpu.VMEM((rows, columns), f32),
            pltpu.SemaphoreType.DMA((2,)),
        ],
    )(row_index, x, seabed_profile)
    even, odd = swap_edges(even, odd)
    h, u, even, odd = call(
        functools.partial(height_kernel, total_rows),
        [smem] + [vmem] * 4, [vmem] * 4, [field, field, edge, edge], 12, 20 * size, 4 * size,
    )(row_index, x, seabed_profile, even, odd)
    u_far = far_gather(u)
    even, odd = swap_edges(even, odd)
    even, odd, *v = call(
        functools.partial(speed_kernel, total_rows),
        [smem] + [vmem] * 6, [vmem] * (2 + len(halves)), [edge, edge, *fields], 12,
        30 * size, 6 * size,
    )(row_index, h, u, x, seabed_profile, even, odd)
    v_far = []
    for block in v:
        v_far.append(far_gather(block))
    even, odd = swap_edges(even, odd)

    lines = gauge_grid_position.shape[0]
    cell = gauge_grid_position - first_row * columns
    row, column = split(cell, columns)
    block, place = split(column, LANES)
    lane = lax.broadcasted_iota(jnp.int32, cell.shape, 1)
    code = (block * rows + row) * LANES + ((lane - place) & (LANES - 1))
    h, even, odd, predicted = call(
        probe_kernel,
        [smem, smem] + [vmem] * (5 + len(v)), [vmem] * 4,
        [field, edge, edge, jax.ShapeDtypeStruct((lines, padded, LANES), f32)], 12,
        20 * size, 4 * size,
        scratch=[pltpu.VMEM((members * rows * columns // LANES, LANES), f32)],
    )(row_index, code, h, u, seabed_profile, even, odd, *v)
    gathered = [predicted] + far_gather(predicted)
    if mems % 2 == 0:
        gathered = gathered + [near_swap(b) for b in gathered]
    n = len(gathered)
    height_rows = n * padded
    reach = -(-(height_rows + padded) // LANES) * LANES
    partial = call(
        functools.partial(gram_kernel, total, members),
        [smem] + [vmem] * (3 + n), vmem, jax.ShapeDtypeStruct((height_rows, reach), f32), 8,
        1000000, 200000,
        scratch=[
            pltpu.VMEM((height_rows, lines * LANES), f32),
            pltpu.VMEM((reach, lines * LANES), f32),
        ],
    )(inflation, observed_values, error_scale, perturbation, *gathered)
    summed = band_sum(partial)
    transform = call(
        functools.partial(solve_kernel, total, members, n),
        [smem, vmem], vmem, jax.ShapeDtypeStruct((height_rows, reach), f32), 4,
        1000000, 40000,
    )(inflation, summed)

    h_far = far_gather(h)
    even, odd = swap_edges(even, odd)
    rim = call(
        functools.partial(pack_kernel, rows), [smem] + [vmem] * 2, vmem,
        jax.ShapeDtypeStruct((members, 2, 8, columns // 8), f32), 4, size // 4, size // 2,
    )(row_index, even, odd)
    rim_far = far_gather(rim)

    def grouped(own, far):
        if mems % 2:
            return [own] + far
        own_near = near_swap(own)
        return [own] + far + [own_near] + [near_swap(b) for b in far]

    speeds, heights, rims = grouped(u, u_far), grouped(h, h_far), grouped(rim, rim_far)
    sides = [grouped(b, f) for b, f in zip(v, v_far)]
    every = [g * padded for g in range(n)]
    near = [0] if mems % 2 else [0, n // 2]
    far = [g for g in range(n) if g not in near]
    side_places, begin = [], 0
    for count in halves:
        side_places += [g + begin for g in every]
        begin += count
    width = math.gcd(512, columns)
    whole = jax.ShapeDtypeStruct((members, 3, rows, columns), f32)

    def blend(lists, blocks):
        return call(
            functools.partial(blend_kernel, lists, height_rows, width),
            [smem] + [vmem] * len(blocks), [vmem] * len(lists), [field] * len(lists),
            4 + 2 * n, 100 * size, 10 * size,
        )(transform, *blocks)

    u_sum, h_part = blend((every, [every[g] for g in near]), [*speeds, *(heights[g] for g in near)])
    (v_sum,) = blend((side_places,), [b for side in sides for b in side])
    h_new = call(
        functools.partial(settle_kernel, [every[g] for g in far], height_rows, width),
        [smem] + [vmem] * (1 + len(far)), vmem, field, 6 + n, 50 * size, 4 * size,
    )(transform, h_part, *(heights[g] for g in far))
    out, v_part = call(
        functools.partial(turn_kernel, total_rows),
        [smem] + [vmem] * 3, [hbm, vmem], [whole, field], 8, 20 * size, 6 * size,
        scratch=[pltpu.VMEM((members, rows, columns), f32), pltpu.SemaphoreType.DMA((2,))],
    )(row_index, h_new, u_sum, v_sum)
    return call(
        functools.partial(finish_kernel, every, height_rows),
        [smem] + [vmem] * (1 + n) + [hbm], hbm, whole, 4 + n,
        20 * size, 3 * size,
        scratch=[
            pltpu.VMEM((members, rows, columns), f32),
            pltpu.SemaphoreType.DMA((members,)),
        ],
        aliases={2 + n: 0},
    )(transform, v_part, *rims, out)


def solution(mesh):
    in_specs = (
        P("mem", None, "band", None),
        P("band", None),
        P("band", None),
        P("band", None),
        P("band", None),
        P("mem", "band", None),
        P(),
    )
    out_specs = P("mem", None, "band", None)

    return jax.shard_map(body, mesh=mesh, in_specs=in_specs, out_specs=out_specs, check_vma=False)
```

time: 135 us -> 125 us (0.926)
  waiting for transfers between devices: 69.3 us -> 59.4 us
  Pallas kernels: 26.9 us -> 24.6 us
  starting transfers between devices: 34.9 us -> 36.8 us
    ppermute x8, waiting for transfers between devices: 19 us -> 7.73 us  [the longest x4 7.72 us: swap_edges(): even = lax.ppermute(even, 'band', pairs(0))]
    ppermute x4 -> x6, starting transfers between devices: 4.18 us -> 7.16 us  [far_gather(): lax.ppermute(block, 'mem', [(i, (i + s) % count) for i in range(count)])]
    ppermute x8 -> x12, waiting for transfers between devices: 3.7 us -> 6.1 us  [near_swap(): return lax.ppermute(block, 'mem', [(i, i ^ 1) for i in range(count)])]
    pallas_call x7 -> x10, Pallas kernels: 24.2 us -> 21.8 us  [the longest x1 5.53 us: body(): call(probe_kernel, [smem, smem] + [vmem] * (5 + len(v)), [vmem] * 4, [fie...]
    ppermute x3, waiting for transfers between devices: 5.47 us -> 3.44 us  [band_sum(): other = lax.ppermute(part, 'band', [(i, i ^ step) for i in range(count)])]
    ppermute x8, starting transfers between devices: 22.4 us -> 20.8 us  [the longest x4 18.1 us: swap_edges(): even = lax.ppermute(even, 'band', pairs(0))]
    ppermute x4 -> x6, waiting for transfers between devices: 41.2 us -> 42.1 us  [far_gather(): lax.ppermute(block, 'mem', [(i, (i + s) % count) for i in range(count)])]
  transfers between devices with their start and end apart: 23 -> 29, of which waited for: 15 -> 10; matrix products, arithmetic and copies ran while one was open for 0% -> 0% of each run, Pallas kernels for 8% -> 9%
where the time goes in v1:
time: 125 us; the launch traced here: 124 us
  waiting for transfers between devices  59.4 us (48%)
  starting transfers between devices  36.8 us (29%)
  Pallas kernels  24.6 us (20%)
  local copies, waits for them, and re-layouts  2.05 us (2%)
    ppermute x6, waiting for transfers between devices, far_gather(): lax.ppermute(block, 'mem', [(i, (i + s) % count) for i in range(count)])  42.1 us
    ppermute x4, starting transfers between devices, swap_edges(): even = lax.ppermute(even, 'band', pairs(0))  18.1 us
    ppermute x4, waiting for transfers between devices, swap_edges(): even = lax.ppermute(even, 'band', pairs(0))  7.72 us
    ppermute x6, starting transfers between devices, far_gather(): lax.ppermute(block, 'mem', [(i, (i + s) % count) for i in range(count)])  7.16 us
    ppermute x3, starting transfers between devices, band_sum(): other = lax.ppermute(part, 'band', [(i, i ^ step) for i in range(count)])  6.63 us
    ppermute x12, waiting for transfers between devices, near_swap(): return lax.ppermute(block, 'mem', [(i, i ^ 1) for i in range(count)])  6.1 us
    pallas_call x1, Pallas kernels, body(): call(probe_kernel, [smem, smem] + [vmem] * (5 + len(v)), [vmem] * 4, [fie...  5.53 us
    pallas_call x2, Pallas kernels, blend(): call(functools.partial(blend_kernel, lists, height_rows, width), [smem] +...  5.44 us
  transfers between devices with their start and end apart: 29, of which 10 were waited for; matrix products, arithmetic and copies ran while one was open for 0% of the time, Pallas kernels for 9%

profile of v1, /device:TPU:0, one launch (start us, length us, event | category | flops | bytes accessed | tf_op | source)
XLA Modules:
  0.0 123.8 jit_solution(16980003601043486408)
XLA Ops:
  0.0 2.3 %shard_map.73 = (f32[6,1,4096]{2,1,0:T(1,128)}, f32[6,1,4096]{2,1,0:T(1,128)}) custom-call(s32[1]{0:T(128)} %bitcast.row_ref, f32[6,3,8,4096]{3,2,1,0:T(8,128)} %x_ref.5, f32[8,4096]{1,0:T(8,128)} %b_ref.7), custom_call_target="tpu_custom_call" | custom-call | flops 786432 | bytes 786432 | tf_op jit(solution)/shard_map/pallas_call | solution.py:398
  2.3 3.1 %collective-permute-start = (f32[6,1,4096]{2,1,0:T(1,128)}, f32[6,1,4096]{2,1,0:T(1,128)S(1)}, u32[]{:S(2)}, u32[]{:S(2)}) collective-permute-start(f32[6,1,4096]{2,1,0:T(1,128)} %get-tuple-element.23), channel_id=1, source_target_pairs={{0,1},{2,3},{4,5},{6,7},{1,0},{3,2},{5,4},{7,6},{8,9},{10,11},{12,... | collective-permute-start | bytes 294920 | tf_op jit(solution)/shard_map/ppermute | solution.py:37
  6.0 2.3 %collective-permute-done.even_ref = f32[6,1,4096]{2,1,0:T(1,128)S(1)} collective-permute-done((f32[6,1,4096]{2,1,0:T(1,128)}, f32[6,1,4096]{2,1,0:T(1,128)S(1)}, u32[]{:S(2)}, u32[]{:S(2)}) %collective-permute-start) | collective-permute-done | bytes 98336 | tf_op jit(solution)/shard_map/ppermute | solution.py:37
  8.4 2.5 %shard_map.74 = (f32[6,8,4096]{2,1,0:T(8,128)S(1)}, f32[6,8,4096]{2,1,0:T(8,128)S(1)}, f32[6,1,4096]{2,1,0:T(1,128)}, f32[6,1,4096]{2,1,0:T(1,128)}) custom-call(s32[1]{0:T(128)} %bitcast.row_ref, f32[6,3,8,4096]{3,2,1,0:T(8,128)S(1)} %copy-done, f32[8,4096]{1,0:T(8,128)S(1)} %copy-done.4, f32[6,1,4096]{2,1,0:T(1,128)S(1)} %collective-permute-done.even_ref, ...), custom_call_target="tpu_custom_call" | custom-call | flops 15728640 | bytes 3145728 | tf_op jit(solution)/shard_map/pallas_call | solution.py:407
  10.8 0.9 copy-done.1
  11.7 4.7 %collective-permute-start.2 = (f32[6,1,4096]{2,1,0:T(1,128)}, f32[6,1,4096]{2,1,0:T(1,128)S(1)}, u32[]{:S(2)}, u32[]{:S(2)}) collective-permute-start(f32[6,1,4096]{2,1,0:T(1,128)} %get-tuple-element.27), channel_id=1, source_target_pairs={{0,1},{2,3},{4,5},{6,7},{1,0},{3,2},{5,4},{7,6},{8,9},{10,11},{12,... | collective-permute-start | bytes 294920 | tf_op jit(solution)/shard_map/ppermute | solution.py:37
  17.1 2.9 %collective-permute-done.2.even_ref = f32[6,1,4096]{2,1,0:T(1,128)S(1)} collective-permute-done((f32[6,1,4096]{2,1,0:T(1,128)}, f32[6,1,4096]{2,1,0:T(1,128)S(1)}, u32[]{:S(2)}, u32[]{:S(2)}) %collective-permute-start.2) | collective-permute-done | bytes 98336 | tf_op jit(solution)/shard_map/ppermute | solution.py:37
  20.0 1.1 copy-done.2
  21.8 4.6 %collective-permute-start.4 = (f32[6,1,4096]{2,1,0:T(1,128)S(1)}, f32[6,1,4096]{2,1,0:T(1,128)S(1)}, u32[]{:S(2)}, u32[]{:S(2)}) collective-permute-start(f32[6,1,4096]{2,1,0:T(1,128)S(1)} %get-tuple-element.29), channel_id=1, source_target_pairs={{0,1},{2,3},{4,5},{6,7},{1,0},{3,2},{5,4},{7,6},{8,9},{10,11},{12,... | collective-permute-start | bytes 294920 | tf_op jit(solution)/shard_map/ppermute | solution.py:37
  27.1 2.5 %collective-permute-done.4.even_ref = f32[6,1,4096]{2,1,0:T(1,128)S(1)} collective-permute-done((f32[6,1,4096]{2,1,0:T(1,128)S(1)}, f32[6,1,4096]{2,1,0:T(1,128)S(1)}, u32[]{:S(2)}, u32[]{:S(2)}) %collective-permute-start.4) | collective-permute-done | bytes 98336 | tf_op jit(solution)/shard_map/ppermute | solution.py:37
  29.6 5.5 %shard_map.76 = (f32[6,8,4096]{2,1,0:T(8,128)S(1)}, f32[6,1,4096]{2,1,0:T(1,128)S(1)}, f32[6,1,4096]{2,1,0:T(1,128)S(1)}, f32[4,8,128]{2,1,0:T(8,128)S(1)}) custom-call(s32[1]{0:T(128)} %bitcast.row_ref, s32[4,128]{1,0:T(4,128)S(1)} %and_add_fusion.code_ref, f32[6,8,4096]{2,1,0:T(8,128)S(1)} %copy-done.3, f32[6,8,4096]{2,1,0:T(8,128)S(1)} %get-tuple-element.26.u_ref.refs_0_, ...), custom_call_target="tpu_custom_call" | custom-call | flops 15728640 | bytes 3145728 | tf_op jit(solution)/shard_map/pallas_call | solution.py:429
  35.2 1.6 %collective-permute-start.6 = (f32[4,8,128]{2,1,0:T(8,128)S(1)}, f32[4,8,128]{2,1,0:T(8,128)S(1)}, u32[]{:S(2)}, u32[]{:S(2)}) collective-permute-start(f32[4,8,128]{2,1,0:T(8,128)S(1)} %get-tuple-element.33.refs_0_), channel_id=1, source_target_pairs={{0,16},{8,24},{16,0},{24,8},{1,17},{9,25},{17,1},{25,9},{2,18},{10... | collective-permute-start | bytes 49160 | tf_op jit(solution)/shard_map/ppermute | solution.py:69
  36.7 2.2 %collective-permute-done.6.refs_1_ = f32[4,8,128]{2,1,0:T(8,128)S(1)} collective-permute-done((f32[4,8,128]{2,1,0:T(8,128)S(1)}, f32[4,8,128]{2,1,0:T(8,128)S(1)}, u32[]{:S(2)}, u32[]{:S(2)}) %collective-permute-start.6) | collective-permute-done | bytes 16416 | tf_op jit(solution)/shard_map/ppermute | solution.py:69
  39.0 5.7 %collective-permute-start.24 = (f32[6,1,4096]{2,1,0:T(1,128)S(1)}, f32[6,1,4096]{2,1,0:T(1,128)S(1)}, u32[]{:S(2)}, u32[]{:S(2)}) collective-permute-start(f32[6,1,4096]{2,1,0:T(1,128)S(1)} %get-tuple-element.38), channel_id=1, source_target_pairs={{0,1},{2,3},{4,5},{6,7},{1,0},{3,2},{5,4},{7,6},{8,9},{10,11},{12,... | collective-permute-start | bytes 294920 | tf_op jit(solution)/shard_map/ppermute | solution.py:37
  46.3 1.5 %collective-permute-start.21 = (f32[2,8,4096]{2,1,0:T(8,128)S(1)}, f32[2,8,4096]{2,1,0:T(8,128)S(1)}, u32[]{:S(2)}, u32[]{:S(2)}) collective-permute-start(f32[2,8,4096]{2,1,0:T(8,128)S(1)} %get-tuple-element.32.refs_1_.refs_4_), channel_id=1, source_target_pairs={{0,16},{8,24},{16,0},{24,8},{1,17},{9,25},{17,1},{25,9},{2,18},{10... | collective-permute-start | bytes 786440 | tf_op jit(solution)/shard_map/ppermute | solution.py:69
  48.4 1.5 %collective-permute-start.16 = (f32[6,8,4096]{2,1,0:T(8,128)S(1)}, f32[6,8,4096]{2,1,0:T(8,128)S(1)}, u32[]{:S(2)}, u32[]{:S(2)}) collective-permute-start(f32[6,8,4096]{2,1,0:T(8,128)S(1)} %get-tuple-element.34.refs_4_), channel_id=1, source_target_pairs={{0,16},{8,24},{16,0},{24,8},{1,17},{9,25},{17,1},{25,9},{2,18},{10... | collective-permute-start | bytes 2359304 | tf_op jit(solution)/shard_map/ppermute | solution.py:69
  49.9 3.0 %collective-permute-start.10 = (f32[32,128]{1,0:T(8,128)S(1)}, f32[32,128]{1,0:T(8,128)S(1)}, u32[]{:S(2)}, u32[]{:S(2)}) collective-permute-start(f32[32,128]{1,0:T(8,128)S(1)} %add.17), channel_id=1, source_target_pairs={{0,2},{1,3},{2,0},{3,1},{4,6},{5,7},{6,4},{7,5},{8,10},{9,11},{10,... | collective-permute-start | bytes 49160 | tf_op jit(solution)/shard_map/ppermute | solution.py:53
  52.9 1.7 %collective-permute-done.10 = f32[32,128]{1,0:T(8,128)S(1)} collective-permute-done((f32[32,128]{1,0:T(8,128)S(1)}, f32[32,128]{1,0:T(8,128)S(1)}, u32[]{:S(2)}, u32[]{:S(2)}) %collective-permute-start.10) | collective-permute-done | bytes 16416 | tf_op jit(solution)/shard_map/ppermute | solution.py:53
  54.6 3.0 %collective-permute-start.11 = (f32[32,128]{1,0:T(8,128)S(1)}, f32[32,128]{1,0:T(8,128)S(1)}, u32[]{:S(2)}, u32[]{:S(2)}) collective-permute-start(f32[32,128]{1,0:T(8,128)S(1)} %add.18), channel_id=1, source_target_pairs={{0,4},{1,5},{2,6},{3,7},{4,0},{5,1},{6,2},{7,3},{8,12},{9,13},{10,... | collective-permute-start | bytes 49160 | tf_op jit(solution)/shard_map/ppermute | solution.py:53
  57.7 1.7 %collective-permute-done.11 = f32[32,128]{1,0:T(8,128)S(1)} collective-permute-done((f32[32,128]{1,0:T(8,128)S(1)}, f32[32,128]{1,0:T(8,128)S(1)}, u32[]{:S(2)}, u32[]{:S(2)}) %collective-permute-start.11) | collective-permute-done | bytes 16416 | tf_op jit(solution)/shard_map/ppermute | solution.py:53
  59.4 0.7 collective-permute-start.25
  61.3 0.9 collective-permute-done.22.refs_6_
  62.2 1.5 %collective-permute-start.26 = (f32[6,2,8,512]{3,2,1,0:T(8,128)S(1)}, f32[6,2,8,512]{3,2,1,0:T(8,128)S(1)}, u32[]{:S(2)}, u32[]{:S(2)}) collective-permute-start(f32[6,2,8,512]{3,2,1,0:T(8,128)S(1)} %shard_map.83.refs_0_), channel_id=1, source_target_pairs={{0,16},{8,24},{16,0},{24,8},{1,17},{9,25},{17,1},{25,9},{2,18},{10... | collective-permute-start | bytes 589832 | tf_op jit(solution)/shard_map/ppermute | solution.py:69
  63.7 39.9 %collective-permute-done.26.refs_1_ = f32[6,2,8,512]{3,2,1,0:T(8,128)S(1)} collective-permute-done((f32[6,2,8,512]{3,2,1,0:T(8,128)S(1)}, f32[6,2,8,512]{3,2,1,0:T(8,128)S(1)}, u32[]{:S(2)}, u32[]{:S(2)}) %collective-permute-start.26) | collective-permute-done | bytes 196640 | tf_op jit(solution)/shard_map/ppermute | solution.py:69
  104.7 1.6 %collective-permute-done.23.refs_7_ = f32[2,8,4096]{2,1,0:T(8,128)S(1)} collective-permute-done((f32[2,8,4096]{2,1,0:T(8,128)S(1)}, f32[2,8,4096]{2,1,0:T(8,128)S(1)}, u32[]{:S(2)}, u32[]{:S(2)}) %collective-permute-start.23) | collective-permute-done | bytes 262176 | tf_op jit(solution)/shard_map/ppermute | solution.py:76
  106.8 3.6 %collective-permute-done.20.refs_3_ = f32[4,8,4096]{2,1,0:T(8,128)S(1)} collective-permute-done((f32[4,8,4096]{2,1,0:T(8,128)S(1)}, f32[4,8,4096]{2,1,0:T(8,128)S(1)}, u32[]{:S(2)}, u32[]{:S(2)}) %collective-permute-start.20) | collective-permute-done | bytes 524320 | tf_op jit(solution)/shard_map/ppermute | solution.py:76
  110.5 2.4 %shard_map.78.t_ref = f32[32,128]{1,0:T(8,128)S(1)} custom-call(f32[1]{0:T(128)S(6)} %copy.10.inf_ref, f32[32,128]{1,0:T(8,128)S(1)} %add.19.part_ref), custom_call_target="tpu_custom_call" | custom-call | flops 1000000 | bytes 40000 | tf_op jit(solution)/shard_map/pallas_call | solution.py:452
  112.9 2.3 %shard_map.81.v_ref = f32[6,8,4096]{2,1,0:T(8,128)S(1)} custom-call(f32[32,128]{1,0:T(8,128)S(1)} %shard_map.78.t_ref, f32[4,8,4096]{2,1,0:T(8,128)S(1)} %get-tuple-element.31.refs_0_, f32[4,8,4096]{2,1,0:T(8,128)S(1)} %collective-permute-done.18.refs_1_, f32[4,8,4096]{2,1,0:T(8,128)S(1)} %collective-permute-done.19.refs_2_, ...), custom_call_target="tpu_custom_call" | custom-call | flops 78643200 | bytes 7864320 | tf_op jit(solution)/shard_map/pallas_call | solution.py:485
  115.2 3.1 %shard_map.79 = (f32[6,8,4096]{2,1,0:T(8,128)S(1)}, f32[6,8,4096]{2,1,0:T(8,128)S(1)}) custom-call(f32[32,128]{1,0:T(8,128)S(1)} %shard_map.78.t_ref, f32[6,8,4096]{2,1,0:T(8,128)S(1)} %get-tuple-element.26.u_ref.refs_0_, f32[6,8,4096]{2,1,0:T(8,128)S(1)} %collective-permute-done.12.refs_1_, f32[6,8,4096]{2,1,0:T(8,128)S(1)} %collective-permute-done.13.refs_2_, ...), custom_call_target="tpu_custom_call" | custom-call | flops 78643200 | bytes 7864320 | tf_op jit(solution)/shard_map/pallas_call | solution.py:485
  118.4 1.6 %shard_map.80.h_ref = f32[6,8,4096]{2,1,0:T(8,128)S(1)} custom-call(f32[32,128]{1,0:T(8,128)S(1)} %shard_map.78.t_ref, f32[6,8,4096]{2,1,0:T(8,128)S(1)} %get-tuple-element.35.part_ref, f32[6,8,4096]{2,1,0:T(8,128)S(1)} %collective-permute-done.16.refs_0_, f32[6,8,4096]{2,1,0:T(8,128)S(1)} %collective-permute-done.17.refs_1_), custom_call_target="tpu_custom_call" | custom-call | flops 39321600 | bytes 3145728 | tf_op jit(solution)/shard_map/pallas_call | solution.py:493
  120.0 1.8 %shard_map.82 = (f32[6,3,8,4096]{3,2,1,0:T(8,128)}, f32[6,8,4096]{2,1,0:T(8,128)S(1)}) custom-call(s32[1]{0:T(128)} %bitcast.row_ref, f32[6,8,4096]{2,1,0:T(8,128)S(1)} %shard_map.80.h_ref, f32[6,8,4096]{2,1,0:T(8,128)S(1)} %get-tuple-element.36.u_ref, f32[6,8,4096]{2,1,0:T(8,128)S(1)} %shard_map.81.v_ref), custom_call_target="tpu_custom_call" | custom-call | flops 15728640 | bytes 4718592 | tf_op jit(solution)/shard_map/pallas_call | solution.py:497
  121.7 2.1 %shard_map.84 = f32[6,3,8,4096]{3,2,1,0:T(8,128)} custom-call(f32[32,128]{1,0:T(8,128)S(1)} %shard_map.78.t_ref, f32[6,8,4096]{2,1,0:T(8,128)S(1)} %get-tuple-element.37.part_ref, f32[6,2,8,512]{3,2,1,0:T(8,128)S(1)} %shard_map.83.refs_0_, f32[6,2,8,512]{3,2,1,0:T(8,128)S(1)} %collective-permute-done.26.refs_1_, ...), custom_call_target="tpu_custom_call", output_to_operand_aliasing={{}: (6, {})} | custom-call | flops 15728640 | bytes 2359296 | tf_op jit(solution)/shard_map/pallas_call | solution.py:502
  (60 shorter events, 7.1 us)
Async XLA Ops:
  2.3 6.1 %collective-permute-start = (f32[6,1,4096]{2,1,0:T(1,128)}, f32[6,1,4096]{2,1,0:T(1,128)S(1)}, u32[]{:S(2)}, u32[]{:S(2)}) collective-permute-start(f32[6,1,4096]{2,1,0:T(1,128)} %get-tuple-element.23), channel_id=1, source_target_pairs={{0,1},{2,3},{4,5},{6,7},{1,0},{3,2},{5,4},{7,6},{8,9},{10,11},{12,... | collective-permute-start | bytes 294920 | tf_op jit(solution)/shard_map/ppermute | solution.py:37
  5.3 3.0 %collective-permute-start.1 = (f32[6,1,4096]{2,1,0:T(1,128)}, f32[6,1,4096]{2,1,0:T(1,128)S(1)}, u32[]{:S(2)}, u32[]{:S(2)}) collective-permute-start(f32[6,1,4096]{2,1,0:T(1,128)} %get-tuple-element.24), channel_id=1, source_target_pairs={{1,2},{3,4},{5,6},{2,1},{4,3},{6,5},{9,10},{11,12},{13,14},{10,9},... | collective-permute-start | bytes 294920 | tf_op jit(solution)/shard_map/ppermute | solution.py:38
  11.7 8.3 %collective-permute-start.2 = (f32[6,1,4096]{2,1,0:T(1,128)}, f32[6,1,4096]{2,1,0:T(1,128)S(1)}, u32[]{:S(2)}, u32[]{:S(2)}) collective-permute-start(f32[6,1,4096]{2,1,0:T(1,128)} %get-tuple-element.27), channel_id=1, source_target_pairs={{0,1},{2,3},{4,5},{6,7},{1,0},{3,2},{5,4},{7,6},{8,9},{10,11},{12,... | collective-permute-start | bytes 294920 | tf_op jit(solution)/shard_map/ppermute | solution.py:37
  16.4 3.5 %collective-permute-start.3 = (f32[6,1,4096]{2,1,0:T(1,128)}, f32[6,1,4096]{2,1,0:T(1,128)S(1)}, u32[]{:S(2)}, u32[]{:S(2)}) collective-permute-start(f32[6,1,4096]{2,1,0:T(1,128)} %get-tuple-element.28), channel_id=1, source_target_pairs={{1,2},{3,4},{5,6},{2,1},{4,3},{6,5},{9,10},{11,12},{13,14},{10,9},... | collective-permute-start | bytes 294920 | tf_op jit(solution)/shard_map/ppermute | solution.py:38
  21.8 23.6 %copy-start.5 = (f32[6,4,128]{2,1,0:T(4,128)S(1)}, f32[6,4,128]{2,1,0:T(4,128)}, u32[]{:S(2)}) copy-start(f32[6,4,128]{2,1,0:T(4,128)} %pert_ref.1) | copy-start | bytes 36868
  21.8 23.6 %copy-start.6 = (f32[4,128]{1,0:T(4,128)S(1)}, f32[4,128]{1,0:T(4,128)}, u32[]{:S(2)}) copy-start(f32[4,128]{1,0:T(4,128)} %obs_ref.1) | copy-start | bytes 6148
  21.8 23.6 %copy-start.7 = (f32[4,128]{1,0:T(4,128)S(1)}, f32[4,128]{1,0:T(4,128)}, u32[]{:S(2)}) copy-start(f32[4,128]{1,0:T(4,128)} %scale_ref.1) | copy-start | bytes 6148
  21.8 7.8 %collective-permute-start.4 = (f32[6,1,4096]{2,1,0:T(1,128)S(1)}, f32[6,1,4096]{2,1,0:T(1,128)S(1)}, u32[]{:S(2)}, u32[]{:S(2)}) collective-permute-start(f32[6,1,4096]{2,1,0:T(1,128)S(1)} %get-tuple-element.29), channel_id=1, source_target_pairs={{0,1},{2,3},{4,5},{6,7},{1,0},{3,2},{5,4},{7,6},{8,9},{10,11},{12,... | collective-permute-start | bytes 294920 | tf_op jit(solution)/shard_map/ppermute | solution.py:37
  26.4 3.2 %collective-permute-start.5 = (f32[6,1,4096]{2,1,0:T(1,128)S(1)}, f32[6,1,4096]{2,1,0:T(1,128)S(1)}, u32[]{:S(2)}, u32[]{:S(2)}) collective-permute-start(f32[6,1,4096]{2,1,0:T(1,128)S(1)} %get-tuple-element.30), channel_id=1, source_target_pairs={{1,2},{3,4},{5,6},{2,1},{4,3},{6,5},{9,10},{11,12},{13,14},{10,9},... | collective-permute-start | bytes 294920 | tf_op jit(solution)/shard_map/ppermute | solution.py:38
  35.2 3.8 %collective-permute-start.6 = (f32[4,8,128]{2,1,0:T(8,128)S(1)}, f32[4,8,128]{2,1,0:T(8,128)S(1)}, u32[]{:S(2)}, u32[]{:S(2)}) collective-permute-start(f32[4,8,128]{2,1,0:T(8,128)S(1)} %get-tuple-element.33.refs_0_), channel_id=1, source_target_pairs={{0,16},{8,24},{16,0},{24,8},{1,17},{9,25},{17,1},{25,9},{2,18},{10... | collective-permute-start | bytes 49160 | tf_op jit(solution)/shard_map/ppermute | solution.py:69
  36.7 8.6 %collective-permute-start.7 = (f32[4,8,128]{2,1,0:T(8,128)S(1)}, f32[4,8,128]{2,1,0:T(8,128)S(1)}, u32[]{:S(2)}, u32[]{:S(2)}) collective-permute-start(f32[4,8,128]{2,1,0:T(8,128)S(1)} %get-tuple-element.33.refs_0_), channel_id=1, source_target_pairs={{0,8},{8,0},{16,24},{24,16},{1,9},{9,1},{17,25},{25,17},{2,10},{10... | collective-permute-start | bytes 49160 | tf_op jit(solution)/shard_map/ppermute | solution.py:76
  39.0 6.4 %collective-permute-start.8 = (f32[4,8,128]{2,1,0:T(8,128)S(1)}, f32[4,8,128]{2,1,0:T(8,128)S(1)}, u32[]{:S(2)}, u32[]{:S(2)}) collective-permute-start(f32[4,8,128]{2,1,0:T(8,128)S(1)} %collective-permute-done.6.refs_1_), channel_id=1, source_target_pairs={{0,8},{8,0},{16,24},{24,16},{1,9},{9,1},{17,25},{25,17},{2,10},{10... | collective-permute-start | bytes 49160 | tf_op jit(solution)/shard_map/ppermute | solution.py:76
  39.0 21.1 %collective-permute-start.24 = (f32[6,1,4096]{2,1,0:T(1,128)S(1)}, f32[6,1,4096]{2,1,0:T(1,128)S(1)}, u32[]{:S(2)}, u32[]{:S(2)}) collective-permute-start(f32[6,1,4096]{2,1,0:T(1,128)S(1)} %get-tuple-element.38), channel_id=1, source_target_pairs={{0,1},{2,3},{4,5},{6,7},{1,0},{3,2},{5,4},{7,6},{8,9},{10,11},{12,... | collective-permute-start | bytes 294920 | tf_op jit(solution)/shard_map/ppermute | solution.py:37
  45.8 4.1 %collective-permute-start.9 = (f32[32,128]{1,0:T(8,128)S(1)}, f32[32,128]{1,0:T(8,128)S(1)}, u32[]{:S(2)}, u32[]{:S(2)}) collective-permute-start(f32[32,128]{1,0:T(8,128)S(1)} %shard_map.77), channel_id=1, source_target_pairs={{0,1},{1,0},{2,3},{3,2},{4,5},{5,4},{6,7},{7,6},{8,9},{9,8},{10,11... | collective-permute-start | bytes 49160 | tf_op jit(solution)/shard_map/ppermute | solution.py:53
  46.3 14.3 %collective-permute-start.21 = (f32[2,8,4096]{2,1,0:T(8,128)S(1)}, f32[2,8,4096]{2,1,0:T(8,128)S(1)}, u32[]{:S(2)}, u32[]{:S(2)}) collective-permute-start(f32[2,8,4096]{2,1,0:T(8,128)S(1)} %get-tuple-element.32.refs_1_.refs_4_), channel_id=1, source_target_pairs={{0,16},{8,24},{16,0},{24,8},{1,17},{9,25},{17,1},{25,9},{2,18},{10... | collective-permute-start | bytes 786440 | tf_op jit(solution)/shard_map/ppermute | solution.py:69
  47.8 56.3 %collective-permute-start.12 = (f32[6,8,4096]{2,1,0:T(8,128)S(1)}, f32[6,8,4096]{2,1,0:T(8,128)S(1)}, u32[]{:S(2)}, u32[]{:S(2)}) collective-permute-start(f32[6,8,4096]{2,1,0:T(8,128)S(1)} %get-tuple-element.26.u_ref.refs_0_), channel_id=1, source_target_pairs={{0,16},{8,24},{16,0},{24,8},{1,17},{9,25},{17,1},{25,9},{2,18},{10... | collective-permute-start | bytes 2359304 | tf_op jit(solution)/shard_map/ppermute | solution.py:69
  48.4 56.3 %collective-permute-start.16 = (f32[6,8,4096]{2,1,0:T(8,128)S(1)}, f32[6,8,4096]{2,1,0:T(8,128)S(1)}, u32[]{:S(2)}, u32[]{:S(2)}) collective-permute-start(f32[6,8,4096]{2,1,0:T(8,128)S(1)} %get-tuple-element.34.refs_4_), channel_id=1, source_target_pairs={{0,16},{8,24},{16,0},{24,8},{1,17},{9,25},{17,1},{25,9},{2,18},{10... | collective-permute-start | bytes 2359304 | tf_op jit(solution)/shard_map/ppermute | solution.py:69
  49.9 4.8 %collective-permute-start.10 = (f32[32,128]{1,0:T(8,128)S(1)}, f32[32,128]{1,0:T(8,128)S(1)}, u32[]{:S(2)}, u32[]{:S(2)}) collective-permute-start(f32[32,128]{1,0:T(8,128)S(1)} %add.17), channel_id=1, source_target_pairs={{0,2},{1,3},{2,0},{3,1},{4,6},{5,7},{6,4},{7,5},{8,10},{9,11},{10,... | collective-permute-start | bytes 49160 | tf_op jit(solution)/shard_map/ppermute | solution.py:53
  54.6 4.7 %collective-permute-start.11 = (f32[32,128]{1,0:T(8,128)S(1)}, f32[32,128]{1,0:T(8,128)S(1)}, u32[]{:S(2)}, u32[]{:S(2)}) collective-permute-start(f32[32,128]{1,0:T(8,128)S(1)} %add.18), channel_id=1, source_target_pairs={{0,4},{1,5},{2,6},{3,7},{4,0},{5,1},{6,2},{7,3},{8,12},{9,13},{10,... | collective-permute-start | bytes 49160 | tf_op jit(solution)/shard_map/ppermute | solution.py:53
  59.4 1.3 %collective-permute-start.25 = (f32[6,1,4096]{2,1,0:T(1,128)S(1)}, f32[6,1,4096]{2,1,0:T(1,128)S(1)}, u32[]{:S(2)}, u32[]{:S(2)}) collective-permute-start(f32[6,1,4096]{2,1,0:T(1,128)S(1)} %get-tuple-element.39), channel_id=1, source_target_pairs={{1,2},{3,4},{5,6},{2,1},{4,3},{6,5},{9,10},{11,12},{13,14},{10,9},... | collective-permute-start | bytes 294920 | tf_op jit(solution)/shard_map/ppermute | solution.py:38
  60.1 43.5 %collective-permute-start.18 = (f32[4,8,4096]{2,1,0:T(8,128)S(1)}, f32[4,8,4096]{2,1,0:T(8,128)S(1)}, u32[]{:S(2)}, u32[]{:S(2)}) collective-permute-start(f32[4,8,4096]{2,1,0:T(8,128)S(1)} %get-tuple-element.31.refs_0_), channel_id=1, source_target_pairs={{0,16},{8,24},{16,0},{24,8},{1,17},{9,25},{17,1},{25,9},{2,18},{10... | collective-permute-start | bytes 1572872 | tf_op jit(solution)/shard_map/ppermute | solution.py:69
  60.7 1.5 %collective-permute-start.22 = (f32[2,8,4096]{2,1,0:T(8,128)S(1)}, f32[2,8,4096]{2,1,0:T(8,128)S(1)}, u32[]{:S(2)}, u32[]{:S(2)}) collective-permute-start(f32[2,8,4096]{2,1,0:T(8,128)S(1)} %get-tuple-element.32.refs_1_.refs_4_), channel_id=1, source_target_pairs={{0,8},{8,0},{16,24},{24,16},{1,9},{9,1},{17,25},{25,17},{2,10},{10... | collective-permute-start | bytes 786440 | tf_op jit(solution)/shard_map/ppermute | solution.py:76
  60.7 43.4 %collective-permute-start.19 = (f32[4,8,4096]{2,1,0:T(8,128)S(1)}, f32[4,8,4096]{2,1,0:T(8,128)S(1)}, u32[]{:S(2)}, u32[]{:S(2)}) collective-permute-start(f32[4,8,4096]{2,1,0:T(8,128)S(1)} %get-tuple-element.31.refs_0_), channel_id=1, source_target_pairs={{0,8},{8,0},{16,24},{24,16},{1,9},{9,1},{17,25},{25,17},{2,10},{10... | collective-permute-start | bytes 1572872 | tf_op jit(solution)/shard_map/ppermute | solution.py:76
  62.2 41.4 %collective-permute-start.26 = (f32[6,2,8,512]{3,2,1,0:T(8,128)S(1)}, f32[6,2,8,512]{3,2,1,0:T(8,128)S(1)}, u32[]{:S(2)}, u32[]{:S(2)}) collective-permute-start(f32[6,2,8,512]{3,2,1,0:T(8,128)S(1)} %shard_map.83.refs_0_), channel_id=1, source_target_pairs={{0,16},{8,24},{16,0},{24,8},{1,17},{9,25},{17,1},{25,9},{2,18},{10... | collective-permute-start | bytes 589832 | tf_op jit(solution)/shard_map/ppermute | solution.py:69
  103.6 2.8 %collective-permute-start.13 = (f32[6,8,4096]{2,1,0:T(8,128)S(1)}, f32[6,8,4096]{2,1,0:T(8,128)S(1)}, u32[]{:S(2)}, u32[]{:S(2)}) collective-permute-start(f32[6,8,4096]{2,1,0:T(8,128)S(1)} %get-tuple-element.26.u_ref.refs_0_), channel_id=1, source_target_pairs={{0,8},{8,0},{16,24},{24,16},{1,9},{9,1},{17,25},{25,17},{2,10},{10... | collective-permute-start | bytes 2359304 | tf_op jit(solution)/shard_map/ppermute | solution.py:76
  103.6 2.7 %collective-permute-start.23 = (f32[2,8,4096]{2,1,0:T(8,128)S(1)}, f32[2,8,4096]{2,1,0:T(8,128)S(1)}, u32[]{:S(2)}, u32[]{:S(2)}) collective-permute-start(f32[2,8,4096]{2,1,0:T(8,128)S(1)} %collective-permute-done.21.refs_5_), channel_id=1, source_target_pairs={{0,8},{8,0},{16,24},{24,16},{1,9},{9,1},{17,25},{25,17},{2,10},{10... | collective-permute-start | bytes 786440 | tf_op jit(solution)/shard_map/ppermute | solution.py:76
  104.1 11.1 %collective-permute-start.15 = (f32[6,8,4096]{2,1,0:T(8,128)S(1)}, f32[6,8,4096]{2,1,0:T(8,128)S(1)}, u32[]{:S(2)}, u32[]{:S(2)}) collective-permute-start(f32[6,8,4096]{2,1,0:T(8,128)S(1)} %get-tuple-element.34.refs_4_), channel_id=1, source_target_pairs={{0,8},{8,0},{16,24},{24,16},{1,9},{9,1},{17,25},{25,17},{2,10},{10... | collective-permute-start | bytes 2359304 | tf_op jit(solution)/shard_map/ppermute | solution.py:76
  104.2 11.1 %collective-permute-start.14 = (f32[6,8,4096]{2,1,0:T(8,128)S(1)}, f32[6,8,4096]{2,1,0:T(8,128)S(1)}, u32[]{:S(2)}, u32[]{:S(2)}) collective-permute-start(f32[6,8,4096]{2,1,0:T(8,128)S(1)} %collective-permute-done.12.refs_1_), channel_id=1, source_target_pairs={{0,8},{8,0},{16,24},{24,16},{1,9},{9,1},{17,25},{25,17},{2,10},{10... | collective-permute-start | bytes 2359304 | tf_op jit(solution)/shard_map/ppermute | solution.py:76
  104.6 13.8 %collective-permute-start.17 = (f32[6,8,4096]{2,1,0:T(8,128)S(1)}, f32[6,8,4096]{2,1,0:T(8,128)S(1)}, u32[]{:S(2)}, u32[]{:S(2)}) collective-permute-start(f32[6,8,4096]{2,1,0:T(8,128)S(1)} %collective-permute-done.16.refs_0_), channel_id=1, source_target_pairs={{0,8},{8,0},{16,24},{24,16},{1,9},{9,1},{17,25},{25,17},{2,10},{10... | collective-permute-start | bytes 2359304 | tf_op jit(solution)/shard_map/ppermute | solution.py:76
  106.2 4.1 %collective-permute-start.20 = (f32[4,8,4096]{2,1,0:T(8,128)S(1)}, f32[4,8,4096]{2,1,0:T(8,128)S(1)}, u32[]{:S(2)}, u32[]{:S(2)}) collective-permute-start(f32[4,8,4096]{2,1,0:T(8,128)S(1)} %collective-permute-done.18.refs_1_), channel_id=1, source_target_pairs={{0,8},{8,0},{16,24},{24,16},{1,9},{9,1},{17,25},{25,17},{2,10},{10... | collective-permute-start | bytes 1572872 | tf_op jit(solution)/shard_map/ppermute | solution.py:76
  106.4 15.3 %collective-permute-start.27 = (f32[6,2,8,512]{3,2,1,0:T(8,128)S(1)}, f32[6,2,8,512]{3,2,1,0:T(8,128)S(1)}, u32[]{:S(2)}, u32[]{:S(2)}) collective-permute-start(f32[6,2,8,512]{3,2,1,0:T(8,128)S(1)} %shard_map.83.refs_0_), channel_id=1, source_target_pairs={{0,8},{8,0},{16,24},{24,16},{1,9},{9,1},{17,25},{25,17},{2,10},{10... | collective-permute-start | bytes 589832 | tf_op jit(solution)/shard_map/ppermute | solution.py:76
  110.4 11.4 %collective-permute-start.28 = (f32[6,2,8,512]{3,2,1,0:T(8,128)S(1)}, f32[6,2,8,512]{3,2,1,0:T(8,128)S(1)}, u32[]{:S(2)}, u32[]{:S(2)}) collective-permute-start(f32[6,2,8,512]{3,2,1,0:T(8,128)S(1)} %collective-permute-done.26.refs_1_), channel_id=1, source_target_pairs={{0,8},{8,0},{16,24},{24,16},{1,9},{9,1},{17,25},{25,17},{2,10},{10... | collective-permute-start | bytes 589832 | tf_op jit(solution)/shard_map/ppermute | solution.py:76
  (6 other events, 42.6 us)

commit v2 on v1

--- a/solution.py
+++ b/solution.py
@@ -112,20 +112,46 @@
     lax.fori_loop(0, x_ref.shape[0], member, 0)
 
 
-def height_kernel(
-    total_rows, row_ref, x_ref, b_ref, even_ref, odd_ref, h_out, u_out, even_out, odd_out
-):
+def index_kernel(rows, columns, row_ref, cell_ref, code_ref):
+    row, column = split(cell_ref[...] - row_ref[0] * columns, columns)
+    block, place = split(column, LANES)
+    lane = lax.broadcasted_iota(jnp.int32, cell_ref.shape, 1)
+    code_ref[...] = (block * rows + row) * LANES + ((lane - place) & (LANES - 1))
+
+
+def begin_kernel(total_rows, row_ref, x_ref, b_ref, h_out, u_out):
     depth = b_ref[...]
-    rows = depth.shape[0]
     turn = spin(row_ref[0], depth.shape, total_rows)
 
     def member(m, _):
         u, v = x_ref[m, 1], x_ref[m, 2]
-        above, below = pick(row_ref, rows, even_ref[m], odd_ref[m])
-        h = x_ref[m, 0] - courant * (east(depth * u) + north(depth * v, above, below))
+        h = x_ref[m, 0] - courant * (east(depth * u) + north(depth * v, 0.0, 0.0))
         h_out[m] = h
         u_out[m] = u - courant * east(h) + turn * v
+        return 0
+
+    lax.fori_loop(0, h_out.shape[0], member, 0)
+
+
+def rim_rows(row_ref, shape, even, odd):
+    rows = shape[0]
+    above, below = pick(row_ref, rows, even, odd)
+    index = lax.broadcasted_iota(jnp.int32, shape, 0)
+    rim = jnp.where(index == 0, above, jnp.where(index == rows - 1, -below, 0.0))
+    return (courant * 0.5) * rim
+
+
+def height_kernel(
+    row_ref, h_ref, u_ref, even_ref, odd_ref, h_out, u_out, even_out, odd_out
+):
+    rows = h_ref.shape[1]
+
+    def member(m, _):
+        rim = rim_rows(row_ref, h_ref.shape[1:], even_ref[m], odd_ref[m])
+        h = h_ref[m] + rim
+        h_out[m] = h
         even_out[m], odd_out[m] = pick(row_ref, rows, h[:1], h[-1:])
+        u_out[m] = u_ref[m] - courant * east(rim)
         return 0
 
     lax.fori_loop(0, h_out.shape[0], member, 0)
@@ -159,29 +185,39 @@
     return lax.shift_right_logical(value, by.bit_length() - 1), value & (by - 1)
 
 
-def probe_kernel(row_ref, code_ref, h_ref, u_ref, b_ref, even_ref, odd_ref, *refs):
-    v_refs, (h_out, even_out, odd_out, out_ref, cells) = refs[:-5], refs[-5:]
-    members, rows, columns = h_ref.shape
-    stride = rows * columns // LANES
+def third_kernel(h_ref, u_ref, b_ref, *refs):
+    v_refs, h_out = refs[:-1], refs[-1]
     depth = b_ref[...]
     offset = 0
     for v_ref in v_refs:
 
         def member(i, _, v_ref=v_ref, offset=offset):
             m = offset + i
-            above, below = pick(row_ref, rows, even_ref[m], odd_ref[m])
-            h = h_ref[m] - courant * (
-                east(depth * u_ref[m]) + north(depth * v_ref[i], above, below)
+            h_out[m] = h_ref[m] - courant * (
+                east(depth * u_ref[m]) + north(depth * v_ref[i], 0.0, 0.0)
             )
-            h_out[m] = h
-            even_out[m], odd_out[m] = pick(row_ref, rows, h[:1], h[-1:])
-            base = pl.multiple_of(m * stride, 8)
-            for c in range(columns // LANES):
-                cells[pl.ds(base + c * rows, rows), :] = h[:, c * LANES : (c + 1) * LANES]
             return 0
 
         lax.fori_loop(0, v_ref.shape[0], member, 0)
         offset += v_ref.shape[0]
+
+
+def probe_kernel(
+    row_ref, code_ref, part_ref, even_ref, odd_ref, h_out, even_out, odd_out, out_ref, cells
+):
+    members, rows, columns = part_ref.shape
+    stride = rows * columns // LANES
+
+    def member(m, _):
+        h = part_ref[m] + rim_rows(row_ref, (rows, columns), even_ref[m], odd_ref[m])
+        h_out[m] = h
+        even_out[m], odd_out[m] = pick(row_ref, rows, h[:1], h[-1:])
+        base = pl.multiple_of(m * stride, 8)
+        for c in range(columns // LANES):
+            cells[pl.ds(base + c * rows, rows), :] = h[:, c * LANES : (c + 1) * LANES]
+        return 0
+
+    lax.fori_loop(0, members, member, 0)
     out_ref[...] = jnp.zeros_like(out_ref)
     lane = lax.broadcasted_iota(jnp.int32, (members, LANES), 1)
     for k in range(out_ref.shape[0]):
@@ -304,35 +340,30 @@
     lax.fori_loop(0, columns // width, chunk, 0)
 
 
-def turn_kernel(total_rows, row_ref, h_ref, u_ref, v_ref, out_ref, v_out, u_new, sems):
-    copies = [pltpu.make_async_copy(h_ref, out_ref.at[:, 0], sems.at[0])]
-    copies[0].start()
+def turn_kernel(total_rows, row_ref, h_ref, u_ref, v_ref, u_out, v_out):
     members, rows, columns = h_ref.shape
     turn = spin(row_ref[0], (rows, columns), total_rows)
 
-    def eastward(j, _):
-        u_new[j] = u_ref[j] - courant * east(h_ref[j]) + turn * v_ref[j]
-        return 0
-
-    lax.fori_loop(0, members, eastward, 0)
-    copies.append(pltpu.make_async_copy(u_new, out_ref.at[:, 1], sems.at[1]))
-    copies[1].start()
-
-    def northward(j, _):
-        v_out[j] = v_ref[j] - courant * north(h_ref[j], 0.0, 0.0) - turn * u_new[j]
-        return 0
-
-    lax.fori_loop(0, members, northward, 0)
-    for copy in copies:
-        copy.wait()
-
-
-def finish_kernel(places, first, t_ref, part_ref, *refs):
-    ins, (held_ref, out_ref, v_new, sems) = refs[:-4], refs[-4:]
-    del held_ref
+    def member(j, _):
+        h, v = h_ref[j], v_ref[j]
+        u = u_ref[j] - courant * east(h) + turn * v
+        u_out[j] = u
+        v_out[j] = v - courant * north(h, 0.0, 0.0) - turn * u
+        return 0
+
+    lax.fori_loop(0, members, member, 0)
+
+
+def finish_kernel(places, first, t_ref, part_ref, h_ref, u_ref, *refs):
+    ins, (out_ref, v_new, sems) = refs[:-3], refs[-3:]
     members, rows, columns = part_ref.shape
     width = columns // 8
-    copies = []
+    copies = [
+        pltpu.make_async_copy(h_ref, out_ref.at[:, 0], sems.at[members]),
+        pltpu.make_async_copy(u_ref, out_ref.at[:, 1], sems.at[members + 1]),
+    ]
+    for copy in copies:
+        copy.start()
     totals = []
     for side in range(2):
         total = [jnp.zeros((8, width), f32)] * members
@@ -404,10 +435,18 @@
         ],
     )(row_index, x, seabed_profile)
     even, odd = swap_edges(even, odd)
+    code = call(
+        functools.partial(index_kernel, rows, columns), [smem, vmem], vmem,
+        jax.ShapeDtypeStruct(gauge_grid_position.shape, jnp.int32), 1, 10000, 4096,
+    )(row_index, gauge_grid_position)
+    h, u = call(
+        functools.partial(begin_kernel, total_rows),
+        [smem] + [vmem] * 2, [vmem] * 2, [field, field], 12, 20 * size, 4 * size,
+    )(row_index, x, seabed_profile)
     h, u, even, odd = call(
-        functools.partial(height_kernel, total_rows),
-        [smem] + [vmem] * 4, [vmem] * 4, [field, field, edge, edge], 12, 20 * size, 4 * size,
-    )(row_index, x, seabed_profile, even, odd)
+        height_kernel,
+        [smem] + [vmem] * 4, [vmem] * 4, [field, field, edge, edge], 12, 5 * size, 4 * size,
+    )(row_index, h, u, even, odd)
     u_far = far_gather(u)
     even, odd = swap_edges(even, odd)
     even, odd, *v = call(
@@ -421,18 +460,16 @@
     even, odd = swap_edges(even, odd)
 
     lines = gauge_grid_position.shape[0]
-    cell = gauge_grid_position - first_row * columns
-    row, column = split(cell, columns)
-    block, place = split(column, LANES)
-    lane = lax.broadcasted_iota(jnp.int32, cell.shape, 1)
-    code = (block * rows + row) * LANES + ((lane - place) & (LANES - 1))
+    h = call(
+        third_kernel, [vmem] * (3 + len(v)), vmem, field, 12, 10 * size, 4 * size,
+    )(h, u, seabed_profile, *v)
     h, even, odd, predicted = call(
         probe_kernel,
-        [smem, smem] + [vmem] * (5 + len(v)), [vmem] * 4,
+        [smem, smem] + [vmem] * 3, [vmem] * 4,
         [field, edge, edge, jax.ShapeDtypeStruct((lines, padded, LANES), f32)], 12,
         20 * size, 4 * size,
         scratch=[pltpu.VMEM((members * rows * columns // LANES, LANES), f32)],
-    )(row_index, code, h, u, seabed_profile, even, odd, *v)
+    )(row_index, code, h, even, odd)
     gathered = [predicted] + far_gather(predicted)
     if mems % 2 == 0:
         gathered = gathered + [near_swap(b) for b in gathered]
@@ -494,21 +531,19 @@
         functools.partial(settle_kernel, [every[g] for g in far], height_rows, width),
         [smem] + [vmem] * (1 + len(far)), vmem, field, 6 + n, 50 * size, 4 * size,
     )(transform, h_part, *(heights[g] for g in far))
-    out, v_part = call(
+    u_new, v_part = call(
         functools.partial(turn_kernel, total_rows),
-        [smem] + [vmem] * 3, [hbm, vmem], [whole, field], 8, 20 * size, 6 * size,
-        scratch=[pltpu.VMEM((members, rows, columns), f32), pltpu.SemaphoreType.DMA((2,))],
+        [smem] + [vmem] * 3, [vmem, vmem], [field, field], 8, 20 * size, 6 * size,
     )(row_index, h_new, u_sum, v_sum)
     return call(
         functools.partial(finish_kernel, every, height_rows),
-        [smem] + [vmem] * (1 + n) + [hbm], hbm, whole, 4 + n,
+        [smem] + [vmem] * (3 + n), hbm, whole, 4 + n,
         20 * size, 3 * size,
         scratch=[
             pltpu.VMEM((members, rows, columns), f32),
-            pltpu.SemaphoreType.DMA((members,)),
+            pltpu.SemaphoreType.DMA((members + 2,)),
         ],
-        aliases={2 + n: 0},
-    )(transform, v_part, *rims, out)
+    )(transform, v_part, h_new, u_new, *rims)
 
 
 def solution(mesh):

time: 125 us -> 120 us (0.960)
  waiting for transfers between devices: 59.4 us -> 56.4 us
  local copies, waits for them, and re-layouts: 2.05 us -> 0.03 us
    ppermute x4, waiting for transfers between devices: 7.72 us -> 4.75 us  [swap_edges(): even = lax.ppermute(even, 'band', pairs(0))]
    unnamed x18 -> x12, local copies, waits for them, and re-layouts: 2.05 us -> 0.03 us
    pallas_call x3 -> x6, Pallas kernels: 9.76 us -> 9.47 us  [the longest x1 4.93 us: body(): call(probe_kernel, [smem, smem] + [vmem] * 3, [vmem] * 4, [field, edge, e...]
  transfers between devices with their start and end apart: 29 -> 29, of which waited for: 10 -> 10; matrix products, arithmetic and copies ran while one was open for 0% -> 0% of each run, Pallas kernels for 9% -> 11%
where the time goes in v2:
time: 120 us; the launch traced here: 119 us
  waiting for transfers between devices  56.4 us (47%)
  starting transfers between devices  37 us (31%)
  Pallas kernels  24.6 us (20%)
    ppermute x6, waiting for transfers between devices, far_gather(): lax.ppermute(block, 'mem', [(i, (i + s) % count) for i in range(count)])  42.1 us
    ppermute x4, starting transfers between devices, swap_edges(): even = lax.ppermute(even, 'band', pairs(0))  18.3 us
    ppermute x6, starting transfers between devices, far_gather(): lax.ppermute(block, 'mem', [(i, (i + s) % count) for i in range(count)])  7.16 us
    ppermute x3, starting transfers between devices, band_sum(): other = lax.ppermute(part, 'band', [(i, i ^ step) for i in range(count)])  6.63 us
    ppermute x12, waiting for transfers between devices, near_swap(): return lax.ppermute(block, 'mem', [(i, i ^ 1) for i in range(count)])  6.1 us
    pallas_call x2, Pallas kernels, blend(): call(functools.partial(blend_kernel, lists, height_rows, width), [smem] +...  5.51 us
    pallas_call x1, Pallas kernels, body(): call(probe_kernel, [smem, smem] + [vmem] * 3, [vmem] * 4, [field, edge, e...  4.93 us
    ppermute x4, waiting for transfers between devices, swap_edges(): even = lax.ppermute(even, 'band', pairs(0))  4.75 us
  transfers between devices with their start and end apart: 29, of which 10 were waited for; matrix products, arithmetic and copies ran while one was open for 0% of the time, Pallas kernels for 11%

profile of v2, /device:TPU:0, one launch (start us, length us, event | category | flops | bytes accessed | tf_op | source)
XLA Modules:
  0.0 119.0 jit_solution(7709997514382369545)
XLA Ops:
  0.0 2.3 %shard_map.75 = (f32[6,1,4096]{2,1,0:T(1,128)}, f32[6,1,4096]{2,1,0:T(1,128)}) custom-call(s32[1]{0:T(128)} %bitcast.row_ref, f32[6,3,8,4096]{3,2,1,0:T(8,128)} %x_ref.5, f32[8,4096]{1,0:T(8,128)} %b_ref.7), custom_call_target="tpu_custom_call" | custom-call | flops 786432 | bytes 786432 | tf_op jit(solution)/shard_map/pallas_call | solution.py:429
  2.3 3.1 %collective-permute-start = (f32[6,1,4096]{2,1,0:T(1,128)}, f32[6,1,4096]{2,1,0:T(1,128)S(1)}, u32[]{:S(2)}, u32[]{:S(2)}) collective-permute-start(f32[6,1,4096]{2,1,0:T(1,128)} %get-tuple-element.27), channel_id=1, source_target_pairs={{0,1},{2,3},{4,5},{6,7},{1,0},{3,2},{5,4},{7,6},{8,9},{10,11},{12,... | collective-permute-start | bytes 294920 | tf_op jit(solution)/shard_map/ppermute | solution.py:37
  6.0 1.7 %shard_map.74 = (f32[6,8,4096]{2,1,0:T(8,128)S(1)}, f32[6,8,4096]{2,1,0:T(8,128)S(1)}) custom-call(s32[1]{0:T(128)} %bitcast.row_ref, f32[6,3,8,4096]{3,2,1,0:T(8,128)S(1)} %copy-done, f32[8,4096]{1,0:T(8,128)S(1)} %copy-done.1), custom_call_target="tpu_custom_call" | custom-call | flops 15728640 | bytes 3145728 | tf_op jit(solution)/shard_map/pallas_call | solution.py:442
  8.4 1.0 shard_map.76
  9.4 4.8 %collective-permute-start.2 = (f32[6,1,4096]{2,1,0:T(1,128)S(1)}, f32[6,1,4096]{2,1,0:T(1,128)S(1)}, u32[]{:S(2)}, u32[]{:S(2)}) collective-permute-start(f32[6,1,4096]{2,1,0:T(1,128)S(1)} %get-tuple-element.31), channel_id=1, source_target_pairs={{0,1},{2,3},{4,5},{6,7},{1,0},{3,2},{5,4},{7,6},{8,9},{10,11},{12,... | collective-permute-start | bytes 294920 | tf_op jit(solution)/shard_map/ppermute | solution.py:37
  14.8 2.6 %collective-permute-done.2.even_ref = f32[6,1,4096]{2,1,0:T(1,128)S(1)} collective-permute-done((f32[6,1,4096]{2,1,0:T(1,128)S(1)}, f32[6,1,4096]{2,1,0:T(1,128)S(1)}, u32[]{:S(2)}, u32[]{:S(2)}) %collective-permute-start.2) | collective-permute-done | bytes 98336 | tf_op jit(solution)/shard_map/ppermute | solution.py:37
  18.1 4.7 %collective-permute-start.4 = (f32[6,1,4096]{2,1,0:T(1,128)S(1)}, f32[6,1,4096]{2,1,0:T(1,128)S(1)}, u32[]{:S(2)}, u32[]{:S(2)}) collective-permute-start(f32[6,1,4096]{2,1,0:T(1,128)S(1)} %get-tuple-element.35), channel_id=1, source_target_pairs={{0,1},{2,3},{4,5},{6,7},{1,0},{3,2},{5,4},{7,6},{8,9},{10,11},{12,... | collective-permute-start | bytes 294920 | tf_op jit(solution)/shard_map/ppermute | solution.py:37
  22.8 0.7 collective-permute-start.5
  23.5 0.9 shard_map.78.part_ref
  24.4 1.6 %collective-permute-done.4.even_ref = f32[6,1,4096]{2,1,0:T(1,128)S(1)} collective-permute-done((f32[6,1,4096]{2,1,0:T(1,128)S(1)}, f32[6,1,4096]{2,1,0:T(1,128)S(1)}, u32[]{:S(2)}, u32[]{:S(2)}) %collective-permute-start.4) | collective-permute-done | bytes 98336 | tf_op jit(solution)/shard_map/ppermute | solution.py:37
  26.0 4.9 %shard_map.79 = (f32[6,8,4096]{2,1,0:T(8,128)S(1)}, f32[6,1,4096]{2,1,0:T(1,128)S(1)}, f32[6,1,4096]{2,1,0:T(1,128)S(1)}, f32[4,8,128]{2,1,0:T(8,128)S(1)}) custom-call(s32[1]{0:T(128)} %bitcast.row_ref, s32[4,128]{1,0:T(4,128)S(1)} %shard_map.73.code_ref, f32[6,8,4096]{2,1,0:T(8,128)S(1)} %shard_map.78.part_ref, ...), custom_call_target="tpu_custom_call" | custom-call | flops 15728640 | bytes 3145728 | tf_op jit(solution)/shard_map/pallas_call | solution.py:466
  30.9 1.5 %collective-permute-start.6 = (f32[4,8,128]{2,1,0:T(8,128)S(1)}, f32[4,8,128]{2,1,0:T(8,128)S(1)}, u32[]{:S(2)}, u32[]{:S(2)}) collective-permute-start(f32[4,8,128]{2,1,0:T(8,128)S(1)} %get-tuple-element.37.refs_0_), channel_id=1, source_target_pairs={{0,16},{8,24},{16,0},{24,8},{1,17},{9,25},{17,1},{25,9},{2,18},{10... | collective-permute-start | bytes 49160 | tf_op jit(solution)/shard_map/ppermute | solution.py:69
  32.5 2.2 %collective-permute-done.6.refs_1_ = f32[4,8,128]{2,1,0:T(8,128)S(1)} collective-permute-done((f32[4,8,128]{2,1,0:T(8,128)S(1)}, f32[4,8,128]{2,1,0:T(8,128)S(1)}, u32[]{:S(2)}, u32[]{:S(2)}) %collective-permute-start.6) | collective-permute-done | bytes 16416 | tf_op jit(solution)/shard_map/ppermute | solution.py:69
  34.7 5.7 %collective-permute-start.24 = (f32[6,1,4096]{2,1,0:T(1,128)S(1)}, f32[6,1,4096]{2,1,0:T(1,128)S(1)}, u32[]{:S(2)}, u32[]{:S(2)}) collective-permute-start(f32[6,1,4096]{2,1,0:T(1,128)S(1)} %get-tuple-element.43), channel_id=1, source_target_pairs={{0,1},{2,3},{4,5},{6,7},{1,0},{3,2},{5,4},{7,6},{8,9},{10,11},{12,... | collective-permute-start | bytes 294920 | tf_op jit(solution)/shard_map/ppermute | solution.py:37
  42.1 1.5 %collective-permute-start.21 = (f32[2,8,4096]{2,1,0:T(8,128)S(1)}, f32[2,8,4096]{2,1,0:T(8,128)S(1)}, u32[]{:S(2)}, u32[]{:S(2)}) collective-permute-start(f32[2,8,4096]{2,1,0:T(8,128)S(1)} %get-tuple-element.34.refs_1_.refs_4_), channel_id=1, source_target_pairs={{0,16},{8,24},{16,0},{24,8},{1,17},{9,25},{17,1},{25,9},{2,18},{10... | collective-permute-start | bytes 786440 | tf_op jit(solution)/shard_map/ppermute | solution.py:69
  44.1 1.5 %collective-permute-start.16 = (f32[6,8,4096]{2,1,0:T(8,128)S(1)}, f32[6,8,4096]{2,1,0:T(8,128)S(1)}, u32[]{:S(2)}, u32[]{:S(2)}) collective-permute-start(f32[6,8,4096]{2,1,0:T(8,128)S(1)} %get-tuple-element.38.refs_4_), channel_id=1, source_target_pairs={{0,16},{8,24},{16,0},{24,8},{1,17},{9,25},{17,1},{25,9},{2,18},{10... | collective-permute-start | bytes 2359304 | tf_op jit(solution)/shard_map/ppermute | solution.py:69
  45.6 3.0 %collective-permute-start.10 = (f32[32,128]{1,0:T(8,128)S(1)}, f32[32,128]{1,0:T(8,128)S(1)}, u32[]{:S(2)}, u32[]{:S(2)}) collective-permute-start(f32[32,128]{1,0:T(8,128)S(1)} %add.9), channel_id=1, source_target_pairs={{0,2},{1,3},{2,0},{3,1},{4,6},{5,7},{6,4},{7,5},{8,10},{9,11},{10,... | collective-permute-start | bytes 49160 | tf_op jit(solution)/shard_map/ppermute | solution.py:53
  48.7 1.7 %collective-permute-done.10 = f32[32,128]{1,0:T(8,128)S(1)} collective-permute-done((f32[32,128]{1,0:T(8,128)S(1)}, f32[32,128]{1,0:T(8,128)S(1)}, u32[]{:S(2)}, u32[]{:S(2)}) %collective-permute-start.10) | collective-permute-done | bytes 16416 | tf_op jit(solution)/shard_map/ppermute | solution.py:53
  50.4 3.0 %collective-permute-start.11 = (f32[32,128]{1,0:T(8,128)S(1)}, f32[32,128]{1,0:T(8,128)S(1)}, u32[]{:S(2)}, u32[]{:S(2)}) collective-permute-start(f32[32,128]{1,0:T(8,128)S(1)} %add.10), channel_id=1, source_target_pairs={{0,4},{1,5},{2,6},{3,7},{4,0},{5,1},{6,2},{7,3},{8,12},{9,13},{10,... | collective-permute-start | bytes 49160 | tf_op jit(solution)/shard_map/ppermute | solution.py:53
  53.4 1.7 %collective-permute-done.11 = f32[32,128]{1,0:T(8,128)S(1)} collective-permute-done((f32[32,128]{1,0:T(8,128)S(1)}, f32[32,128]{1,0:T(8,128)S(1)}, u32[]{:S(2)}, u32[]{:S(2)}) %collective-permute-start.11) | collective-permute-done | bytes 16416 | tf_op jit(solution)/shard_map/ppermute | solution.py:53
  55.2 0.7 collective-permute-start.25
  57.1 0.9 collective-permute-done.22.refs_6_
  58.0 1.5 %collective-permute-start.26 = (f32[6,2,8,512]{3,2,1,0:T(8,128)S(1)}, f32[6,2,8,512]{3,2,1,0:T(8,128)S(1)}, u32[]{:S(2)}, u32[]{:S(2)}) collective-permute-start(f32[6,2,8,512]{3,2,1,0:T(8,128)S(1)} %shard_map.86.refs_0_), channel_id=1, source_target_pairs={{0,16},{8,24},{16,0},{24,8},{1,17},{9,25},{17,1},{25,9},{2,18},{10... | collective-permute-start | bytes 589832 | tf_op jit(solution)/shard_map/ppermute | solution.py:69
  59.5 39.9 %collective-permute-done.26.refs_1_ = f32[6,2,8,512]{3,2,1,0:T(8,128)S(1)} collective-permute-done((f32[6,2,8,512]{3,2,1,0:T(8,128)S(1)}, f32[6,2,8,512]{3,2,1,0:T(8,128)S(1)}, u32[]{:S(2)}, u32[]{:S(2)}) %collective-permute-start.26) | collective-permute-done | bytes 196640 | tf_op jit(solution)/shard_map/ppermute | solution.py:69
  100.5 1.6 %collective-permute-done.23.refs_7_ = f32[2,8,4096]{2,1,0:T(8,128)S(1)} collective-permute-done((f32[2,8,4096]{2,1,0:T(8,128)S(1)}, f32[2,8,4096]{2,1,0:T(8,128)S(1)}, u32[]{:S(2)}, u32[]{:S(2)}) %collective-permute-start.23) | collective-permute-done | bytes 262176 | tf_op jit(solution)/shard_map/ppermute | solution.py:76
  102.5 3.6 %collective-permute-done.20.refs_3_ = f32[4,8,4096]{2,1,0:T(8,128)S(1)} collective-permute-done((f32[4,8,4096]{2,1,0:T(8,128)S(1)}, f32[4,8,4096]{2,1,0:T(8,128)S(1)}, u32[]{:S(2)}, u32[]{:S(2)}) %collective-permute-start.20) | collective-permute-done | bytes 524320 | tf_op jit(solution)/shard_map/ppermute | solution.py:76
  106.3 2.4 %shard_map.81.t_ref = f32[32,128]{1,0:T(8,128)S(1)} custom-call(f32[1]{0:T(128)S(6)} %copy.8.inf_ref, f32[32,128]{1,0:T(8,128)S(1)} %add.11.part_ref), custom_call_target="tpu_custom_call" | custom-call | flops 1000000 | bytes 40000 | tf_op jit(solution)/shard_map/pallas_call | solution.py:489
  108.7 2.4 %shard_map.84.v_ref = f32[6,8,4096]{2,1,0:T(8,128)S(1)} custom-call(f32[32,128]{1,0:T(8,128)S(1)} %shard_map.81.t_ref, f32[4,8,4096]{2,1,0:T(8,128)S(1)} %get-tuple-element.33.refs_0_, f32[4,8,4096]{2,1,0:T(8,128)S(1)} %collective-permute-done.18.refs_1_, f32[4,8,4096]{2,1,0:T(8,128)S(1)} %collective-permute-done.19.refs_2_, ...), custom_call_target="tpu_custom_call" | custom-call | flops 78643200 | bytes 7864320 | tf_op jit(solution)/shard_map/pallas_call | solution.py:522
  111.1 3.1 %shard_map.82 = (f32[6,8,4096]{2,1,0:T(8,128)S(1)}, f32[6,8,4096]{2,1,0:T(8,128)S(1)}) custom-call(f32[32,128]{1,0:T(8,128)S(1)} %shard_map.81.t_ref, f32[6,8,4096]{2,1,0:T(8,128)S(1)} %get-tuple-element.30.u_ref.refs_0_, f32[6,8,4096]{2,1,0:T(8,128)S(1)} %collective-permute-done.12.refs_1_, f32[6,8,4096]{2,1,0:T(8,128)S(1)} %collective-permute-done.13.refs_2_, ...), custom_call_target="tpu_custom_call" | custom-call | flops 78643200 | bytes 7864320 | tf_op jit(solution)/shard_map/pallas_call | solution.py:522
  114.2 1.6 %shard_map.83.h_ref = f32[6,8,4096]{2,1,0:T(8,128)S(1)} custom-call(f32[32,128]{1,0:T(8,128)S(1)} %shard_map.81.t_ref, f32[6,8,4096]{2,1,0:T(8,128)S(1)} %get-tuple-element.39.part_ref, f32[6,8,4096]{2,1,0:T(8,128)S(1)} %collective-permute-done.16.refs_0_, f32[6,8,4096]{2,1,0:T(8,128)S(1)} %collective-permute-done.17.refs_1_), custom_call_target="tpu_custom_call" | custom-call | flops 39321600 | bytes 3145728 | tf_op jit(solution)/shard_map/pallas_call | solution.py:530
  115.8 0.9 shard_map.85
  116.8 2.3 %shard_map.87 = f32[6,3,8,4096]{3,2,1,0:T(8,128)} custom-call(f32[32,128]{1,0:T(8,128)S(1)} %shard_map.81.t_ref, f32[6,8,4096]{2,1,0:T(8,128)S(1)} %get-tuple-element.41.part_ref, f32[6,8,4096]{2,1,0:T(8,128)S(1)} %shard_map.83.h_ref, f32[6,8,4096]{2,1,0:T(8,128)S(1)} %get-tuple-element.42.u_ref, f32[6,2,8,512]{3,2,1,0:T(8,128)S(1)} %shard_map.86.refs_0_, ...), custom_call_target="tpu_custom_call" | custom-call | flops 15728640 | bytes 2359296 | tf_op jit(solution)/shard_map/pallas_call | solution.py:538
  (56 shorter events, 7.1 us)
Async XLA Ops:
  2.3 6.1 %collective-permute-start = (f32[6,1,4096]{2,1,0:T(1,128)}, f32[6,1,4096]{2,1,0:T(1,128)S(1)}, u32[]{:S(2)}, u32[]{:S(2)}) collective-permute-start(f32[6,1,4096]{2,1,0:T(1,128)} %get-tuple-element.27), channel_id=1, source_target_pairs={{0,1},{2,3},{4,5},{6,7},{1,0},{3,2},{5,4},{7,6},{8,9},{10,11},{12,... | collective-permute-start | bytes 294920 | tf_op jit(solution)/shard_map/ppermute | solution.py:37
  5.3 3.0 %collective-permute-start.1 = (f32[6,1,4096]{2,1,0:T(1,128)}, f32[6,1,4096]{2,1,0:T(1,128)S(1)}, u32[]{:S(2)}, u32[]{:S(2)}) collective-permute-start(f32[6,1,4096]{2,1,0:T(1,128)} %get-tuple-element.28), channel_id=1, source_target_pairs={{1,2},{3,4},{5,6},{2,1},{4,3},{6,5},{9,10},{11,12},{13,14},{10,9},... | collective-permute-start | bytes 294920 | tf_op jit(solution)/shard_map/ppermute | solution.py:38
  9.4 8.0 %collective-permute-start.2 = (f32[6,1,4096]{2,1,0:T(1,128)S(1)}, f32[6,1,4096]{2,1,0:T(1,128)S(1)}, u32[]{:S(2)}, u32[]{:S(2)}) collective-permute-start(f32[6,1,4096]{2,1,0:T(1,128)S(1)} %get-tuple-element.31), channel_id=1, source_target_pairs={{0,1},{2,3},{4,5},{6,7},{1,0},{3,2},{5,4},{7,6},{8,9},{10,11},{12,... | collective-permute-start | bytes 294920 | tf_op jit(solution)/shard_map/ppermute | solution.py:37
  14.2 3.2 %collective-permute-start.3 = (f32[6,1,4096]{2,1,0:T(1,128)S(1)}, f32[6,1,4096]{2,1,0:T(1,128)S(1)}, u32[]{:S(2)}, u32[]{:S(2)}) collective-permute-start(f32[6,1,4096]{2,1,0:T(1,128)S(1)} %get-tuple-element.32), channel_id=1, source_target_pairs={{1,2},{3,4},{5,6},{2,1},{4,3},{6,5},{9,10},{11,12},{13,14},{10,9},... | collective-permute-start | bytes 294920 | tf_op jit(solution)/shard_map/ppermute | solution.py:38
  18.0 23.1 %copy-start.2 = (f32[6,4,128]{2,1,0:T(4,128)S(1)}, f32[6,4,128]{2,1,0:T(4,128)}, u32[]{:S(2)}) copy-start(f32[6,4,128]{2,1,0:T(4,128)} %pert_ref.1) | copy-start | bytes 36868
  18.1 23.1 %copy-start.3 = (f32[4,128]{1,0:T(4,128)S(1)}, f32[4,128]{1,0:T(4,128)}, u32[]{:S(2)}) copy-start(f32[4,128]{1,0:T(4,128)} %obs_ref.1) | copy-start | bytes 6148
  18.1 23.1 %copy-start.4 = (f32[4,128]{1,0:T(4,128)S(1)}, f32[4,128]{1,0:T(4,128)}, u32[]{:S(2)}) copy-start(f32[4,128]{1,0:T(4,128)} %scale_ref.1) | copy-start | bytes 6148
  18.1 7.9 %collective-permute-start.4 = (f32[6,1,4096]{2,1,0:T(1,128)S(1)}, f32[6,1,4096]{2,1,0:T(1,128)S(1)}, u32[]{:S(2)}, u32[]{:S(2)}) collective-permute-start(f32[6,1,4096]{2,1,0:T(1,128)S(1)} %get-tuple-element.35), channel_id=1, source_target_pairs={{0,1},{2,3},{4,5},{6,7},{1,0},{3,2},{5,4},{7,6},{8,9},{10,11},{12,... | collective-permute-start | bytes 294920 | tf_op jit(solution)/shard_map/ppermute | solution.py:37
  22.8 3.2 %collective-permute-start.5 = (f32[6,1,4096]{2,1,0:T(1,128)S(1)}, f32[6,1,4096]{2,1,0:T(1,128)S(1)}, u32[]{:S(2)}, u32[]{:S(2)}) collective-permute-start(f32[6,1,4096]{2,1,0:T(1,128)S(1)} %get-tuple-element.36), channel_id=1, source_target_pairs={{1,2},{3,4},{5,6},{2,1},{4,3},{6,5},{9,10},{11,12},{13,14},{10,9},... | collective-permute-start | bytes 294920 | tf_op jit(solution)/shard_map/ppermute | solution.py:38
  30.9 3.8 %collective-permute-start.6 = (f32[4,8,128]{2,1,0:T(8,128)S(1)}, f32[4,8,128]{2,1,0:T(8,128)S(1)}, u32[]{:S(2)}, u32[]{:S(2)}) collective-permute-start(f32[4,8,128]{2,1,0:T(8,128)S(1)} %get-tuple-element.37.refs_0_), channel_id=1, source_target_pairs={{0,16},{8,24},{16,0},{24,8},{1,17},{9,25},{17,1},{25,9},{2,18},{10... | collective-permute-start | bytes 49160 | tf_op jit(solution)/shard_map/ppermute | solution.py:69
  32.5 8.6 %collective-permute-start.7 = (f32[4,8,128]{2,1,0:T(8,128)S(1)}, f32[4,8,128]{2,1,0:T(8,128)S(1)}, u32[]{:S(2)}, u32[]{:S(2)}) collective-permute-start(f32[4,8,128]{2,1,0:T(8,128)S(1)} %get-tuple-element.37.refs_0_), channel_id=1, source_target_pairs={{0,8},{8,0},{16,24},{24,16},{1,9},{9,1},{17,25},{25,17},{2,10},{10... | collective-permute-start | bytes 49160 | tf_op jit(solution)/shard_map/ppermute | solution.py:76
  34.7 6.4 %collective-permute-start.8 = (f32[4,8,128]{2,1,0:T(8,128)S(1)}, f32[4,8,128]{2,1,0:T(8,128)S(1)}, u32[]{:S(2)}, u32[]{:S(2)}) collective-permute-start(f32[4,8,128]{2,1,0:T(8,128)S(1)} %collective-permute-done.6.refs_1_), channel_id=1, source_target_pairs={{0,8},{8,0},{16,24},{24,16},{1,9},{9,1},{17,25},{25,17},{2,10},{10... | collective-permute-start | bytes 49160 | tf_op jit(solution)/shard_map/ppermute | solution.py:76
  34.7 21.1 %collective-permute-start.24 = (f32[6,1,4096]{2,1,0:T(1,128)S(1)}, f32[6,1,4096]{2,1,0:T(1,128)S(1)}, u32[]{:S(2)}, u32[]{:S(2)}) collective-permute-start(f32[6,1,4096]{2,1,0:T(1,128)S(1)} %get-tuple-element.43), channel_id=1, source_target_pairs={{0,1},{2,3},{4,5},{6,7},{1,0},{3,2},{5,4},{7,6},{8,9},{10,11},{12,... | collective-permute-start | bytes 294920 | tf_op jit(solution)/shard_map/ppermute | solution.py:37
  41.6 4.1 %collective-permute-start.9 = (f32[32,128]{1,0:T(8,128)S(1)}, f32[32,128]{1,0:T(8,128)S(1)}, u32[]{:S(2)}, u32[]{:S(2)}) collective-permute-start(f32[32,128]{1,0:T(8,128)S(1)} %shard_map.80), channel_id=1, source_target_pairs={{0,1},{1,0},{2,3},{3,2},{4,5},{5,4},{6,7},{7,6},{8,9},{9,8},{10,11... | collective-permute-start | bytes 49160 | tf_op jit(solution)/shard_map/ppermute | solution.py:53
  42.1 14.3 %collective-permute-start.21 = (f32[2,8,4096]{2,1,0:T(8,128)S(1)}, f32[2,8,4096]{2,1,0:T(8,128)S(1)}, u32[]{:S(2)}, u32[]{:S(2)}) collective-permute-start(f32[2,8,4096]{2,1,0:T(8,128)S(1)} %get-tuple-element.34.refs_1_.refs_4_), channel_id=1, source_target_pairs={{0,16},{8,24},{16,0},{24,8},{1,17},{9,25},{17,1},{25,9},{2,18},{10... | collective-permute-start | bytes 786440 | tf_op jit(solution)/shard_map/ppermute | solution.py:69
  43.6 56.3 %collective-permute-start.12 = (f32[6,8,4096]{2,1,0:T(8,128)S(1)}, f32[6,8,4096]{2,1,0:T(8,128)S(1)}, u32[]{:S(2)}, u32[]{:S(2)}) collective-permute-start(f32[6,8,4096]{2,1,0:T(8,128)S(1)} %get-tuple-element.30.u_ref.refs_0_), channel_id=1, source_target_pairs={{0,16},{8,24},{16,0},{24,8},{1,17},{9,25},{17,1},{25,9},{2,18},{10... | collective-permute-start | bytes 2359304 | tf_op jit(solution)/shard_map/ppermute | solution.py:69
  44.1 56.3 %collective-permute-start.16 = (f32[6,8,4096]{2,1,0:T(8,128)S(1)}, f32[6,8,4096]{2,1,0:T(8,128)S(1)}, u32[]{:S(2)}, u32[]{:S(2)}) collective-permute-start(f32[6,8,4096]{2,1,0:T(8,128)S(1)} %get-tuple-element.38.refs_4_), channel_id=1, source_target_pairs={{0,16},{8,24},{16,0},{24,8},{1,17},{9,25},{17,1},{25,9},{2,18},{10... | collective-permute-start | bytes 2359304 | tf_op jit(solution)/shard_map/ppermute | solution.py:69
  45.6 4.8 %collective-permute-start.10 = (f32[32,128]{1,0:T(8,128)S(1)}, f32[32,128]{1,0:T(8,128)S(1)}, u32[]{:S(2)}, u32[]{:S(2)}) collective-permute-start(f32[32,128]{1,0:T(8,128)S(1)} %add.9), channel_id=1, source_target_pairs={{0,2},{1,3},{2,0},{3,1},{4,6},{5,7},{6,4},{7,5},{8,10},{9,11},{10,... | collective-permute-start | bytes 49160 | tf_op jit(solution)/shard_map/ppermute | solution.py:53
  50.4 4.7 %collective-permute-start.11 = (f32[32,128]{1,0:T(8,128)S(1)}, f32[32,128]{1,0:T(8,128)S(1)}, u32[]{:S(2)}, u32[]{:S(2)}) collective-permute-start(f32[32,128]{1,0:T(8,128)S(1)} %add.10), channel_id=1, source_target_pairs={{0,4},{1,5},{2,6},{3,7},{4,0},{5,1},{6,2},{7,3},{8,12},{9,13},{10,... | collective-permute-start | bytes 49160 | tf_op jit(solution)/shard_map/ppermute | solution.py:53
  55.2 1.3 %collective-permute-start.25 = (f32[6,1,4096]{2,1,0:T(1,128)S(1)}, f32[6,1,4096]{2,1,0:T(1,128)S(1)}, u32[]{:S(2)}, u32[]{:S(2)}) collective-permute-start(f32[6,1,4096]{2,1,0:T(1,128)S(1)} %get-tuple-element.44), channel_id=1, source_target_pairs={{1,2},{3,4},{5,6},{2,1},{4,3},{6,5},{9,10},{11,12},{13,14},{10,9},... | collective-permute-start | bytes 294920 | tf_op jit(solution)/shard_map/ppermute | solution.py:38
  55.8 43.5 %collective-permute-start.18 = (f32[4,8,4096]{2,1,0:T(8,128)S(1)}, f32[4,8,4096]{2,1,0:T(8,128)S(1)}, u32[]{:S(2)}, u32[]{:S(2)}) collective-permute-start(f32[4,8,4096]{2,1,0:T(8,128)S(1)} %get-tuple-element.33.refs_0_), channel_id=1, source_target_pairs={{0,16},{8,24},{16,0},{24,8},{1,17},{9,25},{17,1},{25,9},{2,18},{10... | collective-permute-start | bytes 1572872 | tf_op jit(solution)/shard_map/ppermute | solution.py:69
  56.4 1.5 %collective-permute-start.22 = (f32[2,8,4096]{2,1,0:T(8,128)S(1)}, f32[2,8,4096]{2,1,0:T(8,128)S(1)}, u32[]{:S(2)}, u32[]{:S(2)}) collective-permute-start(f32[2,8,4096]{2,1,0:T(8,128)S(1)} %get-tuple-element.34.refs_1_.refs_4_), channel_id=1, source_target_pairs={{0,8},{8,0},{16,24},{24,16},{1,9},{9,1},{17,25},{25,17},{2,10},{10... | collective-permute-start | bytes 786440 | tf_op jit(solution)/shard_map/ppermute | solution.py:76
  56.4 43.4 %collective-permute-start.19 = (f32[4,8,4096]{2,1,0:T(8,128)S(1)}, f32[4,8,4096]{2,1,0:T(8,128)S(1)}, u32[]{:S(2)}, u32[]{:S(2)}) collective-permute-start(f32[4,8,4096]{2,1,0:T(8,128)S(1)} %get-tuple-element.33.refs_0_), channel_id=1, source_target_pairs={{0,8},{8,0},{16,24},{24,16},{1,9},{9,1},{17,25},{25,17},{2,10},{10... | collective-permute-start | bytes 1572872 | tf_op jit(solution)/shard_map/ppermute | solution.py:76
  58.0 41.4 %collective-permute-start.26 = (f32[6,2,8,512]{3,2,1,0:T(8,128)S(1)}, f32[6,2,8,512]{3,2,1,0:T(8,128)S(1)}, u32[]{:S(2)}, u32[]{:S(2)}) collective-permute-start(f32[6,2,8,512]{3,2,1,0:T(8,128)S(1)} %shard_map.86.refs_0_), channel_id=1, source_target_pairs={{0,16},{8,24},{16,0},{24,8},{1,17},{9,25},{17,1},{25,9},{2,18},{10... | collective-permute-start | bytes 589832 | tf_op jit(solution)/shard_map/ppermute | solution.py:69
  99.4 2.8 %collective-permute-start.13 = (f32[6,8,4096]{2,1,0:T(8,128)S(1)}, f32[6,8,4096]{2,1,0:T(8,128)S(1)}, u32[]{:S(2)}, u32[]{:S(2)}) collective-permute-start(f32[6,8,4096]{2,1,0:T(8,128)S(1)} %get-tuple-element.30.u_ref.refs_0_), channel_id=1, source_target_pairs={{0,8},{8,0},{16,24},{24,16},{1,9},{9,1},{17,25},{25,17},{2,10},{10... | collective-permute-start | bytes 2359304 | tf_op jit(solution)/shard_map/ppermute | solution.py:76
  99.4 2.7 %collective-permute-start.23 = (f32[2,8,4096]{2,1,0:T(8,128)S(1)}, f32[2,8,4096]{2,1,0:T(8,128)S(1)}, u32[]{:S(2)}, u32[]{:S(2)}) collective-permute-start(f32[2,8,4096]{2,1,0:T(8,128)S(1)} %collective-permute-done.21.refs_5_), channel_id=1, source_target_pairs={{0,8},{8,0},{16,24},{24,16},{1,9},{9,1},{17,25},{25,17},{2,10},{10... | collective-permute-start | bytes 786440 | tf_op jit(solution)/shard_map/ppermute | solution.py:76
  99.9 11.2 %collective-permute-start.15 = (f32[6,8,4096]{2,1,0:T(8,128)S(1)}, f32[6,8,4096]{2,1,0:T(8,128)S(1)}, u32[]{:S(2)}, u32[]{:S(2)}) collective-permute-start(f32[6,8,4096]{2,1,0:T(8,128)S(1)} %get-tuple-element.38.refs_4_), channel_id=1, source_target_pairs={{0,8},{8,0},{16,24},{24,16},{1,9},{9,1},{17,25},{25,17},{2,10},{10... | collective-permute-start | bytes 2359304 | tf_op jit(solution)/shard_map/ppermute | solution.py:76
  100.0 11.1 %collective-permute-start.14 = (f32[6,8,4096]{2,1,0:T(8,128)S(1)}, f32[6,8,4096]{2,1,0:T(8,128)S(1)}, u32[]{:S(2)}, u32[]{:S(2)}) collective-permute-start(f32[6,8,4096]{2,1,0:T(8,128)S(1)} %collective-permute-done.12.refs_1_), channel_id=1, source_target_pairs={{0,8},{8,0},{16,24},{24,16},{1,9},{9,1},{17,25},{25,17},{2,10},{10... | collective-permute-start | bytes 2359304 | tf_op jit(solution)/shard_map/ppermute | solution.py:76
  100.4 13.8 %collective-permute-start.17 = (f32[6,8,4096]{2,1,0:T(8,128)S(1)}, f32[6,8,4096]{2,1,0:T(8,128)S(1)}, u32[]{:S(2)}, u32[]{:S(2)}) collective-permute-start(f32[6,8,4096]{2,1,0:T(8,128)S(1)} %collective-permute-done.16.refs_0_), channel_id=1, source_target_pairs={{0,8},{8,0},{16,24},{24,16},{1,9},{9,1},{17,25},{25,17},{2,10},{10... | collective-permute-start | bytes 2359304 | tf_op jit(solution)/shard_map/ppermute | solution.py:76
  102.0 4.1 %collective-permute-start.20 = (f32[4,8,4096]{2,1,0:T(8,128)S(1)}, f32[4,8,4096]{2,1,0:T(8,128)S(1)}, u32[]{:S(2)}, u32[]{:S(2)}) collective-permute-start(f32[4,8,4096]{2,1,0:T(8,128)S(1)} %collective-permute-done.18.refs_1_), channel_id=1, source_target_pairs={{0,8},{8,0},{16,24},{24,16},{1,9},{9,1},{17,25},{25,17},{2,10},{10... | collective-permute-start | bytes 1572872 | tf_op jit(solution)/shard_map/ppermute | solution.py:76
  102.2 14.6 %collective-permute-start.27 = (f32[6,2,8,512]{3,2,1,0:T(8,128)S(1)}, f32[6,2,8,512]{3,2,1,0:T(8,128)S(1)}, u32[]{:S(2)}, u32[]{:S(2)}) collective-permute-start(f32[6,2,8,512]{3,2,1,0:T(8,128)S(1)} %shard_map.86.refs_0_), channel_id=1, source_target_pairs={{0,8},{8,0},{16,24},{24,16},{1,9},{9,1},{17,25},{25,17},{2,10},{10... | collective-permute-start | bytes 589832 | tf_op jit(solution)/shard_map/ppermute | solution.py:76
  106.1 10.6 %collective-permute-start.28 = (f32[6,2,8,512]{3,2,1,0:T(8,128)S(1)}, f32[6,2,8,512]{3,2,1,0:T(8,128)S(1)}, u32[]{:S(2)}, u32[]{:S(2)}) collective-permute-start(f32[6,2,8,512]{3,2,1,0:T(8,128)S(1)} %collective-permute-done.26.refs_1_), channel_id=1, source_target_pairs={{0,8},{8,0},{16,24},{24,16},{1,9},{9,1},{17,25},{25,17},{2,10},{10... | collective-permute-start | bytes 589832 | tf_op jit(solution)/shard_map/ppermute | solution.py:76
  (3 other events, 26.2 us)

commit v3 on v2

--- a/solution.py
+++ b/solution.py
@@ -95,18 +95,22 @@
 
 
 def edge_kernel(row_ref, x_ref, b_ref, even_out, odd_out, speed, depth, sems):
-    copies = [
-        pltpu.make_async_copy(b_ref, depth, sems.at[0]),
-        pltpu.make_async_copy(x_ref.at[:, 2], speed, sems.at[1]),
-    ]
+    rows = b_ref.shape[0]
+    copies = []
+    for k, row in enumerate((0, rows - 1)):
+        copies += [
+            pltpu.make_async_copy(b_ref.at[pl.ds(row, 1)], depth.at[k], sems.at[2 * k]),
+            pltpu.make_async_copy(x_ref.at[:, 2, pl.ds(row, 1)], speed.at[k], sems.at[2 * k + 1]),
+        ]
     for copy in copies:
         copy.start()
     for copy in copies:
         copy.wait()
 
     def member(m, _):
-        flux = depth[...] * speed[m]
-        even_out[m], odd_out[m] = pick(row_ref, depth.shape[0], flux[:1], flux[-1:])
+        even_out[m], odd_out[m] = pick(
+            row_ref, rows, depth[0] * speed[0, m], depth[1] * speed[1, m]
+        )
         return 0
 
     lax.fori_loop(0, x_ref.shape[0], member, 0)
@@ -233,13 +237,15 @@
         )
 
 
-def pack_kernel(rows, row_ref, even_ref, odd_ref, out_ref):
+def pack_kernel(rows, row_ref, *refs):
+    ins, out_ref = refs[:-1], refs[-1]
     width = out_ref.shape[-1]
 
     def member(m, _):
-        for side, line in enumerate(pick(row_ref, rows, even_ref[m], odd_ref[m])):
-            for s in range(8):
-                out_ref[m, side, s : s + 1, :] = line[:, s * width : (s + 1) * width]
+        for k in range(0, len(ins), 2):
+            for side, line in enumerate(pick(row_ref, rows, ins[k][m], ins[k + 1][m])):
+                for s in range(8):
+                    out_ref[m, k + side, s : s + 1, :] = line[:, s * width : (s + 1) * width]
         return 0
 
     lax.fori_loop(0, out_ref.shape[0], member, 0)
@@ -354,35 +360,66 @@
     lax.fori_loop(0, members, member, 0)
 
 
-def finish_kernel(places, first, t_ref, part_ref, h_ref, u_ref, *refs):
-    ins, (out_ref, v_new, sems) = refs[:-3], refs[-3:]
-    members, rows, columns = part_ref.shape
+def packed_east(q):
+    count, width = q.shape
+    lane = lax.broadcasted_iota(jnp.int32, q.shape, 1)
+    up, down = pltpu.roll(q, width - 1, 1), pltpu.roll(q, 1, 1)
+    up = jnp.where(lane == width - 1, pltpu.roll(up, count - 1, 0), up)
+    down = jnp.where(lane == 0, pltpu.roll(down, 1, 0), down)
+    return (up - down) * 0.5
+
+
+def rim_totals(t_ref, pieces, first, members, side, start):
+    total = list(start)
+    for g, ref in pieces:
+        for i in range(members):
+            value = ref[i, side]
+            for j in range(members):
+                total[j] = total[j] + t_ref[g + i, first + j] * value
+    return total
+
+
+def rim_kernel(places, first, t_ref, *refs):
+    pieces, out_ref = list(zip(places, refs)), refs[-1]
+    members, sides, _, width = out_ref.shape
+    for side in range(sides):
+        zeros = [jnp.zeros((8, width), f32)] * members
+        for j, t in enumerate(rim_totals(t_ref, pieces, first, members, side, zeros)):
+            out_ref[j, side] = t
+
+
+def finish_kernel(places, first, total_rows, row_ref, t_ref, v_ref, h_ref, u_ref, part_ref, *refs):
+    ins, (out_ref, v_new, u_new, sems) = refs[:-4], refs[-4:]
+    members, rows, columns = v_ref.shape
     width = columns // 8
-    copies = [
-        pltpu.make_async_copy(h_ref, out_ref.at[:, 0], sems.at[members]),
-        pltpu.make_async_copy(u_ref, out_ref.at[:, 1], sems.at[members + 1]),
+    copies = [pltpu.make_async_copy(h_ref, out_ref.at[:, 0], sems.at[2 * members])]
+    copies[0].start()
+    turn = spin(row_ref[0], (rows, width), total_rows)
+    pieces = list(zip(places, ins))
+    totals = [
+        rim_totals(
+            t_ref, pieces, first, members, side, [part_ref[j, side] for j in range(members)]
+        )
+        for side in range(4)
     ]
-    for copy in copies:
-        copy.start()
-    totals = []
-    for side in range(2):
-        total = [jnp.zeros((8, width), f32)] * members
-        for g, ref in zip(places, ins):
-            for i in range(members):
-                value = ref[i, side]
-                for j in range(members):
-                    total[j] = total[j] + t_ref[g + i, first + j] * value
-        totals.append(total)
     for j in range(members):
-        v_new[j] = part_ref[j]
-        for s in range(8):
-            at = slice(s * width, (s + 1) * width)
-            v_new[j, :1, at] = v_new[j, :1, at] + (courant * 0.5) * totals[0][j][s : s + 1]
-            v_new[j, rows - 1 :, at] = (
-                v_new[j, rows - 1 :, at] - (courant * 0.5) * totals[1][j][s : s + 1]
+        v_new[j] = v_ref[j]
+        u_new[j] = u_ref[j]
+        for side, sign, row in ((0, 1.0, 0), (1, -1.0, rows - 1)):
+            at_row = slice(row, row + 1)
+            u_term = (-sign * courant * courant * 0.5) * packed_east(totals[2 + side][j])
+            v_term = (sign * courant * 0.5) * totals[side][j] - turn[at_row] * u_term
+            for s in range(8):
+                at = slice(s * width, (s + 1) * width)
+                u_new[j, at_row, at] = u_new[j, at_row, at] + u_term[s : s + 1]
+                v_new[j, at_row, at] = v_new[j, at_row, at] + v_term[s : s + 1]
+        for q, ref in ((1, u_new), (2, v_new)):
+            copies.append(
+                pltpu.make_async_copy(
+                    ref.at[j], out_ref.at[j, q], sems.at[(q - 1) * members + j]
+                )
             )
-        copies.append(pltpu.make_async_copy(v_new.at[j], out_ref.at[j, 2], sems.at[j]))
-        copies[-1].start()
+            copies[-1].start()
     for copy in copies:
         copy.wait()
 
@@ -429,25 +466,26 @@
     even, odd = call(
         edge_kernel, [smem, hbm, hbm], [vmem] * 2, [edge, edge], 60, size, size,
         scratch=[
-            pltpu.VMEM((members, rows, columns), f32),
-            pltpu.VMEM((rows, columns), f32),
-            pltpu.SemaphoreType.DMA((2,)),
+            pltpu.VMEM((2, members, 1, columns), f32),
+            pltpu.VMEM((2, 1, columns), f32),
+            pltpu.SemaphoreType.DMA((4,)),
         ],
     )(row_index, x, seabed_profile)
     even, odd = swap_edges(even, odd)
+    first_rim = [even, odd]
     code = call(
         functools.partial(index_kernel, rows, columns), [smem, vmem], vmem,
         jax.ShapeDtypeStruct(gauge_grid_position.shape, jnp.int32), 1, 10000, 4096,
     )(row_index, gauge_grid_position)
-    h, u = call(
+    h, u_part = call(
         functools.partial(begin_kernel, total_rows),
         [smem] + [vmem] * 2, [vmem] * 2, [field, field], 12, 20 * size, 4 * size,
     )(row_index, x, seabed_profile)
+    u_far = far_gather(u_part)
     h, u, even, odd = call(
         height_kernel,
         [smem] + [vmem] * 4, [vmem] * 4, [field, field, edge, edge], 12, 5 * size, 4 * size,
-    )(row_index, h, u, even, odd)
-    u_far = far_gather(u)
+    )(row_index, h, u_part, even, odd)
     even, odd = swap_edges(even, odd)
     even, odd, *v = call(
         functools.partial(speed_kernel, total_rows),
@@ -495,9 +533,9 @@
     h_far = far_gather(h)
     even, odd = swap_edges(even, odd)
     rim = call(
-        functools.partial(pack_kernel, rows), [smem] + [vmem] * 2, vmem,
-        jax.ShapeDtypeStruct((members, 2, 8, columns // 8), f32), 4, size // 4, size // 2,
-    )(row_index, even, odd)
+        functools.partial(pack_kernel, rows), [smem] + [vmem] * 4, vmem,
+        jax.ShapeDtypeStruct((members, 4, 8, columns // 8), f32), 4, size // 4, size // 2,
+    )(row_index, even, odd, *first_rim)
     rim_far = far_gather(rim)
 
     def grouped(own, far):
@@ -506,7 +544,7 @@
         own_near = near_swap(own)
         return [own] + far + [own_near] + [near_swap(b) for b in far]
 
-    speeds, heights, rims = grouped(u, u_far), grouped(h, h_far), grouped(rim, rim_far)
+    speeds, heights, rims = grouped(u_part, u_far), grouped(h, h_far), grouped(rim, rim_far)
     sides = [grouped(b, f) for b, f in zip(v, v_far)]
     every = [g * padded for g in range(n)]
     near = [0] if mems % 2 else [0, n // 2]
@@ -535,15 +573,21 @@
         functools.partial(turn_kernel, total_rows),
         [smem] + [vmem] * 3, [vmem, vmem], [field, field], 8, 20 * size, 6 * size,
     )(row_index, h_new, u_sum, v_sum)
+    rim_part = call(
+        functools.partial(rim_kernel, [every[g] for g in near], height_rows),
+        [smem] + [vmem] * len(near), vmem, jax.ShapeDtypeStruct(rim.shape, f32), 4,
+        10 * size, size,
+    )(transform, *(rims[g] for g in near))
     return call(
-        functools.partial(finish_kernel, every, height_rows),
-        [smem] + [vmem] * (3 + n), hbm, whole, 4 + n,
+        functools.partial(finish_kernel, [every[g] for g in far], height_rows, total_rows),
+        [smem] * 2 + [vmem] * (4 + len(far)), hbm, whole, 6 + n,
         20 * size, 3 * size,
         scratch=[
             pltpu.VMEM((members, rows, columns), f32),
-            pltpu.SemaphoreType.DMA((members + 2,)),
+            pltpu.VMEM((members, rows, columns), f32),
+            pltpu.SemaphoreType.DMA((2 * members + 1,)),
         ],
-    )(transform, v_part, h_new, u_new, *rims)
+    )(row_index, transform, v_part, h_new, u_new, rim_part, *(rims[g] for g in far))
 
 
 def solution(mesh):

time: 120 us -> 118 us (0.983)
  waiting for transfers between devices: 56.4 us -> 55.1 us
    ppermute x3, starting transfers between devices: 6.63 us -> 12 us  [band_sum(): other = lax.ppermute(part, 'band', [(i, i ^ step) for i in range(count)])]
    ppermute x4, starting transfers between devices: 18.3 us -> 13.1 us  [swap_edges(): even = lax.ppermute(even, 'band', pairs(0))]
    ppermute x12, waiting for transfers between devices: 6.1 us -> 3.46 us  [near_swap(): return lax.ppermute(block, 'mem', [(i, i ^ 1) for i in range(count)])]
    ppermute x4, waiting for transfers between devices: 4.75 us -> 6.99 us  [swap_edges(): even = lax.ppermute(even, 'band', pairs(0))]
    pallas_call x2 -> x3, Pallas kernels: 2.36 us -> 3.75 us  [the longest x1 2.46 us: body(): call(functools.partial(finish_kernel, [every[g] for g in far], height_row...]
  transfers between devices with their start and end apart: 29 -> 29, of which waited for: 10 -> 13; matrix products, arithmetic and copies ran while one was open for 0% -> 0% of each run, Pallas kernels for 11% -> 12%
where the time goes in v3:
time: 118 us
  waiting for transfers between devices  55.1 us (47%)
  starting transfers between devices  36.2 us (31%)
  Pallas kernels  25.6 us (22%)
    ppermute x6, waiting for transfers between devices, far_gather(): lax.ppermute(block, 'mem', [(i, (i + s) % count) for i in range(count)])  41.7 us
    ppermute x4, starting transfers between devices, swap_edges(): even = lax.ppermute(even, 'band', pairs(0))  13.1 us
    ppermute x3, starting transfers between devices, band_sum(): other = lax.ppermute(part, 'band', [(i, i ^ step) for i in range(count)])  12 us
    ppermute x6, starting transfers between devices, far_gather(): lax.ppermute(block, 'mem', [(i, (i + s) % count) for i in range(count)])  7.09 us
    ppermute x4, waiting for transfers between devices, swap_edges(): even = lax.ppermute(even, 'band', pairs(0))  6.99 us
    pallas_call x2, Pallas kernels, blend(): call(functools.partial(blend_kernel, lists, height_rows, width), [smem] +...  5.44 us
    pallas_call x1, Pallas kernels, body(): call(probe_kernel, [smem, smem] + [vmem] * 3, [vmem] * 4, [field, edge, e...  4.93 us
    ppermute x12, waiting for transfers between devices, near_swap(): return lax.ppermute(block, 'mem', [(i, i ^ 1) for i in range(count)])  3.46 us
  transfers between devices with their start and end apart: 29, of which 13 were waited for; matrix products, arithmetic and copies ran while one was open for 0% of the time, Pallas kernels for 12%

profile of v3, /device:TPU:0, one launch (start us, length us, event | category | flops | bytes accessed | tf_op | source)
XLA Modules:
  0.0 117.8 jit_solution(6811293407730529923)
XLA Ops:
  0.0 1.9 %shard_map.75 = (f32[6,1,4096]{2,1,0:T(1,128)}, f32[6,1,4096]{2,1,0:T(1,128)}) custom-call(s32[1]{0:T(128)} %bitcast.row_ref, f32[6,3,8,4096]{3,2,1,0:T(8,128)} %x_ref.5, f32[8,4096]{1,0:T(8,128)} %b_ref.7), custom_call_target="tpu_custom_call" | custom-call | flops 786432 | bytes 786432 | tf_op jit(solution)/shard_map/pallas_call | solution.py:466
  1.9 3.1 %collective-permute-start = (f32[6,1,4096]{2,1,0:T(1,128)}, f32[6,1,4096]{2,1,0:T(1,128)S(1)}, u32[]{:S(2)}, u32[]{:S(2)}) collective-permute-start(f32[6,1,4096]{2,1,0:T(1,128)} %get-tuple-element.27), channel_id=1, source_target_pairs={{0,1},{2,3},{4,5},{6,7},{1,0},{3,2},{5,4},{7,6},{8,9},{10,11},{12,... | collective-permute-start | bytes 294920 | tf_op jit(solution)/shard_map/ppermute | solution.py:37
  5.6 1.7 %shard_map.74 = (f32[6,8,4096]{2,1,0:T(8,128)S(1)}, f32[6,8,4096]{2,1,0:T(8,128)S(1)}) custom-call(s32[1]{0:T(128)} %bitcast.row_ref, f32[6,3,8,4096]{3,2,1,0:T(8,128)S(1)} %copy-done, f32[8,4096]{1,0:T(8,128)S(1)} %copy-done.1), custom_call_target="tpu_custom_call" | custom-call | flops 15728640 | bytes 3145728 | tf_op jit(solution)/shard_map/pallas_call | solution.py:480
  8.0 1.0 shard_map.76
  9.0 4.8 %collective-permute-start.2 = (f32[6,1,4096]{2,1,0:T(1,128)S(1)}, f32[6,1,4096]{2,1,0:T(1,128)S(1)}, u32[]{:S(2)}, u32[]{:S(2)}) collective-permute-start(f32[6,1,4096]{2,1,0:T(1,128)S(1)} %get-tuple-element.31), channel_id=1, source_target_pairs={{0,1},{2,3},{4,5},{6,7},{1,0},{3,2},{5,4},{7,6},{8,9},{10,11},{12,... | collective-permute-start | bytes 294920 | tf_op jit(solution)/shard_map/ppermute | solution.py:37
  14.4 2.6 %collective-permute-done.2.even_ref = f32[6,1,4096]{2,1,0:T(1,128)S(1)} collective-permute-done((f32[6,1,4096]{2,1,0:T(1,128)S(1)}, f32[6,1,4096]{2,1,0:T(1,128)S(1)}, u32[]{:S(2)}, u32[]{:S(2)}) %collective-permute-start.2) | collective-permute-done | bytes 98336 | tf_op jit(solution)/shard_map/ppermute | solution.py:37
  17.7 4.7 %collective-permute-start.4 = (f32[6,1,4096]{2,1,0:T(1,128)S(1)}, f32[6,1,4096]{2,1,0:T(1,128)S(1)}, u32[]{:S(2)}, u32[]{:S(2)}) collective-permute-start(f32[6,1,4096]{2,1,0:T(1,128)S(1)} %get-tuple-element.35), channel_id=1, source_target_pairs={{0,1},{2,3},{4,5},{6,7},{1,0},{3,2},{5,4},{7,6},{8,9},{10,11},{12,... | collective-permute-start | bytes 294920 | tf_op jit(solution)/shard_map/ppermute | solution.py:37
  24.0 1.6 %collective-permute-done.4.even_ref = f32[6,1,4096]{2,1,0:T(1,128)S(1)} collective-permute-done((f32[6,1,4096]{2,1,0:T(1,128)S(1)}, f32[6,1,4096]{2,1,0:T(1,128)S(1)}, u32[]{:S(2)}, u32[]{:S(2)}) %collective-permute-start.4) | collective-permute-done | bytes 98336 | tf_op jit(solution)/shard_map/ppermute | solution.py:37
  25.6 4.9 %shard_map.79 = (f32[6,8,4096]{2,1,0:T(8,128)S(1)}, f32[6,1,4096]{2,1,0:T(1,128)S(1)}, f32[6,1,4096]{2,1,0:T(1,128)S(1)}, f32[4,8,128]{2,1,0:T(8,128)S(1)}) custom-call(s32[1]{0:T(128)} %bitcast.row_ref, s32[4,128]{1,0:T(4,128)S(1)} %shard_map.73.code_ref, f32[6,8,4096]{2,1,0:T(8,128)S(1)} %shard_map.78.part_ref, ...), custom_call_target="tpu_custom_call" | custom-call | flops 15728640 | bytes 3145728 | tf_op jit(solution)/shard_map/pallas_call | solution.py:504
  30.6 1.5 %collective-permute-start.6 = (f32[4,8,128]{2,1,0:T(8,128)S(1)}, f32[4,8,128]{2,1,0:T(8,128)S(1)}, u32[]{:S(2)}, u32[]{:S(2)}) collective-permute-start(f32[4,8,128]{2,1,0:T(8,128)S(1)} %get-tuple-element.37.refs_0_), channel_id=1, source_target_pairs={{0,16},{8,24},{16,0},{24,8},{1,17},{9,25},{17,1},{25,9},{2,18},{10... | collective-permute-start | bytes 49160 | tf_op jit(solution)/shard_map/ppermute | solution.py:69
  32.1 2.2 %collective-permute-done.6.refs_1_ = f32[4,8,128]{2,1,0:T(8,128)S(1)} collective-permute-done((f32[4,8,128]{2,1,0:T(8,128)S(1)}, f32[4,8,128]{2,1,0:T(8,128)S(1)}, u32[]{:S(2)}, u32[]{:S(2)}) %collective-permute-start.6) | collective-permute-done | bytes 16416 | tf_op jit(solution)/shard_map/ppermute | solution.py:69
  35.9 5.8 %collective-permute-start.9 = (f32[32,128]{1,0:T(8,128)S(1)}, f32[32,128]{1,0:T(8,128)S(1)}, u32[]{:S(2)}, u32[]{:S(2)}) collective-permute-start(f32[32,128]{1,0:T(8,128)S(1)} %shard_map.80), channel_id=1, source_target_pairs={{0,1},{1,0},{2,3},{3,2},{4,5},{5,4},{6,7},{7,6},{8,9},{9,8},{10,11... | collective-permute-start | bytes 49160 | tf_op jit(solution)/shard_map/ppermute | solution.py:53
  41.7 1.5 %collective-permute-start.21 = (f32[2,8,4096]{2,1,0:T(8,128)S(1)}, f32[2,8,4096]{2,1,0:T(8,128)S(1)}, u32[]{:S(2)}, u32[]{:S(2)}) collective-permute-start(f32[2,8,4096]{2,1,0:T(8,128)S(1)} %get-tuple-element.34.refs_1_.refs_4_), channel_id=1, source_target_pairs={{0,16},{8,24},{16,0},{24,8},{1,17},{9,25},{17,1},{25,9},{2,18},{10... | collective-permute-start | bytes 786440 | tf_op jit(solution)/shard_map/ppermute | solution.py:69
  43.8 3.2 %collective-permute-start.10 = (f32[32,128]{1,0:T(8,128)S(1)}, f32[32,128]{1,0:T(8,128)S(1)}, u32[]{:S(2)}, u32[]{:S(2)}) collective-permute-start(f32[32,128]{1,0:T(8,128)S(1)} %add.9), channel_id=1, source_target_pairs={{0,2},{1,3},{2,0},{3,1},{4,6},{5,7},{6,4},{7,5},{8,10},{9,11},{10,... | collective-permute-start | bytes 49160 | tf_op jit(solution)/shard_map/ppermute | solution.py:53
  46.9 1.7 %collective-permute-done.10 = f32[32,128]{1,0:T(8,128)S(1)} collective-permute-done((f32[32,128]{1,0:T(8,128)S(1)}, f32[32,128]{1,0:T(8,128)S(1)}, u32[]{:S(2)}, u32[]{:S(2)}) %collective-permute-start.10) | collective-permute-done | bytes 16416 | tf_op jit(solution)/shard_map/ppermute | solution.py:53
  48.6 3.0 %collective-permute-start.11 = (f32[32,128]{1,0:T(8,128)S(1)}, f32[32,128]{1,0:T(8,128)S(1)}, u32[]{:S(2)}, u32[]{:S(2)}) collective-permute-start(f32[32,128]{1,0:T(8,128)S(1)} %add.10), channel_id=1, source_target_pairs={{0,4},{1,5},{2,6},{3,7},{4,0},{5,1},{6,2},{7,3},{8,12},{9,13},{10,... | collective-permute-start | bytes 49160 | tf_op jit(solution)/shard_map/ppermute | solution.py:53
  52.2 1.2 %collective-permute-done.11 = f32[32,128]{1,0:T(8,128)S(1)} collective-permute-done((f32[32,128]{1,0:T(8,128)S(1)}, f32[32,128]{1,0:T(8,128)S(1)}, u32[]{:S(2)}, u32[]{:S(2)}) %collective-permute-start.11) | collective-permute-done | bytes 16416 | tf_op jit(solution)/shard_map/ppermute | solution.py:53
  54.1 2.2 %collective-permute-done.24.refs_0_ = f32[6,1,4096]{2,1,0:T(1,128)S(1)} collective-permute-done((f32[6,1,4096]{2,1,0:T(1,128)S(1)}, f32[6,1,4096]{2,1,0:T(1,128)S(1)}, u32[]{:S(2)}, u32[]{:S(2)}) %collective-permute-start.24) | collective-permute-done | bytes 98336 | tf_op jit(solution)/shard_map/ppermute | solution.py:37
  56.3 1.5 %collective-permute-start.12 = (f32[6,8,4096]{2,1,0:T(8,128)S(1)}, f32[6,8,4096]{2,1,0:T(8,128)S(1)}, u32[]{:S(2)}, u32[]{:S(2)}) collective-permute-start(f32[6,8,4096]{2,1,0:T(8,128)S(1)} %get-tuple-element.26.u_ref.refs_0_), channel_id=1, source_target_pairs={{0,16},{8,24},{16,0},{24,8},{1,17},{9,25},{17,1},{25,9},{2,18},{10... | collective-permute-start | bytes 2359304 | tf_op jit(solution)/shard_map/ppermute | solution.py:69
  58.5 1.4 %collective-permute-done.22.refs_6_ = f32[2,8,4096]{2,1,0:T(8,128)S(1)} collective-permute-done((f32[2,8,4096]{2,1,0:T(8,128)S(1)}, f32[2,8,4096]{2,1,0:T(8,128)S(1)}, u32[]{:S(2)}, u32[]{:S(2)}) %collective-permute-start.22) | collective-permute-done | bytes 262176 | tf_op jit(solution)/shard_map/ppermute | solution.py:76
  60.0 2.1 %collective-permute-done.18.refs_1_ = f32[4,8,4096]{2,1,0:T(8,128)S(1)} collective-permute-done((f32[4,8,4096]{2,1,0:T(8,128)S(1)}, f32[4,8,4096]{2,1,0:T(8,128)S(1)}, u32[]{:S(2)}, u32[]{:S(2)}) %collective-permute-start.18) | collective-permute-done | bytes 524320 | tf_op jit(solution)/shard_map/ppermute | solution.py:69
  62.1 1.5 %collective-permute-start.27 = (f32[6,4,8,512]{3,2,1,0:T(8,128)S(1)}, f32[6,4,8,512]{3,2,1,0:T(8,128)S(1)}, u32[]{:S(2)}, u32[]{:S(2)}) collective-permute-start(f32[6,4,8,512]{3,2,1,0:T(8,128)S(1)} %shard_map.86.refs_0_), channel_id=1, source_target_pairs={{0,16},{8,24},{16,0},{24,8},{1,17},{9,25},{17,1},{25,9},{2,18},{10... | collective-permute-start | bytes 1179656 | tf_op jit(solution)/shard_map/ppermute | solution.py:69
  63.6 1.5 %collective-permute-done.23.refs_7_ = f32[2,8,4096]{2,1,0:T(8,128)S(1)} collective-permute-done((f32[2,8,4096]{2,1,0:T(8,128)S(1)}, f32[2,8,4096]{2,1,0:T(8,128)S(1)}, u32[]{:S(2)}, u32[]{:S(2)}) %collective-permute-start.23) | collective-permute-done | bytes 262176 | tf_op jit(solution)/shard_map/ppermute | solution.py:76
  65.3 13.7 %collective-permute-done.12.refs_1_ = f32[6,8,4096]{2,1,0:T(8,128)S(1)} collective-permute-done((f32[6,8,4096]{2,1,0:T(8,128)S(1)}, f32[6,8,4096]{2,1,0:T(8,128)S(1)}, u32[]{:S(2)}, u32[]{:S(2)}) %collective-permute-start.12) | collective-permute-done | bytes 786464 | tf_op jit(solution)/shard_map/ppermute | solution.py:69
  79.5 23.7 %collective-permute-done.27.refs_0_ = f32[6,4,8,512]{3,2,1,0:T(8,128)S(1)} collective-permute-done((f32[6,4,8,512]{3,2,1,0:T(8,128)S(1)}, f32[6,4,8,512]{3,2,1,0:T(8,128)S(1)}, u32[]{:S(2)}, u32[]{:S(2)}) %collective-permute-start.27) | collective-permute-done | bytes 393248 | tf_op jit(solution)/shard_map/ppermute | solution.py:69
  103.8 2.4 %shard_map.81.t_ref = f32[32,128]{1,0:T(8,128)S(1)} custom-call(f32[1]{0:T(128)S(6)} %copy.8.inf_ref, f32[32,128]{1,0:T(8,128)S(1)} %add.11.part_ref), custom_call_target="tpu_custom_call" | custom-call | flops 1000000 | bytes 40000 | tf_op jit(solution)/shard_map/pallas_call | solution.py:527
  106.2 1.1 shard_map.87.part_ref
  107.3 2.3 %shard_map.84.v_ref = f32[6,8,4096]{2,1,0:T(8,128)S(1)} custom-call(f32[32,128]{1,0:T(8,128)S(1)} %shard_map.81.t_ref, f32[4,8,4096]{2,1,0:T(8,128)S(1)} %get-tuple-element.33.refs_0_, f32[4,8,4096]{2,1,0:T(8,128)S(1)} %collective-permute-done.18.refs_1_, f32[4,8,4096]{2,1,0:T(8,128)S(1)} %collective-permute-done.19.refs_2_, ...), custom_call_target="tpu_custom_call" | custom-call | flops 78643200 | bytes 7864320 | tf_op jit(solution)/shard_map/pallas_call | solution.py:560
  109.7 3.1 %shard_map.82 = (f32[6,8,4096]{2,1,0:T(8,128)S(1)}, f32[6,8,4096]{2,1,0:T(8,128)S(1)}) custom-call(f32[32,128]{1,0:T(8,128)S(1)} %shard_map.81.t_ref, f32[6,8,4096]{2,1,0:T(8,128)S(1)} %get-tuple-element.26.u_ref.refs_0_, f32[6,8,4096]{2,1,0:T(8,128)S(1)} %collective-permute-done.12.refs_1_, f32[6,8,4096]{2,1,0:T(8,128)S(1)} %collective-permute-done.13.refs_2_, ...), custom_call_target="tpu_custom_call" | custom-call | flops 78643200 | bytes 7864320 | tf_op jit(solution)/shard_map/pallas_call | solution.py:560
  112.8 1.6 %shard_map.83.h_ref = f32[6,8,4096]{2,1,0:T(8,128)S(1)} custom-call(f32[32,128]{1,0:T(8,128)S(1)} %shard_map.81.t_ref, f32[6,8,4096]{2,1,0:T(8,128)S(1)} %get-tuple-element.39.part_ref, f32[6,8,4096]{2,1,0:T(8,128)S(1)} %collective-permute-done.16.refs_0_, f32[6,8,4096]{2,1,0:T(8,128)S(1)} %collective-permute-done.17.refs_1_), custom_call_target="tpu_custom_call" | custom-call | flops 39321600 | bytes 3145728 | tf_op jit(solution)/shard_map/pallas_call | solution.py:568
  114.4 1.0 shard_map.85
  115.4 2.5 %shard_map.88 = f32[6,3,8,4096]{3,2,1,0:T(8,128)} custom-call(s32[1]{0:T(128)} %bitcast.row_ref, f32[32,128]{1,0:T(8,128)S(1)} %shard_map.81.t_ref, f32[6,8,4096]{2,1,0:T(8,128)S(1)} %get-tuple-element.41.v_ref, f32[6,8,4096]{2,1,0:T(8,128)S(1)} %shard_map.83.h_ref, f32[6,8,4096]{2,1,0:T(8,128)S(1)} %get-tuple-element.42.u_ref, ...), custom_call_target="tpu_custom_call" | custom-call | flops 15728640 | bytes 2359296 | tf_op jit(solution)/shard_map/pallas_call | solution.py:581
  (57 shorter events, 8.8 us)
Async XLA Ops:
  1.9 6.1 %collective-permute-start = (f32[6,1,4096]{2,1,0:T(1,128)}, f32[6,1,4096]{2,1,0:T(1,128)S(1)}, u32[]{:S(2)}, u32[]{:S(2)}) collective-permute-start(f32[6,1,4096]{2,1,0:T(1,128)} %get-tuple-element.27), channel_id=1, source_target_pairs={{0,1},{2,3},{4,5},{6,7},{1,0},{3,2},{5,4},{7,6},{8,9},{10,11},{12,... | collective-permute-start | bytes 294920 | tf_op jit(solution)/shard_map/ppermute | solution.py:37
  5.0 3.0 %collective-permute-start.1 = (f32[6,1,4096]{2,1,0:T(1,128)}, f32[6,1,4096]{2,1,0:T(1,128)S(1)}, u32[]{:S(2)}, u32[]{:S(2)}) collective-permute-start(f32[6,1,4096]{2,1,0:T(1,128)} %get-tuple-element.28), channel_id=1, source_target_pairs={{1,2},{3,4},{5,6},{2,1},{4,3},{6,5},{9,10},{11,12},{13,14},{10,9},... | collective-permute-start | bytes 294920 | tf_op jit(solution)/shard_map/ppermute | solution.py:38
  9.0 8.0 %collective-permute-start.2 = (f32[6,1,4096]{2,1,0:T(1,128)S(1)}, f32[6,1,4096]{2,1,0:T(1,128)S(1)}, u32[]{:S(2)}, u32[]{:S(2)}) collective-permute-start(f32[6,1,4096]{2,1,0:T(1,128)S(1)} %get-tuple-element.31), channel_id=1, source_target_pairs={{0,1},{2,3},{4,5},{6,7},{1,0},{3,2},{5,4},{7,6},{8,9},{10,11},{12,... | collective-permute-start | bytes 294920 | tf_op jit(solution)/shard_map/ppermute | solution.py:37
  13.8 3.2 %collective-permute-start.3 = (f32[6,1,4096]{2,1,0:T(1,128)S(1)}, f32[6,1,4096]{2,1,0:T(1,128)S(1)}, u32[]{:S(2)}, u32[]{:S(2)}) collective-permute-start(f32[6,1,4096]{2,1,0:T(1,128)S(1)} %get-tuple-element.32), channel_id=1, source_target_pairs={{1,2},{3,4},{5,6},{2,1},{4,3},{6,5},{9,10},{11,12},{13,14},{10,9},... | collective-permute-start | bytes 294920 | tf_op jit(solution)/shard_map/ppermute | solution.py:38
  17.7 17.9 %copy-start.2 = (f32[6,4,128]{2,1,0:T(4,128)S(1)}, f32[6,4,128]{2,1,0:T(4,128)}, u32[]{:S(2)}) copy-start(f32[6,4,128]{2,1,0:T(4,128)} %pert_ref.1) | copy-start | bytes 36868
  17.7 17.9 %copy-start.3 = (f32[4,128]{1,0:T(4,128)S(1)}, f32[4,128]{1,0:T(4,128)}, u32[]{:S(2)}) copy-start(f32[4,128]{1,0:T(4,128)} %obs_ref.1) | copy-start | bytes 6148
  17.7 17.9 %copy-start.4 = (f32[4,128]{1,0:T(4,128)S(1)}, f32[4,128]{1,0:T(4,128)}, u32[]{:S(2)}) copy-start(f32[4,128]{1,0:T(4,128)} %scale_ref.1) | copy-start | bytes 6148
  17.7 7.9 %collective-permute-start.4 = (f32[6,1,4096]{2,1,0:T(1,128)S(1)}, f32[6,1,4096]{2,1,0:T(1,128)S(1)}, u32[]{:S(2)}, u32[]{:S(2)}) collective-permute-start(f32[6,1,4096]{2,1,0:T(1,128)S(1)} %get-tuple-element.35), channel_id=1, source_target_pairs={{0,1},{2,3},{4,5},{6,7},{1,0},{3,2},{5,4},{7,6},{8,9},{10,11},{12,... | collective-permute-start | bytes 294920 | tf_op jit(solution)/shard_map/ppermute | solution.py:37
  22.4 3.2 %collective-permute-start.5 = (f32[6,1,4096]{2,1,0:T(1,128)S(1)}, f32[6,1,4096]{2,1,0:T(1,128)S(1)}, u32[]{:S(2)}, u32[]{:S(2)}) collective-permute-start(f32[6,1,4096]{2,1,0:T(1,128)S(1)} %get-tuple-element.36), channel_id=1, source_target_pairs={{1,2},{3,4},{5,6},{2,1},{4,3},{6,5},{9,10},{11,12},{13,14},{10,9},... | collective-permute-start | bytes 294920 | tf_op jit(solution)/shard_map/ppermute | solution.py:38
  30.6 3.8 %collective-permute-start.6 = (f32[4,8,128]{2,1,0:T(8,128)S(1)}, f32[4,8,128]{2,1,0:T(8,128)S(1)}, u32[]{:S(2)}, u32[]{:S(2)}) collective-permute-start(f32[4,8,128]{2,1,0:T(8,128)S(1)} %get-tuple-element.37.refs_0_), channel_id=1, source_target_pairs={{0,16},{8,24},{16,0},{24,8},{1,17},{9,25},{17,1},{25,9},{2,18},{10... | collective-permute-start | bytes 49160 | tf_op jit(solution)/shard_map/ppermute | solution.py:69
  32.1 2.9 %collective-permute-start.7 = (f32[4,8,128]{2,1,0:T(8,128)S(1)}, f32[4,8,128]{2,1,0:T(8,128)S(1)}, u32[]{:S(2)}, u32[]{:S(2)}) collective-permute-start(f32[4,8,128]{2,1,0:T(8,128)S(1)} %get-tuple-element.37.refs_0_), channel_id=1, source_target_pairs={{0,8},{8,0},{16,24},{24,16},{1,9},{9,1},{17,25},{25,17},{2,10},{10... | collective-permute-start | bytes 49160 | tf_op jit(solution)/shard_map/ppermute | solution.py:76
  34.3 1.2 %collective-permute-start.8 = (f32[4,8,128]{2,1,0:T(8,128)S(1)}, f32[4,8,128]{2,1,0:T(8,128)S(1)}, u32[]{:S(2)}, u32[]{:S(2)}) collective-permute-start(f32[4,8,128]{2,1,0:T(8,128)S(1)} %collective-permute-done.6.refs_1_), channel_id=1, source_target_pairs={{0,8},{8,0},{16,24},{24,16},{1,9},{9,1},{17,25},{25,17},{2,10},{10... | collective-permute-start | bytes 49160 | tf_op jit(solution)/shard_map/ppermute | solution.py:76
  35.9 7.8 %collective-permute-start.9 = (f32[32,128]{1,0:T(8,128)S(1)}, f32[32,128]{1,0:T(8,128)S(1)}, u32[]{:S(2)}, u32[]{:S(2)}) collective-permute-start(f32[32,128]{1,0:T(8,128)S(1)} %shard_map.80), channel_id=1, source_target_pairs={{0,1},{1,0},{2,3},{3,2},{4,5},{5,4},{6,7},{7,6},{8,9},{9,8},{10,11... | collective-permute-start | bytes 49160 | tf_op jit(solution)/shard_map/ppermute | solution.py:53
  41.7 16.6 %collective-permute-start.21 = (f32[2,8,4096]{2,1,0:T(8,128)S(1)}, f32[2,8,4096]{2,1,0:T(8,128)S(1)}, u32[]{:S(2)}, u32[]{:S(2)}) collective-permute-start(f32[2,8,4096]{2,1,0:T(8,128)S(1)} %get-tuple-element.34.refs_1_.refs_4_), channel_id=1, source_target_pairs={{0,16},{8,24},{16,0},{24,8},{1,17},{9,25},{17,1},{25,9},{2,18},{10... | collective-permute-start | bytes 786440 | tf_op jit(solution)/shard_map/ppermute | solution.py:69
  43.2 18.9 %collective-permute-start.18 = (f32[4,8,4096]{2,1,0:T(8,128)S(1)}, f32[4,8,4096]{2,1,0:T(8,128)S(1)}, u32[]{:S(2)}, u32[]{:S(2)}) collective-permute-start(f32[4,8,4096]{2,1,0:T(8,128)S(1)} %get-tuple-element.33.refs_0_), channel_id=1, source_target_pairs={{0,16},{8,24},{16,0},{24,8},{1,17},{9,25},{17,1},{25,9},{2,18},{10... | collective-permute-start | bytes 1572872 | tf_op jit(solution)/shard_map/ppermute | solution.py:69
  43.8 4.9 %collective-permute-start.10 = (f32[32,128]{1,0:T(8,128)S(1)}, f32[32,128]{1,0:T(8,128)S(1)}, u32[]{:S(2)}, u32[]{:S(2)}) collective-permute-start(f32[32,128]{1,0:T(8,128)S(1)} %add.9), channel_id=1, source_target_pairs={{0,2},{1,3},{2,0},{3,1},{4,6},{5,7},{6,4},{7,5},{8,10},{9,11},{10,... | collective-permute-start | bytes 49160 | tf_op jit(solution)/shard_map/ppermute | solution.py:53
  46.9 16.7 %collective-permute-start.19 = (f32[4,8,4096]{2,1,0:T(8,128)S(1)}, f32[4,8,4096]{2,1,0:T(8,128)S(1)}, u32[]{:S(2)}, u32[]{:S(2)}) collective-permute-start(f32[4,8,4096]{2,1,0:T(8,128)S(1)} %get-tuple-element.33.refs_0_), channel_id=1, source_target_pairs={{0,8},{8,0},{16,24},{24,16},{1,9},{9,1},{17,25},{25,17},{2,10},{10... | collective-permute-start | bytes 1572872 | tf_op jit(solution)/shard_map/ppermute | solution.py:76
  48.6 4.8 %collective-permute-start.11 = (f32[32,128]{1,0:T(8,128)S(1)}, f32[32,128]{1,0:T(8,128)S(1)}, u32[]{:S(2)}, u32[]{:S(2)}) collective-permute-start(f32[32,128]{1,0:T(8,128)S(1)} %add.10), channel_id=1, source_target_pairs={{0,4},{1,5},{2,6},{3,7},{4,0},{5,1},{6,2},{7,3},{8,12},{9,13},{10,... | collective-permute-start | bytes 49160 | tf_op jit(solution)/shard_map/ppermute | solution.py:53
  51.7 4.6 %collective-permute-start.24 = (f32[6,1,4096]{2,1,0:T(1,128)S(1)}, f32[6,1,4096]{2,1,0:T(1,128)S(1)}, u32[]{:S(2)}, u32[]{:S(2)}) collective-permute-start(f32[6,1,4096]{2,1,0:T(1,128)S(1)} %get-tuple-element.43), channel_id=1, source_target_pairs={{0,1},{2,3},{4,5},{6,7},{1,0},{3,2},{5,4},{7,6},{8,9},{10,11},{12,... | collective-permute-start | bytes 294920 | tf_op jit(solution)/shard_map/ppermute | solution.py:37
  53.4 4.4 %collective-permute-start.25 = (f32[6,1,4096]{2,1,0:T(1,128)S(1)}, f32[6,1,4096]{2,1,0:T(1,128)S(1)}, u32[]{:S(2)}, u32[]{:S(2)}) collective-permute-start(f32[6,1,4096]{2,1,0:T(1,128)S(1)} %get-tuple-element.44), channel_id=1, source_target_pairs={{1,2},{3,4},{5,6},{2,1},{4,3},{6,5},{9,10},{11,12},{13,14},{10,9},... | collective-permute-start | bytes 294920 | tf_op jit(solution)/shard_map/ppermute | solution.py:38
  56.3 22.7 %collective-permute-start.12 = (f32[6,8,4096]{2,1,0:T(8,128)S(1)}, f32[6,8,4096]{2,1,0:T(8,128)S(1)}, u32[]{:S(2)}, u32[]{:S(2)}) collective-permute-start(f32[6,8,4096]{2,1,0:T(8,128)S(1)} %get-tuple-element.26.u_ref.refs_0_), channel_id=1, source_target_pairs={{0,16},{8,24},{16,0},{24,8},{1,17},{9,25},{17,1},{25,9},{2,18},{10... | collective-permute-start | bytes 2359304 | tf_op jit(solution)/shard_map/ppermute | solution.py:69
  57.8 45.4 %collective-permute-start.16 = (f32[6,8,4096]{2,1,0:T(8,128)S(1)}, f32[6,8,4096]{2,1,0:T(8,128)S(1)}, u32[]{:S(2)}, u32[]{:S(2)}) collective-permute-start(f32[6,8,4096]{2,1,0:T(8,128)S(1)} %get-tuple-element.38.refs_4_), channel_id=1, source_target_pairs={{0,16},{8,24},{16,0},{24,8},{1,17},{9,25},{17,1},{25,9},{2,18},{10... | collective-permute-start | bytes 2359304 | tf_op jit(solution)/shard_map/ppermute | solution.py:69
  58.3 1.5 %collective-permute-start.22 = (f32[2,8,4096]{2,1,0:T(8,128)S(1)}, f32[2,8,4096]{2,1,0:T(8,128)S(1)}, u32[]{:S(2)}, u32[]{:S(2)}) collective-permute-start(f32[2,8,4096]{2,1,0:T(8,128)S(1)} %get-tuple-element.34.refs_1_.refs_4_), channel_id=1, source_target_pairs={{0,8},{8,0},{16,24},{24,16},{1,9},{9,1},{17,25},{25,17},{2,10},{10... | collective-permute-start | bytes 786440 | tf_op jit(solution)/shard_map/ppermute | solution.py:76
  59.9 19.1 %collective-permute-start.26 = (f32[6,4,8,512]{3,2,1,0:T(8,128)S(1)}, f32[6,4,8,512]{3,2,1,0:T(8,128)S(1)}, u32[]{:S(2)}, u32[]{:S(2)}) collective-permute-start(f32[6,4,8,512]{3,2,1,0:T(8,128)S(1)} %shard_map.86.refs_0_), channel_id=1, source_target_pairs={{0,8},{8,0},{16,24},{24,16},{1,9},{9,1},{17,25},{25,17},{2,10},{10... | collective-permute-start | bytes 1179656 | tf_op jit(solution)/shard_map/ppermute | solution.py:76
  62.1 41.0 %collective-permute-start.27 = (f32[6,4,8,512]{3,2,1,0:T(8,128)S(1)}, f32[6,4,8,512]{3,2,1,0:T(8,128)S(1)}, u32[]{:S(2)}, u32[]{:S(2)}) collective-permute-start(f32[6,4,8,512]{3,2,1,0:T(8,128)S(1)} %shard_map.86.refs_0_), channel_id=1, source_target_pairs={{0,16},{8,24},{16,0},{24,8},{1,17},{9,25},{17,1},{25,9},{2,18},{10... | collective-permute-start | bytes 1179656 | tf_op jit(solution)/shard_map/ppermute | solution.py:69
  63.6 1.5 %collective-permute-start.23 = (f32[2,8,4096]{2,1,0:T(8,128)S(1)}, f32[2,8,4096]{2,1,0:T(8,128)S(1)}, u32[]{:S(2)}, u32[]{:S(2)}) collective-permute-start(f32[2,8,4096]{2,1,0:T(8,128)S(1)} %collective-permute-done.21.refs_5_), channel_id=1, source_target_pairs={{0,8},{8,0},{16,24},{24,16},{1,9},{9,1},{17,25},{25,17},{2,10},{10... | collective-permute-start | bytes 786440 | tf_op jit(solution)/shard_map/ppermute | solution.py:76
  65.2 38.5 %collective-permute-start.20 = (f32[4,8,4096]{2,1,0:T(8,128)S(1)}, f32[4,8,4096]{2,1,0:T(8,128)S(1)}, u32[]{:S(2)}, u32[]{:S(2)}) collective-permute-start(f32[4,8,4096]{2,1,0:T(8,128)S(1)} %collective-permute-done.18.refs_1_), channel_id=1, source_target_pairs={{0,8},{8,0},{16,24},{24,16},{1,9},{9,1},{17,25},{25,17},{2,10},{10... | collective-permute-start | bytes 1572872 | tf_op jit(solution)/shard_map/ppermute | solution.py:76
  79.0 30.7 %collective-permute-start.13 = (f32[6,8,4096]{2,1,0:T(8,128)S(1)}, f32[6,8,4096]{2,1,0:T(8,128)S(1)}, u32[]{:S(2)}, u32[]{:S(2)}) collective-permute-start(f32[6,8,4096]{2,1,0:T(8,128)S(1)} %get-tuple-element.26.u_ref.refs_0_), channel_id=1, source_target_pairs={{0,8},{8,0},{16,24},{24,16},{1,9},{9,1},{17,25},{25,17},{2,10},{10... | collective-permute-start | bytes 2359304 | tf_op jit(solution)/shard_map/ppermute | solution.py:76
  79.0 30.7 %collective-permute-start.15 = (f32[6,8,4096]{2,1,0:T(8,128)S(1)}, f32[6,8,4096]{2,1,0:T(8,128)S(1)}, u32[]{:S(2)}, u32[]{:S(2)}) collective-permute-start(f32[6,8,4096]{2,1,0:T(8,128)S(1)} %get-tuple-element.38.refs_4_), channel_id=1, source_target_pairs={{0,8},{8,0},{16,24},{24,16},{1,9},{9,1},{17,25},{25,17},{2,10},{10... | collective-permute-start | bytes 2359304 | tf_op jit(solution)/shard_map/ppermute | solution.py:76
  103.2 6.5 %collective-permute-start.14 = (f32[6,8,4096]{2,1,0:T(8,128)S(1)}, f32[6,8,4096]{2,1,0:T(8,128)S(1)}, u32[]{:S(2)}, u32[]{:S(2)}) collective-permute-start(f32[6,8,4096]{2,1,0:T(8,128)S(1)} %collective-permute-done.12.refs_1_), channel_id=1, source_target_pairs={{0,8},{8,0},{16,24},{24,16},{1,9},{9,1},{17,25},{25,17},{2,10},{10... | collective-permute-start | bytes 2359304 | tf_op jit(solution)/shard_map/ppermute | solution.py:76
  103.2 9.6 %collective-permute-start.17 = (f32[6,8,4096]{2,1,0:T(8,128)S(1)}, f32[6,8,4096]{2,1,0:T(8,128)S(1)}, u32[]{:S(2)}, u32[]{:S(2)}) collective-permute-start(f32[6,8,4096]{2,1,0:T(8,128)S(1)} %collective-permute-done.16.refs_0_), channel_id=1, source_target_pairs={{0,8},{8,0},{16,24},{24,16},{1,9},{9,1},{17,25},{25,17},{2,10},{10... | collective-permute-start | bytes 2359304 | tf_op jit(solution)/shard_map/ppermute | solution.py:76
  103.7 11.7 %collective-permute-start.28 = (f32[6,4,8,512]{3,2,1,0:T(8,128)S(1)}, f32[6,4,8,512]{3,2,1,0:T(8,128)S(1)}, u32[]{:S(2)}, u32[]{:S(2)}) collective-permute-start(f32[6,4,8,512]{3,2,1,0:T(8,128)S(1)} %collective-permute-done.27.refs_0_), channel_id=1, source_target_pairs={{0,8},{8,0},{16,24},{24,16},{1,9},{9,1},{17,25},{25,17},{2,10},{10... | collective-permute-start | bytes 1179656 | tf_op jit(solution)/shard_map/ppermute | solution.py:76
  (3 other events, 25.4 us)
